TPU v7x, 512 devices: a whole 4x4x16 slice. The times are simulated.
512 devices in a mesh: attn: 8 (over z_lo), expert: 8 (over y, core), hidden: 4 (over x), pair: 2 (over z_hi).
Axes of the slice: x: 4, y: 4, z: 16 (z_hi: 2, z_lo: 8; z = z_hi * 8 + z_lo), core: 2. Of those that a mesh axis runs over, the one named last changes fastest.
Arguments:
- queries: bfloat16 [16, 128, 4096], P(('expert', 'pair'), None, ('attn', 'hidden')), may hold values from -5 to 5
- keys: bfloat16 [16, 128, 1024], P(('expert', 'pair'), None, 'attn'), may hold values from -5 to 5
- values: bfloat16 [16, 128, 1024], P(('expert', 'pair'), None, 'attn'), may hold values from -6 to 6
- out_weight: bfloat16 [4096, 4096], P(('attn', 'hidden')), may hold values from -0.09375 to 0.09375
- residual: bfloat16 [16, 128, 4096], P(('expert', 'pair'), ('attn', 'hidden')), may hold values from -4 to 4
- norm_gain: float32 [4096], replicated, may hold values from 0.1 to 1.9
- route_logits: float32 [16, 128, 2], P(('expert', 'pair'), ('attn', 'hidden')), may hold values from -6 to 6
- expert_ids: int32 [16, 128, 2], P(('expert', 'pair'), ('attn', 'hidden')), may hold values from 0 to 7, all different within a row; in each aligned block of 4 rows (0 to 3, 4 to 7, ..., all dimensions but the last counted through in order) at most 2 rows name the same one
- doc_lengths: int32 [16, 2], P(('expert', 'pair')), may hold values from 32 to 96, as said below
- gate_up_weight: bfloat16 [8, 2, 4096, 8192], P('expert', None, None, ('attn', 'hidden', 'pair')), may hold values from -0.09375 to 0.09375
- down_weight: bfloat16 [8, 8192, 4096], P('expert', 'attn', ('hidden', 'pair')), may hold values from -0.0625 to 0.0625
Outputs:
- layer_out: bfloat16 [16, 128, 4096], P(('expert', 'pair'), ('attn', 'hidden'))
Inputs may be any that keep to these rules, and one draw needn't show every extreme that they name: `expert_ids`: A token names two different experts; in every aligned block of 4 tokens (all leading dimensions taken together, in order) no expert is named by more than 2 tokens, and in some block one expert is named by exactly 2 tokens. `doc_lengths`: each group has one document of 96 tokens and one of 32 tokens, in either order.
All inputs are finite; a program needn't handle non-finite values.
Results may differ from a plain program's by a relative error of at most 0.022.
Values may be sent and summed in bfloat16 or wider, within the bound.
No kernel may reach another device: no remote copies, remote signals or barrier semaphores. Data moves between devices by JAX's collectives and lax.ppermute only.
A program may use at most 64 MiB of HBM per device.

v0:
```python
import jax
import jax.numpy as jnp
from jax import lax
from jax.sharding import Mesh
from jax.sharding import PartitionSpec as P


D = 4096
HD = 128
EPSILON = 1e-05
BF16 = jnp.bfloat16
F32 = jnp.float32


ATTN = ("ab", "aa")
Z_AXES = ("ab", "aa", "pair")
ROUTE = ("y", "core", "pair", "ab", "hidden")


def z_shift(step):
    def place(z):
        return ((z % 8) // 4) * 8 + (z % 4) * 2 + z // 8

    return [(place(z), place((z + step) % 16)) for z in range(16)]


def exchange(value, axes):
    return lax.all_to_all(value, axes, 0, 0, tiled=True)


def attention(queries, keys, values, doc_lengths):
    tok_group = queries.shape[0]
    doc_ends = jnp.cumsum(doc_lengths)
    positions = jnp.arange(tok_group, dtype=jnp.int32)
    document = jnp.sum((positions[:, None] >= doc_ends[None, :]).astype(jnp.int32), axis=1)
    allowed = (document[:, None] == document[None, :]) & (positions[None, :] <= positions[:, None])
    scores = jnp.dot(queries, keys.T, preferred_element_type=F32) * HD ** (-0.5)
    scores = jnp.where(allowed, scores, -1e30)
    row_top = jnp.max(scores, axis=1, keepdims=True)
    weights = jnp.exp(scores - row_top)
    probabilities = (weights / jnp.sum(weights, axis=1, keepdims=True)).astype(BF16)
    return jnp.dot(probabilities, values, preferred_element_type=F32).astype(BF16)


def slot_selector(chosen, experts, capacity):
    rows = chosen.shape[0]
    row_ids = jnp.arange(rows, dtype=jnp.int32)
    earlier = row_ids[None, :] < row_ids[:, None]
    same = chosen[:, None] == chosen[None, :]
    ranking = jnp.sum((same & earlier).astype(jnp.int32), axis=-1)
    slots = jnp.arange(experts * capacity, dtype=jnp.int32)
    return (chosen[None, :] == (slots // capacity)[:, None]) & (
        ranking[None, :] == (slots % capacity)[:, None]
    )


def layer(
    queries,
    keys,
    values,
    out_weight,
    residual,
    norm_gain,
    route_logits,
    expert_ids,
    doc_lengths,
    gate_up_weight,
    down_weight,
):
    xs = lax.axis_size("hidden")
    zl = lax.axis_size(ATTN)
    pairs = lax.axis_size("pair")
    experts = lax.axis_size(("y", "core"))
    capacity = 2
    chunk = D // xs
    z_hi = lax.axis_index("pair")

    unit = gate_up_weight.shape[-1]
    down = down_weight[0].reshape(xs, pairs, unit, -1)
    width = down.shape[-1]
    kept = lax.dynamic_index_in_dim(down, z_hi, 1, keepdims=False).reshape(xs * unit, width)
    sent = lax.dynamic_index_in_dim(down, 1 - z_hi, 1, keepdims=False).reshape(xs * unit, width)
    other = lax.ppermute(sent, "pair", [(0, 1), (1, 0)])
    down = jnp.concatenate(
        [jnp.where(z_hi == 0, kept, other), jnp.where(z_hi == 0, other, kept)], axis=1
    )

    heads_out = attention(queries[0], keys[0], values[0], doc_lengths[0])
    tok_group = heads_out.shape[0]
    owned = tok_group // (zl * xs)
    projected = jnp.dot(heads_out, out_weight, preferred_element_type=F32).astype(BF16)
    projected = projected.reshape(zl, xs, owned, D).transpose(1, 0, 2, 3)
    projected = jnp.sum(exchange(projected, "hidden").astype(F32), axis=0).astype(BF16)
    gate_up = gate_up_weight[0].reshape(2, xs, chunk, unit)
    projected, gate_up = lax.optimization_barrier((projected, gate_up))
    me = lax.axis_index("hidden")
    gathered = jnp.zeros((xs, 2, chunk, unit), BF16)
    for d in range(xs):
        block = lax.dynamic_index_in_dim(gate_up, (me + d) % xs, 1, keepdims=False)
        if d > 0:
            block = lax.ppermute(block, "hidden", [(i, (i + d) % xs) for i in range(xs)])
        gathered = lax.dynamic_update_index_in_dim(gathered, block, (me - d) % xs, 0)
    projected = jnp.sum(exchange(projected, ATTN).astype(F32), axis=0)
    gate_up = gathered.transpose(2, 1, 0, 3).reshape(chunk, 2 * xs * unit)
    attended = residual[0].astype(F32) + projected
    scale = lax.rsqrt(jnp.mean(attended * attended, axis=1, keepdims=True) + EPSILON)
    normed = (attended * scale * norm_gain).astype(BF16)

    chosen = expert_ids[0].reshape(2 * owned)
    selector = slot_selector(chosen, experts, capacity)
    picker = selector[:, 0::2] | selector[:, 1::2]
    picked = jnp.dot(picker.astype(BF16), normed, preferred_element_type=F32).astype(BF16)
    picked = picked.reshape(experts, 1, capacity, xs, chunk).transpose(0, 1, 3, 2, 4)
    far = lax.axis_size(("pair", "ab"))
    outgoing = jnp.broadcast_to(picked, (experts, far, xs, capacity, chunk))
    rows = exchange(outgoing.reshape(-1, capacity, chunk), ROUTE).reshape(-1, chunk)
    steps = (1, -1, 2)
    window = [rows] + [lax.ppermute(rows, Z_AXES, z_shift(d)) for d in steps]

    rows = jnp.concatenate(window, axis=0)
    partial = jnp.dot(rows, gate_up, preferred_element_type=F32).astype(BF16)
    partial = partial.reshape(xs, -1, partial.shape[1])
    summed = jnp.sum(exchange(partial, "hidden").astype(F32), axis=0)
    half = xs * unit
    activated = (jax.nn.silu(summed[:, :half]) * summed[:, half:]).astype(BF16)
    activated = exchange(jnp.broadcast_to(activated, (xs, *activated.shape)), "hidden")
    activated = activated.reshape(-1, half)
    out = jnp.dot(activated, down, preferred_element_type=F32)
    blocks = out.reshape(len(window), -1, chunk)
    total = blocks[0]
    for k, d in enumerate(steps):
        back = lax.ppermute(blocks[k + 1].astype(BF16), Z_AXES, z_shift(-d))
        total = total + back.astype(F32)

    total = total.astype(BF16).reshape(-1, capacity, chunk)
    returned = exchange(total, ROUTE).reshape(experts, far, xs, capacity, chunk)
    returned = jnp.sum(returned.astype(F32), axis=1).astype(BF16)
    returned = returned.transpose(0, 2, 1, 3).reshape(experts * capacity, D)
    per_row = jnp.einsum(
        "sr,sd->rd", selector.astype(BF16), returned, preferred_element_type=F32
    ).reshape(owned, 2, D)
    logits = route_logits[0]
    first_share = jax.nn.sigmoid(logits[:, 0] - logits[:, 1])
    layer_out = (
        attended
        + first_share[:, None] * per_row[:, 0]
        + (1.0 - first_share)[:, None] * per_row[:, 1]
    )
    return layer_out.astype(BF16)[None]


def solution(mesh):
    cut = Mesh(
        mesh.devices.reshape(2, 4, 4, 2, 4, 2), ("ab", "aa", "y", "core", "hidden", "pair")
    )
    expert = ("y", "core")
    group = ("y", "core", "pair")
    owner = ("ab", "aa", "hidden")
    in_specs = (
        P(group, None, owner),
        P(group, None, ATTN),
        P(group, None, ATTN),
        P(owner, None),
        P(group, owner, None),
        P(),
        P(group, owner, None),
        P(group, owner, None),
        P(group, None),
        P(expert, None, None, ("ab", "aa", "hidden", "pair")),
        P(expert, ATTN, ("hidden", "pair")),
    )
    return jax.shard_map(
        layer, mesh=cut, in_specs=in_specs, out_specs=P(group, owner, None), check_vma=False
    )
```

profile of v0, /device:TPU:96, one launch (start us, length us, event | category | flops | bytes accessed | tf_op | source)
XLA Modules:
  0.0 297.0 jit_solution(11303807898691483075)
XLA Ops:
  4.3 19.3 %all_to_all.30 = bf16[4,8,4,4096]{3,2,1,0:T(4,128)(2,1)S(1)} all-to-all(bf16[4,8,4,4096]{3,2,1,0:T(4,128)(2,1)S(1)} %bitcast.83), channel_id=1, replica_groups=mesh['ab'=2,'aa'=4,'y'=4,'core'=2,'hidden'=4,'pair'=2] {'hidden'}, dimensions={0} | all-to-all | bytes 2097152 | tf_op jit(solution)/shard_map/all_to_all | solution.py:28
  25.0 11.7 %all-to-all-start.1 = ((bf16[8,4,4096]{2,1,0:T(4,128)(2,1)}), bf16[8,4,4096]{2,1,0:T(4,128)(2,1)S(1)}, u32[]{:S(2)}, u32[]{:S(2)}) async-start(bf16[8,4,4096]{2,1,0:T(4,128)(2,1)} %reduce_sum.82), calls=%async_computation.1 | async-start | bytes 524288 | tf_op jit(solution)/shard_map/all_to_all | solution.py:28
  37.3 12.0 %all-to-all-done.1 = bf16[8,4,4096]{2,1,0:T(4,128)(2,1)S(1)} async-done(((bf16[8,4,4096]{2,1,0:T(4,128)(2,1)}), bf16[8,4,4096]{2,1,0:T(4,128)(2,1)S(1)}, u32[]{:S(2)}, u32[]{:S(2)}) %all-to-all-start.1) | async-done | bytes 262176 | tf_op jit(solution)/shard_map/all_to_all | solution.py:28
  51.6 13.6 %all-to-all-start.2 = ((bf16[128,2,1024]{2,1,0:T(2,128)(2,1)}), bf16[128,2,1024]{2,1,0:T(2,128)(2,1)}, u32[]{:S(2)}, u32[]{:S(2)}) async-start(bf16[128,2,1024]{2,1,0:T(2,128)(2,1)} %bitcast.14), calls=%async_computation.2 | async-start | bytes 1048576 | tf_op jit(solution)/shard_map/all_to_all | solution.py:28
  65.2 3.0 %copy.63 = bf16[2,4,1024,128]{2,3,0,1:T(8,128)(2,1)S(1)} copy(bf16[2,4,1024,128]{3,2,1,0:T(8,128)(2,1)} %bitcast.84) | data formatting | bytes 4194304 | tf_op jit(solution)/shard_map/optimization_barrier | solution.py:95
  69.4 3.0 collective-permute-start.3
  72.4 4.6 %collective-permute-start.4 = (bf16[2,1024,128]{1,2,0:T(8,128)(2,1)}, bf16[2,1024,128]{1,2,0:T(8,128)(2,1)}, u32[]{:S(2)}, u32[]{:S(2)}) collective-permute-start(bf16[2,1024,128]{1,2,0:T(8,128)(2,1)} %get-tuple-element.15), channel_id=1, source_target_pairs={{0,4},{2,6},{4,0},{6,2},{1,5},{3,7},{5,1},{7,3},{8,12},{10,14},{12... | collective-permute-start | bytes 1572872 | tf_op jit(solution)/shard_map/ppermute | solution.py:101
  77.1 3.4 %collective-permute-start.5 = (bf16[2,1024,128]{1,2,0:T(8,128)(2,1)}, bf16[2,1024,128]{1,2,0:T(8,128)(2,1)}, u32[]{:S(2)}, u32[]{:S(2)}) collective-permute-start(bf16[2,1024,128]{1,2,0:T(8,128)(2,1)} %get-tuple-element.14), channel_id=1, source_target_pairs={{0,6},{2,0},{4,2},{6,4},{1,7},{3,1},{5,3},{7,5},{8,14},{10,8},{12,... | collective-permute-start | bytes 1572872 | tf_op jit(solution)/shard_map/ppermute | solution.py:101
  80.5 1.6 broadcast_in_dim.51
  82.9 8.3 %all-to-all-done.2 = bf16[128,2,1024]{2,1,0:T(2,128)(2,1)} async-done(((bf16[128,2,1024]{2,1,0:T(2,128)(2,1)}), bf16[128,2,1024]{2,1,0:T(2,128)(2,1)}, u32[]{:S(2)}, u32[]{:S(2)}) %all-to-all-start.2) | async-done | bytes 524320 | tf_op jit(solution)/shard_map/all_to_all | solution.py:28
  92.4 11.9 %collective-permute-start = (bf16[256,1024]{1,0:T(8,128)(2,1)S(1)}, bf16[256,1024]{1,0:T(8,128)(2,1)S(1)}, u32[]{:S(2)}, u32[]{:S(2)}) collective-permute-start(bf16[256,1024]{1,0:T(8,128)(2,1)S(1)} %reshape.219), channel_id=1, source_target_pairs={{0,64},{64,128},{128,192},{192,256},{256,320},{320,384},{384,448},... | collective-permute-start | bytes 1572872 | tf_op jit(solution)/shard_map/ppermute | solution.py:118
  104.3 3.9 %collective-permute-start.1 = (bf16[256,1024]{1,0:T(8,128)(2,1)S(1)}, bf16[256,1024]{1,0:T(8,128)(2,1)S(1)}, u32[]{:S(2)}, u32[]{:S(2)}) collective-permute-start(bf16[256,1024]{1,0:T(8,128)(2,1)S(1)} %reshape.219), channel_id=1, source_target_pairs={{0,449},{64,0},{128,64},{192,128},{256,192},{320,256},{384,320},{4... | collective-permute-start | bytes 1572872 | tf_op jit(solution)/shard_map/ppermute | solution.py:118
  108.2 3.7 %collective-permute-start.2 = (bf16[256,1024]{1,0:T(8,128)(2,1)S(1)}, bf16[256,1024]{1,0:T(8,128)(2,1)S(1)}, u32[]{:S(2)}, u32[]{:S(2)}) collective-permute-start(bf16[256,1024]{1,0:T(8,128)(2,1)S(1)} %reshape.219), channel_id=1, source_target_pairs={{0,128},{64,192},{128,256},{192,320},{256,384},{320,448},{384,1},{... | collective-permute-start | bytes 1572872 | tf_op jit(solution)/shard_map/ppermute | solution.py:118
  111.8 1.9 bitcast_dynamic-update-slice_fusion.2
  113.7 1.9 bitcast_dynamic-update-slice_fusion.1
  115.6 1.9 bitcast_dynamic-update-slice_fusion
  117.5 3.6 %collective-permute-done = bf16[256,1024]{1,0:T(8,128)(2,1)S(1)} collective-permute-done((bf16[256,1024]{1,0:T(8,128)(2,1)S(1)}, bf16[256,1024]{1,0:T(8,128)(2,1)S(1)}, u32[]{:S(2)}, u32[]{:S(2)}) %collective-permute-start) | collective-permute-done | bytes 524320 | tf_op jit(solution)/shard_map/ppermute | solution.py:118
  121.3 13.0 %collective-permute-done.2 = bf16[256,1024]{1,0:T(8,128)(2,1)S(1)} collective-permute-done((bf16[256,1024]{1,0:T(8,128)(2,1)S(1)}, bf16[256,1024]{1,0:T(8,128)(2,1)S(1)}, u32[]{:S(2)}, u32[]{:S(2)}) %collective-permute-start.2) | collective-permute-done | bytes 524320 | tf_op jit(solution)/shard_map/ppermute | solution.py:118
  134.3 5.3 %fusion.8 = bf16[1024,1024]{1,0:T(8,128)(2,1)} fusion(bf16[1024,1024]{0,1:T(8,128)(2,1)} %bitcast.23, bf16[256,1024]{1,0:T(8,128)(2,1)S(1)} %collective-permute-done.2, bf16[256,1024]{1,0:T(8,128)(2,1)S(1)} %collective-permute-done.1, bf16[256,1024]{1,0:T(8,128)(2,1)S(1)} %collective-permute-done, bf16[256,1024]{1,0:T(8,128)(2,1)S(1)} %reshape.219), kind=kOutput, calls=%fused_computation.11 | convolution fusion | flops 2156920832 | bytes 6291456 | tf_op jit(solution)/shard_map/dot_general | solution.py:121
  139.6 5.6 %all-to-all-start.3 = ((bf16[4,256,1024]{2,1,0:T(8,128)(2,1)}), bf16[4,256,1024]{2,1,0:T(8,128)(2,1)S(1)}, u32[]{:S(2)}, u32[]{:S(2)}) async-start(bf16[4,256,1024]{2,1,0:T(8,128)(2,1)} %bitcast.85), calls=%async_computation.3 | async-start | bytes 4194304 | tf_op jit(solution)/shard_map/all_to_all | solution.py:28
  145.1 2.3 constant_dynamic-slice_fusion
  147.4 6.8 %collective-permute-start.6 = (bf16[512,512]{1,0:T(8,128)(2,1)}, bf16[512,512]{1,0:T(8,128)(2,1)}, u32[]{:S(2)}, u32[]{:S(2)}) collective-permute-start(bf16[512,512]{1,0:T(8,128)(2,1)} %bitcast.28), channel_id=1, source_target_pairs={{0,1},{1,0},{2,3},{3,2},{4,5},{5,4},{6,7},{7,6},{8,9},{9,8},{10,11... | collective-permute-start | bytes 1572872 | tf_op jit(solution)/shard_map/ppermute | solution.py:83
  154.2 18.6 %all-to-all-done.3 = bf16[4,256,1024]{2,1,0:T(8,128)(2,1)S(1)} async-done(((bf16[4,256,1024]{2,1,0:T(8,128)(2,1)}), bf16[4,256,1024]{2,1,0:T(8,128)(2,1)S(1)}, u32[]{:S(2)}, u32[]{:S(2)}) %all-to-all-start.3) | async-done | bytes 2097184 | tf_op jit(solution)/shard_map/all_to_all | solution.py:28
  174.4 3.5 %all-to-all-start.4 = ((bf16[4,256,512]{2,1,0:T(8,128)(2,1)}), bf16[4,256,512]{2,1,0:T(8,128)(2,1)S(1)}, u32[]{:S(2)}, u32[]{:S(2)}) async-start(bf16[4,256,512]{2,1,0:T(8,128)(2,1)} %broadcast_in_dim.56), calls=%async_computation.4 | async-start | bytes 2097152 | tf_op jit(solution)/shard_map/all_to_all | solution.py:28
  178.0 28.9 %collective-permute-done.6 = bf16[512,512]{1,0:T(8,128)(2,1)} collective-permute-done((bf16[512,512]{1,0:T(8,128)(2,1)}, bf16[512,512]{1,0:T(8,128)(2,1)}, u32[]{:S(2)}, u32[]{:S(2)}) %collective-permute-start.6) | collective-permute-done | bytes 524320 | tf_op jit(solution)/shard_map/ppermute | solution.py:83
  209.5 1.9 collective-permute-start.7
  211.5 5.1 %collective-permute-start.8 = (bf16[256,1024]{1,0:T(8,128)(2,1)S(1)}, bf16[256,1024]{1,0:T(8,128)(2,1)S(1)}, u32[]{:S(2)}, u32[]{:S(2)}) collective-permute-start(bf16[256,1024]{1,0:T(8,128)(2,1)S(1)} %get-tuple-element.13), channel_id=1, source_target_pairs={{0,64},{64,128},{128,192},{192,256},{256,320},{320,384},{384,448},... | collective-permute-start | bytes 1572872 | tf_op jit(solution)/shard_map/ppermute | solution.py:132
  216.6 2.3 collective-permute-start.9
  218.9 18.6 %collective-permute-done.7 = bf16[256,1024]{1,0:T(8,128)(2,1)S(1)} collective-permute-done((bf16[256,1024]{1,0:T(8,128)(2,1)S(1)}, bf16[256,1024]{1,0:T(8,128)(2,1)S(1)}, u32[]{:S(2)}, u32[]{:S(2)}) %collective-permute-start.7) | collective-permute-done | bytes 524320 | tf_op jit(solution)/shard_map/ppermute | solution.py:132
  237.5 7.5 %collective-permute-done.9 = bf16[256,1024]{1,0:T(8,128)(2,1)S(1)} collective-permute-done((bf16[256,1024]{1,0:T(8,128)(2,1)S(1)}, bf16[256,1024]{1,0:T(8,128)(2,1)S(1)}, u32[]{:S(2)}, u32[]{:S(2)}) %collective-permute-start.9) | collective-permute-done | bytes 524320 | tf_op jit(solution)/shard_map/ppermute | solution.py:132
  246.4 15.3 %all-to-all-start.5 = ((bf16[128,2,1024]{2,1,0:T(2,128)(2,1)}), bf16[128,2,1024]{2,1,0:T(2,128)(2,1)S(1)}, u32[]{:S(2)}, u32[]{:S(2)}) async-start(bf16[128,2,1024]{2,1,0:T(2,128)(2,1)} %reshape.225), calls=%async_computation.5 | async-start | bytes 1048576 | tf_op jit(solution)/shard_map/all_to_all | solution.py:28
  261.9 33.4 %all-to-all-done.5 = bf16[128,2,1024]{2,1,0:T(2,128)(2,1)S(1)} async-done(((bf16[128,2,1024]{2,1,0:T(2,128)(2,1)}), bf16[128,2,1024]{2,1,0:T(2,128)(2,1)S(1)}, u32[]{:S(2)}, u32[]{:S(2)}) %all-to-all-start.5) | async-done | bytes 524320 | tf_op jit(solution)/shard_map/all_to_all | solution.py:28
  (57 shorter events, 19.5 us)
Async XLA Ops:
  0.0 2.0 copy-start
  4.2 32.5 %copy-start.3 = (s32[1,4,2]{1,2,0:T(2,128)S(1)}, s32[1,4,2]{1,2,0:T(2,128)}, u32[]{:S(2)}) copy-start(s32[1,4,2]{1,2,0:T(2,128)} %param.18) | copy-start | bytes 100
  4.2 45.4 %copy-start.1 = (bf16[1,4,4096]{2,1,0:T(4,128)(2,1)S(1)}, bf16[1,4,4096]{2,1,0:T(4,128)(2,1)}, u32[]{:S(2)}) copy-start(bf16[1,4,4096]{2,1,0:T(4,128)(2,1)} %param.15) | copy-start | bytes 98308
  4.2 45.6 %copy-start.2 = (f32[4096]{0:T(1024)S(1)}, f32[4096]{0:T(1024)}, u32[]{:S(2)}) copy-start(f32[4096]{0:T(1024)} %param.16) | copy-start | bytes 49156
  25.0 24.4 %all-to-all-start.1 = ((bf16[8,4,4096]{2,1,0:T(4,128)(2,1)}), bf16[8,4,4096]{2,1,0:T(4,128)(2,1)S(1)}, u32[]{:S(2)}, u32[]{:S(2)}) async-start(bf16[8,4,4096]{2,1,0:T(4,128)(2,1)} %reduce_sum.82), calls=%async_computation.1 | async-start | bytes 524288 | tf_op jit(solution)/shard_map/all_to_all | solution.py:28
  51.6 39.5 %all-to-all-start.2 = ((bf16[128,2,1024]{2,1,0:T(2,128)(2,1)}), bf16[128,2,1024]{2,1,0:T(2,128)(2,1)}, u32[]{:S(2)}, u32[]{:S(2)}) async-start(bf16[128,2,1024]{2,1,0:T(2,128)(2,1)} %bitcast.14), calls=%async_computation.2 | async-start | bytes 1048576 | tf_op jit(solution)/shard_map/all_to_all | solution.py:28
  69.4 38.7 %collective-permute-start.3 = (bf16[2,1024,128]{1,2,0:T(8,128)(2,1)}, bf16[2,1024,128]{1,2,0:T(8,128)(2,1)}, u32[]{:S(2)}, u32[]{:S(2)}) collective-permute-start(bf16[2,1024,128]{1,2,0:T(8,128)(2,1)} %get-tuple-element.16), channel_id=1, source_target_pairs={{0,2},{2,4},{4,6},{6,0},{1,3},{3,5},{5,7},{7,1},{8,10},{10,12},{12... | collective-permute-start | bytes 1572872 | tf_op jit(solution)/shard_map/ppermute | solution.py:101
  72.4 41.3 %collective-permute-start.4 = (bf16[2,1024,128]{1,2,0:T(8,128)(2,1)}, bf16[2,1024,128]{1,2,0:T(8,128)(2,1)}, u32[]{:S(2)}, u32[]{:S(2)}) collective-permute-start(bf16[2,1024,128]{1,2,0:T(8,128)(2,1)} %get-tuple-element.15), channel_id=1, source_target_pairs={{0,4},{2,6},{4,0},{6,2},{1,5},{3,7},{5,1},{7,3},{8,12},{10,14},{12... | collective-permute-start | bytes 1572872 | tf_op jit(solution)/shard_map/ppermute | solution.py:101
  77.1 38.5 %collective-permute-start.5 = (bf16[2,1024,128]{1,2,0:T(8,128)(2,1)}, bf16[2,1024,128]{1,2,0:T(8,128)(2,1)}, u32[]{:S(2)}, u32[]{:S(2)}) collective-permute-start(bf16[2,1024,128]{1,2,0:T(8,128)(2,1)} %get-tuple-element.14), channel_id=1, source_target_pairs={{0,6},{2,0},{4,2},{6,4},{1,7},{3,1},{5,3},{7,5},{8,14},{10,8},{12,... | collective-permute-start | bytes 1572872 | tf_op jit(solution)/shard_map/ppermute | solution.py:101
  92.4 28.7 %collective-permute-start = (bf16[256,1024]{1,0:T(8,128)(2,1)S(1)}, bf16[256,1024]{1,0:T(8,128)(2,1)S(1)}, u32[]{:S(2)}, u32[]{:S(2)}) collective-permute-start(bf16[256,1024]{1,0:T(8,128)(2,1)S(1)} %reshape.219), channel_id=1, source_target_pairs={{0,64},{64,128},{128,192},{192,256},{256,320},{320,384},{384,448},... | collective-permute-start | bytes 1572872 | tf_op jit(solution)/shard_map/ppermute | solution.py:118
  104.3 17.0 %collective-permute-start.1 = (bf16[256,1024]{1,0:T(8,128)(2,1)S(1)}, bf16[256,1024]{1,0:T(8,128)(2,1)S(1)}, u32[]{:S(2)}, u32[]{:S(2)}) collective-permute-start(bf16[256,1024]{1,0:T(8,128)(2,1)S(1)} %reshape.219), channel_id=1, source_target_pairs={{0,449},{64,0},{128,64},{192,128},{256,192},{320,256},{384,320},{4... | collective-permute-start | bytes 1572872 | tf_op jit(solution)/shard_map/ppermute | solution.py:118
  108.2 26.1 %collective-permute-start.2 = (bf16[256,1024]{1,0:T(8,128)(2,1)S(1)}, bf16[256,1024]{1,0:T(8,128)(2,1)S(1)}, u32[]{:S(2)}, u32[]{:S(2)}) collective-permute-start(bf16[256,1024]{1,0:T(8,128)(2,1)S(1)} %reshape.219), channel_id=1, source_target_pairs={{0,128},{64,192},{128,256},{192,320},{256,384},{320,448},{384,1},{... | collective-permute-start | bytes 1572872 | tf_op jit(solution)/shard_map/ppermute | solution.py:118
  139.6 33.3 %all-to-all-start.3 = ((bf16[4,256,1024]{2,1,0:T(8,128)(2,1)}), bf16[4,256,1024]{2,1,0:T(8,128)(2,1)S(1)}, u32[]{:S(2)}, u32[]{:S(2)}) async-start(bf16[4,256,1024]{2,1,0:T(8,128)(2,1)} %bitcast.85), calls=%async_computation.3 | async-start | bytes 4194304 | tf_op jit(solution)/shard_map/all_to_all | solution.py:28
  147.4 59.5 %collective-permute-start.6 = (bf16[512,512]{1,0:T(8,128)(2,1)}, bf16[512,512]{1,0:T(8,128)(2,1)}, u32[]{:S(2)}, u32[]{:S(2)}) collective-permute-start(bf16[512,512]{1,0:T(8,128)(2,1)} %bitcast.28), channel_id=1, source_target_pairs={{0,1},{1,0},{2,3},{3,2},{4,5},{5,4},{6,7},{7,6},{8,9},{9,8},{10,11... | collective-permute-start | bytes 1572872 | tf_op jit(solution)/shard_map/ppermute | solution.py:83
  174.4 33.7 %all-to-all-start.4 = ((bf16[4,256,512]{2,1,0:T(8,128)(2,1)}), bf16[4,256,512]{2,1,0:T(8,128)(2,1)S(1)}, u32[]{:S(2)}, u32[]{:S(2)}) async-start(bf16[4,256,512]{2,1,0:T(8,128)(2,1)} %broadcast_in_dim.56), calls=%async_computation.4 | async-start | bytes 2097152 | tf_op jit(solution)/shard_map/all_to_all | solution.py:28
  209.5 28.0 %collective-permute-start.7 = (bf16[256,1024]{1,0:T(8,128)(2,1)S(1)}, bf16[256,1024]{1,0:T(8,128)(2,1)S(1)}, u32[]{:S(2)}, u32[]{:S(2)}) collective-permute-start(bf16[256,1024]{1,0:T(8,128)(2,1)S(1)} %get-tuple-element.11), channel_id=1, source_target_pairs={{0,449},{64,0},{128,64},{192,128},{256,192},{320,256},{384,320},{4... | collective-permute-start | bytes 1572872 | tf_op jit(solution)/shard_map/ppermute | solution.py:132
  211.5 26.1 %collective-permute-start.8 = (bf16[256,1024]{1,0:T(8,128)(2,1)S(1)}, bf16[256,1024]{1,0:T(8,128)(2,1)S(1)}, u32[]{:S(2)}, u32[]{:S(2)}) collective-permute-start(bf16[256,1024]{1,0:T(8,128)(2,1)S(1)} %get-tuple-element.13), channel_id=1, source_target_pairs={{0,64},{64,128},{128,192},{192,256},{256,320},{320,384},{384,448},... | collective-permute-start | bytes 1572872 | tf_op jit(solution)/shard_map/ppermute | solution.py:132
  216.6 28.4 %collective-permute-start.9 = (bf16[256,1024]{1,0:T(8,128)(2,1)S(1)}, bf16[256,1024]{1,0:T(8,128)(2,1)S(1)}, u32[]{:S(2)}, u32[]{:S(2)}) collective-permute-start(bf16[256,1024]{1,0:T(8,128)(2,1)S(1)} %get-tuple-element.12), channel_id=1, source_target_pairs={{0,385},{64,449},{128,0},{192,64},{256,128},{320,192},{384,256},{4... | collective-permute-start | bytes 1572872 | tf_op jit(solution)/shard_map/ppermute | solution.py:132
  245.0 16.8 %copy-start.4 = (f32[1,4,2]{1,2,0:T(2,128)S(1)}, f32[1,4,2]{1,2,0:T(2,128)}, u32[]{:S(2)}) copy-start(f32[1,4,2]{1,2,0:T(2,128)} %param.17) | copy-start | bytes 100
  246.4 48.9 %all-to-all-start.5 = ((bf16[128,2,1024]{2,1,0:T(2,128)(2,1)}), bf16[128,2,1024]{2,1,0:T(2,128)(2,1)S(1)}, u32[]{:S(2)}, u32[]{:S(2)}) async-start(bf16[128,2,1024]{2,1,0:T(2,128)(2,1)} %reshape.225), calls=%async_computation.5 | async-start | bytes 1048576 | tf_op jit(solution)/shard_map/all_to_all | solution.py:28
where the time goes:
time: 298 us; the launch traced here: 297 us
  waiting for transfers between devices  144 us (48%)
  starting transfers between devices  96.1 us (32%)
  local copies, waits for them, and re-layouts  21 us (7%)
  blocking collectives  19.3 us (6%)
  matrix products  9.28 us (3%)
  other arithmetic  6.76 us (2%)
    all_to_all x5, waiting for transfers between devices, exchange(): return lax.all_to_all(value, axes, 0, 0, tiled=True)  72.3 us
    all_to_all x5, starting transfers between devices, exchange(): return lax.all_to_all(value, axes, 0, 0, tiled=True)  49.6 us
    ppermute x1, waiting for transfers between devices, layer(): other = lax.ppermute(sent, 'pair', [(0, 1), (1, 0)])  28.9 us
    ppermute x3, waiting for transfers between devices, layer(): back = lax.ppermute(blocks[k + 1].astype(BF16), Z_AXES, z_shift(-d))  26.1 us
    ppermute x3, starting transfers between devices, layer(): window = [rows] + [lax.ppermute(rows, Z_AXES, z_shift(d)) for d in steps]  19.4 us
    all_to_all x1, blocking collectives, exchange(): return lax.all_to_all(value, axes, 0, 0, tiled=True)  19.3 us
    ppermute x3, waiting for transfers between devices, layer(): window = [rows] + [lax.ppermute(rows, Z_AXES, z_shift(d)) for d in steps]  16.8 us
    ppermute x3, starting transfers between devices, layer(): lax.ppermute(block, 'hidden', [(i, (i + d) % xs) for i in range(xs)])  10.9 us
  transfers between devices with their start and end apart: 15, of which 10 were waited for; matrix products, arithmetic and copies ran while one was open for 7% of the time, Pallas kernels for 0%

commit v1 on v0

--- a/solution.py
+++ b/solution.py
@@ -13,15 +13,17 @@
 
 
 ATTN = ("ab", "aa")
-Z_AXES = ("ab", "aa", "pair")
+Z_AXES = ("ab", "aa", "core", "pair")
 ROUTE = ("y", "core", "pair", "ab", "hidden")
 
 
-def z_shift(step):
-    def place(z):
-        return ((z % 8) // 4) * 8 + (z % 4) * 2 + z // 8
+def z_shift(steps):
+    def place(z, core):
+        return (((z % 8) * 2) + core) * 2 + z // 8
 
-    return [(place(z), place((z + step) % 16)) for z in range(16)]
+    return [
+        (place(z, core), place((z + steps[core]) % 16, core)) for z in range(16) for core in (0, 1)
+    ]
 
 
 def exchange(value, axes):
@@ -78,12 +80,10 @@
     unit = gate_up_weight.shape[-1]
     down = down_weight[0].reshape(xs, pairs, unit, -1)
     width = down.shape[-1]
-    kept = lax.dynamic_index_in_dim(down, z_hi, 1, keepdims=False).reshape(xs * unit, width)
-    sent = lax.dynamic_index_in_dim(down, 1 - z_hi, 1, keepdims=False).reshape(xs * unit, width)
-    other = lax.ppermute(sent, "pair", [(0, 1), (1, 0)])
-    down = jnp.concatenate(
-        [jnp.where(z_hi == 0, kept, other), jnp.where(z_hi == 0, other, kept)], axis=1
-    )
+    kept = lax.dynamic_index_in_dim(down, z_hi, 1, keepdims=False)
+    sent = lax.dynamic_index_in_dim(down, 1 - z_hi, 1, keepdims=False)
+    swap = [(0, 1), (1, 0)]
+    other_a = lax.ppermute(sent[: xs // 2], "pair", swap)
 
     heads_out = attention(queries[0], keys[0], values[0], doc_lengths[0])
     tok_group = heads_out.shape[0]
@@ -92,7 +92,6 @@
     projected = projected.reshape(zl, xs, owned, D).transpose(1, 0, 2, 3)
     projected = jnp.sum(exchange(projected, "hidden").astype(F32), axis=0).astype(BF16)
     gate_up = gate_up_weight[0].reshape(2, xs, chunk, unit)
-    projected, gate_up = lax.optimization_barrier((projected, gate_up))
     me = lax.axis_index("hidden")
     gathered = jnp.zeros((xs, 2, chunk, unit), BF16)
     for d in range(xs):
@@ -114,22 +113,29 @@
     far = lax.axis_size(("pair", "ab"))
     outgoing = jnp.broadcast_to(picked, (experts, far, xs, capacity, chunk))
     rows = exchange(outgoing.reshape(-1, capacity, chunk), ROUTE).reshape(-1, chunk)
-    steps = (1, -1, 2)
+    steps = ((1, 1), (-1, -1), (2, -2))
     window = [rows] + [lax.ppermute(rows, Z_AXES, z_shift(d)) for d in steps]
 
     rows = jnp.concatenate(window, axis=0)
     partial = jnp.dot(rows, gate_up, preferred_element_type=F32).astype(BF16)
     partial = partial.reshape(xs, -1, partial.shape[1])
+    partial, sent_b = lax.optimization_barrier((partial, sent[xs // 2 :]))
+    other_b = lax.ppermute(sent_b, "pair", swap)
     summed = jnp.sum(exchange(partial, "hidden").astype(F32), axis=0)
     half = xs * unit
     activated = (jax.nn.silu(summed[:, :half]) * summed[:, half:]).astype(BF16)
     activated = exchange(jnp.broadcast_to(activated, (xs, *activated.shape)), "hidden")
     activated = activated.reshape(-1, half)
+    kept = kept.reshape(half, width)
+    other = jnp.concatenate([other_a, other_b], axis=0).reshape(half, width)
+    down = jnp.concatenate(
+        [jnp.where(z_hi == 0, kept, other), jnp.where(z_hi == 0, other, kept)], axis=1
+    )
     out = jnp.dot(activated, down, preferred_element_type=F32)
     blocks = out.reshape(len(window), -1, chunk)
     total = blocks[0]
-    for k, d in enumerate(steps):
-        back = lax.ppermute(blocks[k + 1].astype(BF16), Z_AXES, z_shift(-d))
+    for n, d in enumerate(steps):
+        back = lax.ppermute(blocks[n + 1].astype(BF16), Z_AXES, z_shift([-k for k in d]))
         total = total + back.astype(F32)
 
     total = total.astype(BF16).reshape(-1, capacity, chunk)

time: 298 us -> 310 us (1.040)
  the two profiles are of different devices: /device:TPU:96 before, /device:TPU:33 now
where the time goes in v1:
time: 310 us; the launch traced here: 308 us
  waiting for transfers between devices  139 us (45%)
  starting transfers between devices  87.7 us (28%)
  blocking collectives  45 us (15%)
  local copies, waits for them, and re-layouts  22.2 us (7%)
  other arithmetic  6.71 us (2%)
  matrix products  6.36 us (2%)
    all_to_all x4, waiting for transfers between devices, exchange(): return lax.all_to_all(value, axes, 0, 0, tiled=True)  62 us
    all_to_all x4, starting transfers between devices, exchange(): return lax.all_to_all(value, axes, 0, 0, tiled=True)  45.5 us
    all_to_all x2, blocking collectives, exchange(): return lax.all_to_all(value, axes, 0, 0, tiled=True)  45 us
    ppermute x1, waiting for transfers between devices, layer(): other_a = lax.ppermute(sent[:xs // 2], 'pair', swap)  29.7 us
    ppermute x3, waiting for transfers between devices, layer(): lax.ppermute(blocks[n + 1].astype(BF16), Z_AXES, z_shift([-k for k in d]))  19.5 us
    ppermute x3, waiting for transfers between devices, layer(): window = [rows] + [lax.ppermute(rows, Z_AXES, z_shift(d)) for d in steps]  18.1 us
    ppermute x1, starting transfers between devices, layer(): other_b = lax.ppermute(sent_b, 'pair', swap)  12.1 us
    ppermute x3, starting transfers between devices, layer(): lax.ppermute(block, 'hidden', [(i, (i + d) % xs) for i in range(xs)])  10.6 us
  transfers between devices with their start and end apart: 15, of which 11 were waited for; matrix products, arithmetic and copies ran while one was open for 6% of the time, Pallas kernels for 0%

profile of v1, /device:TPU:33, one launch (start us, length us, event | category | flops | bytes accessed | tf_op | source)
XLA Modules:
  0.0 308.0 jit_solution(8706455941087481306)
XLA Ops:
  4.3 18.2 %all_to_all.30 = bf16[4,8,4,4096]{3,2,1,0:T(4,128)(2,1)S(1)} all-to-all(bf16[4,8,4,4096]{3,2,1,0:T(4,128)(2,1)S(1)} %bitcast.88), channel_id=1, replica_groups=mesh['ab'=2,'aa'=4,'y'=4,'core'=2,'hidden'=4,'pair'=2] {'hidden'}, dimensions={0} | all-to-all | bytes 2097152 | tf_op jit(solution)/shard_map/all_to_all | solution.py:30
  23.8 12.2 %all-to-all-start.1 = ((bf16[8,4,4096]{2,1,0:T(4,128)(2,1)}), bf16[8,4,4096]{2,1,0:T(4,128)(2,1)S(1)}, u32[]{:S(2)}, u32[]{:S(2)}) async-start(bf16[8,4,4096]{2,1,0:T(4,128)(2,1)} %reduce_sum.82), calls=%async_computation.1 | async-start | bytes 524288 | tf_op jit(solution)/shard_map/all_to_all | solution.py:30
  36.7 12.5 %all-to-all-done.1 = bf16[8,4,4096]{2,1,0:T(4,128)(2,1)S(1)} async-done(((bf16[8,4,4096]{2,1,0:T(4,128)(2,1)}), bf16[8,4,4096]{2,1,0:T(4,128)(2,1)S(1)}, u32[]{:S(2)}, u32[]{:S(2)}) %all-to-all-start.1) | async-done | bytes 262176 | tf_op jit(solution)/shard_map/all_to_all | solution.py:30
  51.4 17.0 %all-to-all-start.2 = ((bf16[128,2,1024]{2,1,0:T(2,128)(2,1)}), bf16[128,2,1024]{2,1,0:T(2,128)(2,1)}, u32[]{:S(2)}, u32[]{:S(2)}) async-start(bf16[128,2,1024]{2,1,0:T(2,128)(2,1)} %bitcast.13), calls=%async_computation.2 | async-start | bytes 1048576 | tf_op jit(solution)/shard_map/all_to_all | solution.py:30
  69.8 2.1 copy.76
  72.0 3.2 %collective-permute-start.3 = (bf16[2,1024,128]{1,2,0:T(8,128)(2,1)}, bf16[2,1024,128]{1,2,0:T(8,128)(2,1)}, u32[]{:S(2)}, u32[]{:S(2)}) collective-permute-start(bf16[2,1024,128]{1,2,0:T(8,128)(2,1)} %bitcast.16), channel_id=1, source_target_pairs={{0,2},{2,4},{4,6},{6,0},{1,3},{3,5},{5,7},{7,1},{8,10},{10,12},{12... | collective-permute-start | bytes 1572872 | tf_op jit(solution)/shard_map/ppermute | solution.py:100
  75.2 2.0 copy.77
  77.3 4.3 %collective-permute-start.4 = (bf16[2,1024,128]{1,2,0:T(8,128)(2,1)}, bf16[2,1024,128]{1,2,0:T(8,128)(2,1)}, u32[]{:S(2)}, u32[]{:S(2)}) collective-permute-start(bf16[2,1024,128]{1,2,0:T(8,128)(2,1)} %bitcast.18), channel_id=1, source_target_pairs={{0,4},{2,6},{4,0},{6,2},{1,5},{3,7},{5,1},{7,3},{8,12},{10,14},{12... | collective-permute-start | bytes 1572872 | tf_op jit(solution)/shard_map/ppermute | solution.py:100
  82.6 3.1 collective-permute-start.5
  87.8 2.1 constant_dynamic-slice_fusion
  90.0 14.2 %all-to-all-done.2 = bf16[128,2,1024]{2,1,0:T(2,128)(2,1)} async-done(((bf16[128,2,1024]{2,1,0:T(2,128)(2,1)}), bf16[128,2,1024]{2,1,0:T(2,128)(2,1)}, u32[]{:S(2)}, u32[]{:S(2)}) %all-to-all-start.2) | async-done | bytes 524320 | tf_op jit(solution)/shard_map/all_to_all | solution.py:30
  104.2 2.0 reshape.220
  106.2 2.0 collective-permute-start
  108.3 3.4 %collective-permute-start.1 = (bf16[256,1024]{1,0:T(8,128)(2,1)}, bf16[256,1024]{1,0:T(8,128)(2,1)S(1)}, u32[]{:S(2)}, u32[]{:S(2)}) collective-permute-start(bf16[256,1024]{1,0:T(8,128)(2,1)} %reshape.220), channel_id=1, source_target_pairs={{0,449},{8,457},{64,0},{72,8},{128,64},{136,72},{192,128},{200,136... | collective-permute-start | bytes 1572872 | tf_op jit(solution)/shard_map/ppermute | solution.py:117
  111.6 1.9 collective-permute-start.2
  116.9 4.2 %collective-permute-done = bf16[256,1024]{1,0:T(8,128)(2,1)S(1)} collective-permute-done((bf16[256,1024]{1,0:T(8,128)(2,1)}, bf16[256,1024]{1,0:T(8,128)(2,1)S(1)}, u32[]{:S(2)}, u32[]{:S(2)}) %collective-permute-start) | collective-permute-done | bytes 524320 | tf_op jit(solution)/shard_map/ppermute | solution.py:117
  122.7 12.3 %collective-permute-done.2 = bf16[256,1024]{1,0:T(8,128)(2,1)S(1)} collective-permute-done((bf16[256,1024]{1,0:T(8,128)(2,1)}, bf16[256,1024]{1,0:T(8,128)(2,1)S(1)}, u32[]{:S(2)}, u32[]{:S(2)}) %collective-permute-start.2) | collective-permute-done | bytes 524320 | tf_op jit(solution)/shard_map/ppermute | solution.py:117
  134.9 2.4 fusion.8
  137.3 26.8 %all_to_all.31 = bf16[4,256,1024]{2,1,0:T(8,128)(2,1)S(1)} all-to-all(bf16[4,256,1024]{2,1,0:T(8,128)(2,1)S(1)} %bitcast.90), channel_id=1, replica_groups=mesh['ab'=2,'aa'=4,'y'=4,'core'=2,'hidden'=4,'pair'=2] {'hidden'}, dimensions={0} | all-to-all | bytes 4194304 | tf_op jit(solution)/shard_map/all_to_all | solution.py:30
  165.8 3.5 %all-to-all-start.4 = ((bf16[4,256,512]{2,1,0:T(8,128)(2,1)}), bf16[4,256,512]{2,1,0:T(8,128)(2,1)S(1)}, u32[]{:S(2)}, u32[]{:S(2)}) async-start(bf16[4,256,512]{2,1,0:T(8,128)(2,1)} %broadcast_in_dim.56), calls=%async_computation.4 | async-start | bytes 2097152 | tf_op jit(solution)/shard_map/all_to_all | solution.py:30
  170.3 1.9 collective-permute-start.6
  172.2 12.1 %collective-permute-start.7 = (bf16[2,128,512]{2,1,0:T(8,128)(2,1)S(1)}, bf16[2,128,512]{2,1,0:T(8,128)(2,1)S(1)}, u32[]{:S(2)}, u32[]{:S(2)}) collective-permute-start(bf16[2,128,512]{2,1,0:T(8,128)(2,1)S(1)} %slice_bitcast_fusion), channel_id=1, source_target_pairs={{0,1},{1,0},{2,3},{3,2},{4,5},{5,4},{6,7},{7,6},{8,9},{9,8},{10,11... | collective-permute-start | bytes 786440 | tf_op jit(solution)/shard_map/ppermute | solution.py:123
  184.3 29.7 %collective-permute-done.6 = bf16[2,128,512]{2,1,0:T(8,128)(2,1)S(1)} collective-permute-done((bf16[2,128,512]{2,1,0:T(8,128)(2,1)S(1)}, bf16[2,128,512]{2,1,0:T(8,128)(2,1)S(1)}, u32[]{:S(2)}, u32[]{:S(2)}) %collective-permute-start.6) | collective-permute-done | bytes 262176 | tf_op jit(solution)/shard_map/ppermute | solution.py:86
  214.0 10.2 %collective-permute-done.7 = bf16[2,128,512]{2,1,0:T(8,128)(2,1)S(1)} collective-permute-done((bf16[2,128,512]{2,1,0:T(8,128)(2,1)S(1)}, bf16[2,128,512]{2,1,0:T(8,128)(2,1)S(1)}, u32[]{:S(2)}, u32[]{:S(2)}) %collective-permute-start.7) | collective-permute-done | bytes 262176 | tf_op jit(solution)/shard_map/ppermute | solution.py:123
  226.8 1.9 collective-permute-start.10
  228.7 6.4 %collective-permute-start.8 = (bf16[256,1024]{1,0:T(8,128)(2,1)S(1)}, bf16[256,1024]{1,0:T(8,128)(2,1)S(1)}, u32[]{:S(2)}, u32[]{:S(2)}) collective-permute-start(bf16[256,1024]{1,0:T(8,128)(2,1)S(1)} %get-tuple-element.11), channel_id=1, source_target_pairs={{0,449},{8,457},{64,0},{72,8},{128,64},{136,72},{192,128},{200,136... | collective-permute-start | bytes 1572872 | tf_op jit(solution)/shard_map/ppermute | solution.py:138
  235.1 1.9 collective-permute-start.9
  237.1 7.4 %collective-permute-done.10 = bf16[256,1024]{1,0:T(8,128)(2,1)S(1)} collective-permute-done((bf16[256,1024]{1,0:T(8,128)(2,1)S(1)}, bf16[256,1024]{1,0:T(8,128)(2,1)S(1)}, u32[]{:S(2)}, u32[]{:S(2)}) %collective-permute-start.10) | collective-permute-done | bytes 524320 | tf_op jit(solution)/shard_map/ppermute | solution.py:138
  244.5 7.9 %collective-permute-done.8 = bf16[256,1024]{1,0:T(8,128)(2,1)S(1)} collective-permute-done((bf16[256,1024]{1,0:T(8,128)(2,1)S(1)}, bf16[256,1024]{1,0:T(8,128)(2,1)S(1)}, u32[]{:S(2)}, u32[]{:S(2)}) %collective-permute-start.8) | collective-permute-done | bytes 524320 | tf_op jit(solution)/shard_map/ppermute | solution.py:138
  252.4 4.2 %collective-permute-done.9 = bf16[256,1024]{1,0:T(8,128)(2,1)S(1)} collective-permute-done((bf16[256,1024]{1,0:T(8,128)(2,1)S(1)}, bf16[256,1024]{1,0:T(8,128)(2,1)S(1)}, u32[]{:S(2)}, u32[]{:S(2)}) %collective-permute-start.9) | collective-permute-done | bytes 524320 | tf_op jit(solution)/shard_map/ppermute | solution.py:138
  257.9 12.8 %all-to-all-start.5 = ((bf16[128,2,1024]{2,1,0:T(2,128)(2,1)}), bf16[128,2,1024]{2,1,0:T(2,128)(2,1)S(1)}, u32[]{:S(2)}, u32[]{:S(2)}) async-start(bf16[128,2,1024]{2,1,0:T(2,128)(2,1)} %reshape.226), calls=%async_computation.5 | async-start | bytes 1048576 | tf_op jit(solution)/shard_map/all_to_all | solution.py:30
  270.9 35.4 %all-to-all-done.5 = bf16[128,2,1024]{2,1,0:T(2,128)(2,1)S(1)} async-done(((bf16[128,2,1024]{2,1,0:T(2,128)(2,1)}), bf16[128,2,1024]{2,1,0:T(2,128)(2,1)S(1)}, u32[]{:S(2)}, u32[]{:S(2)}) %all-to-all-start.5) | async-done | bytes 524320 | tf_op jit(solution)/shard_map/all_to_all | solution.py:30
  (74 shorter events, 26.2 us)
Async XLA Ops:
  0.0 2.0 copy-start
  4.2 31.8 %copy-start.8 = (s32[1,4,2]{1,2,0:T(2,128)S(1)}, s32[1,4,2]{1,2,0:T(2,128)}, u32[]{:S(2)}) copy-start(s32[1,4,2]{1,2,0:T(2,128)} %param.18) | copy-start | bytes 100
  4.2 45.3 %copy-start.6 = (bf16[1,4,4096]{2,1,0:T(4,128)(2,1)S(1)}, bf16[1,4,4096]{2,1,0:T(4,128)(2,1)}, u32[]{:S(2)}) copy-start(bf16[1,4,4096]{2,1,0:T(4,128)(2,1)} %param.15) | copy-start | bytes 98308
  4.2 45.4 %copy-start.7 = (f32[4096]{0:T(1024)S(1)}, f32[4096]{0:T(1024)}, u32[]{:S(2)}) copy-start(f32[4096]{0:T(1024)} %param.16) | copy-start | bytes 49156
  23.8 44.6 %copy-start.2 = (bf16[1,2,4096,128]{3,2,1,0:T(8,128)(2,1)S(1)}, bf16[1,2,4096,128]{3,2,1,0:T(8,128)(2,1)}, u32[]{:S(2)}) copy-start(bf16[1,2,4096,128]{3,2,1,0:T(8,128)(2,1)} %param.20) | copy-start | bytes 6291460
  23.8 25.4 %all-to-all-start.1 = ((bf16[8,4,4096]{2,1,0:T(4,128)(2,1)}), bf16[8,4,4096]{2,1,0:T(4,128)(2,1)S(1)}, u32[]{:S(2)}, u32[]{:S(2)}) async-start(bf16[8,4,4096]{2,1,0:T(4,128)(2,1)} %reduce_sum.82), calls=%async_computation.1 | async-start | bytes 524288 | tf_op jit(solution)/shard_map/all_to_all | solution.py:30
  51.4 52.8 %all-to-all-start.2 = ((bf16[128,2,1024]{2,1,0:T(2,128)(2,1)}), bf16[128,2,1024]{2,1,0:T(2,128)(2,1)}, u32[]{:S(2)}, u32[]{:S(2)}) async-start(bf16[128,2,1024]{2,1,0:T(2,128)(2,1)} %bitcast.13), calls=%async_computation.2 | async-start | bytes 1048576 | tf_op jit(solution)/shard_map/all_to_all | solution.py:30
  69.8 11.8 %copy-start.4 = (bf16[2,1,1024,128]{3,2,1,0:T(8,128)(2,1)S(1)}, bf16[2,1,1024,128]{3,2,1,0:T(8,128)(2,1)}, u32[]{:S(2)}) copy-start(bf16[2,1,1024,128]{3,2,1,0:T(8,128)(2,1)} %get-tuple-element.14) | copy-start | bytes 1572868
  69.8 15.9 %copy-start.3 = (bf16[2,1,1024,128]{3,2,1,0:T(8,128)(2,1)S(1)}, bf16[2,1,1024,128]{3,2,1,0:T(8,128)(2,1)}, u32[]{:S(2)}) copy-start(bf16[2,1,1024,128]{3,2,1,0:T(8,128)(2,1)} %get-tuple-element.17) | copy-start | bytes 1572868
  72.0 39.6 %collective-permute-start.3 = (bf16[2,1024,128]{1,2,0:T(8,128)(2,1)}, bf16[2,1024,128]{1,2,0:T(8,128)(2,1)}, u32[]{:S(2)}, u32[]{:S(2)}) collective-permute-start(bf16[2,1024,128]{1,2,0:T(8,128)(2,1)} %bitcast.16), channel_id=1, source_target_pairs={{0,2},{2,4},{4,6},{6,0},{1,3},{3,5},{5,7},{7,1},{8,10},{10,12},{12... | collective-permute-start | bytes 1572872 | tf_op jit(solution)/shard_map/ppermute | solution.py:100
  77.3 37.4 %collective-permute-start.4 = (bf16[2,1024,128]{1,2,0:T(8,128)(2,1)}, bf16[2,1024,128]{1,2,0:T(8,128)(2,1)}, u32[]{:S(2)}, u32[]{:S(2)}) collective-permute-start(bf16[2,1024,128]{1,2,0:T(8,128)(2,1)} %bitcast.18), channel_id=1, source_target_pairs={{0,4},{2,6},{4,0},{6,2},{1,5},{3,7},{5,1},{7,3},{8,12},{10,14},{12... | collective-permute-start | bytes 1572872 | tf_op jit(solution)/shard_map/ppermute | solution.py:100
  82.6 33.1 %collective-permute-start.5 = (bf16[2,1024,128]{1,2,0:T(8,128)(2,1)}, bf16[2,1024,128]{1,2,0:T(8,128)(2,1)}, u32[]{:S(2)}, u32[]{:S(2)}) collective-permute-start(bf16[2,1024,128]{1,2,0:T(8,128)(2,1)} %bitcast.20), channel_id=1, source_target_pairs={{0,6},{2,0},{4,2},{6,4},{1,7},{3,1},{5,3},{7,5},{8,14},{10,8},{12,... | collective-permute-start | bytes 1572872 | tf_op jit(solution)/shard_map/ppermute | solution.py:100
  86.7 1.0 copy-start.1
  106.2 28.7 %copy-start.5 = (bf16[256,1024]{1,0:T(8,128)(2,1)S(1)}, bf16[256,1024]{1,0:T(8,128)(2,1)}, u32[]{:S(2)}) copy-start(bf16[256,1024]{1,0:T(8,128)(2,1)} %reshape.220) | copy-start | bytes 1572868
  106.2 14.8 %collective-permute-start = (bf16[256,1024]{1,0:T(8,128)(2,1)}, bf16[256,1024]{1,0:T(8,128)(2,1)S(1)}, u32[]{:S(2)}, u32[]{:S(2)}) collective-permute-start(bf16[256,1024]{1,0:T(8,128)(2,1)} %reshape.220), channel_id=1, source_target_pairs={{0,64},{8,72},{64,128},{72,136},{128,192},{136,200},{192,256},{200... | collective-permute-start | bytes 1572872 | tf_op jit(solution)/shard_map/ppermute | solution.py:117
  108.3 14.4 %collective-permute-start.1 = (bf16[256,1024]{1,0:T(8,128)(2,1)}, bf16[256,1024]{1,0:T(8,128)(2,1)S(1)}, u32[]{:S(2)}, u32[]{:S(2)}) collective-permute-start(bf16[256,1024]{1,0:T(8,128)(2,1)} %reshape.220), channel_id=1, source_target_pairs={{0,449},{8,457},{64,0},{72,8},{128,64},{136,72},{192,128},{200,136... | collective-permute-start | bytes 1572872 | tf_op jit(solution)/shard_map/ppermute | solution.py:117
  111.6 23.3 %collective-permute-start.2 = (bf16[256,1024]{1,0:T(8,128)(2,1)}, bf16[256,1024]{1,0:T(8,128)(2,1)S(1)}, u32[]{:S(2)}, u32[]{:S(2)}) collective-permute-start(bf16[256,1024]{1,0:T(8,128)(2,1)} %reshape.220), channel_id=1, source_target_pairs={{0,128},{8,393},{64,192},{72,457},{128,256},{136,8},{192,320},{200... | collective-permute-start | bytes 1572872 | tf_op jit(solution)/shard_map/ppermute | solution.py:117
  165.8 59.7 %all-to-all-start.4 = ((bf16[4,256,512]{2,1,0:T(8,128)(2,1)}), bf16[4,256,512]{2,1,0:T(8,128)(2,1)S(1)}, u32[]{:S(2)}, u32[]{:S(2)}) async-start(bf16[4,256,512]{2,1,0:T(8,128)(2,1)} %broadcast_in_dim.56), calls=%async_computation.4 | async-start | bytes 2097152 | tf_op jit(solution)/shard_map/all_to_all | solution.py:30
  170.3 43.7 %collective-permute-start.6 = (bf16[2,128,512]{2,1,0:T(8,128)(2,1)S(1)}, bf16[2,128,512]{2,1,0:T(8,128)(2,1)S(1)}, u32[]{:S(2)}, u32[]{:S(2)}) collective-permute-start(bf16[2,128,512]{2,1,0:T(8,128)(2,1)S(1)} %dynamic-slice_bitcast_fusion.1), channel_id=1, source_target_pairs={{0,1},{1,0},{2,3},{3,2},{4,5},{5,4},{6,7},{7,6},{8,9},{9,8},{10,11... | collective-permute-start | bytes 786440 | tf_op jit(solution)/shard_map/ppermute | solution.py:86
  172.2 52.0 %collective-permute-start.7 = (bf16[2,128,512]{2,1,0:T(8,128)(2,1)S(1)}, bf16[2,128,512]{2,1,0:T(8,128)(2,1)S(1)}, u32[]{:S(2)}, u32[]{:S(2)}) collective-permute-start(bf16[2,128,512]{2,1,0:T(8,128)(2,1)S(1)} %slice_bitcast_fusion), channel_id=1, source_target_pairs={{0,1},{1,0},{2,3},{3,2},{4,5},{5,4},{6,7},{7,6},{8,9},{9,8},{10,11... | collective-permute-start | bytes 786440 | tf_op jit(solution)/shard_map/ppermute | solution.py:123
  226.8 17.7 %collective-permute-start.10 = (bf16[256,1024]{1,0:T(8,128)(2,1)S(1)}, bf16[256,1024]{1,0:T(8,128)(2,1)S(1)}, u32[]{:S(2)}, u32[]{:S(2)}) collective-permute-start(bf16[256,1024]{1,0:T(8,128)(2,1)S(1)} %get-tuple-element.12), channel_id=1, source_target_pairs={{0,385},{8,136},{64,449},{72,200},{128,0},{136,264},{192,64},{200,... | collective-permute-start | bytes 1572872 | tf_op jit(solution)/shard_map/ppermute | solution.py:138
  228.7 23.6 %collective-permute-start.8 = (bf16[256,1024]{1,0:T(8,128)(2,1)S(1)}, bf16[256,1024]{1,0:T(8,128)(2,1)S(1)}, u32[]{:S(2)}, u32[]{:S(2)}) collective-permute-start(bf16[256,1024]{1,0:T(8,128)(2,1)S(1)} %get-tuple-element.11), channel_id=1, source_target_pairs={{0,449},{8,457},{64,0},{72,8},{128,64},{136,72},{192,128},{200,136... | collective-permute-start | bytes 1572872 | tf_op jit(solution)/shard_map/ppermute | solution.py:138
  235.1 21.4 %collective-permute-start.9 = (bf16[256,1024]{1,0:T(8,128)(2,1)S(1)}, bf16[256,1024]{1,0:T(8,128)(2,1)S(1)}, u32[]{:S(2)}, u32[]{:S(2)}) collective-permute-start(bf16[256,1024]{1,0:T(8,128)(2,1)S(1)} %get-tuple-element.13), channel_id=1, source_target_pairs={{0,64},{8,72},{64,128},{72,136},{128,192},{136,200},{192,256},{200... | collective-permute-start | bytes 1572872 | tf_op jit(solution)/shard_map/ppermute | solution.py:138
  256.5 14.3 %copy-start.9 = (f32[1,4,2]{1,2,0:T(2,128)S(1)}, f32[1,4,2]{1,2,0:T(2,128)}, u32[]{:S(2)}) copy-start(f32[1,4,2]{1,2,0:T(2,128)} %param.17) | copy-start | bytes 100
  257.9 48.3 %all-to-all-start.5 = ((bf16[128,2,1024]{2,1,0:T(2,128)(2,1)}), bf16[128,2,1024]{2,1,0:T(2,128)(2,1)S(1)}, u32[]{:S(2)}, u32[]{:S(2)}) async-start(bf16[128,2,1024]{2,1,0:T(2,128)(2,1)} %reshape.226), calls=%async_computation.5 | async-start | bytes 1048576 | tf_op jit(solution)/shard_map/all_to_all | solution.py:30

commit v2 on v1

--- a/solution.py
+++ b/solution.py
@@ -1,6 +1,7 @@
 import jax
 import jax.numpy as jnp
 from jax import lax
+from jax.experimental import pallas as pl
 from jax.sharding import Mesh
 from jax.sharding import PartitionSpec as P
 
@@ -13,17 +14,9 @@
 
 
 ATTN = ("ab", "aa")
-Z_AXES = ("ab", "aa", "core", "pair")
-ROUTE = ("y", "core", "pair", "ab", "hidden")
-
-
-def z_shift(steps):
-    def place(z, core):
-        return (((z % 8) * 2) + core) * 2 + z // 8
-
-    return [
-        (place(z, core), place((z + steps[core]) % 16, core)) for z in range(16) for core in (0, 1)
-    ]
+Z_AXES = ("pair", "ab", "aa")
+ROUTE = ("hidden", "y", "core")
+LANES = 128
 
 
 def exchange(value, axes):
@@ -44,16 +37,77 @@
     return jnp.dot(probabilities, values, preferred_element_type=F32).astype(BF16)
 
 
-def slot_selector(chosen, experts, capacity):
+def slot_numbers(chosen, place, places, capacity):
     rows = chosen.shape[0]
     row_ids = jnp.arange(rows, dtype=jnp.int32)
     earlier = row_ids[None, :] < row_ids[:, None]
     same = chosen[:, None] == chosen[None, :]
     ranking = jnp.sum((same & earlier).astype(jnp.int32), axis=-1)
-    slots = jnp.arange(experts * capacity, dtype=jnp.int32)
-    return (chosen[None, :] == (slots // capacity)[:, None]) & (
-        ranking[None, :] == (slots % capacity)[:, None]
-    )
+    return (chosen * places + place) * capacity + ranking
+
+
+def note_of(slots, share):
+    high = lax.reduce_precision(share, 8, 7)
+    middle = lax.reduce_precision(share - high, 8, 7)
+    low = share - high - middle
+    parts = jnp.stack([slots[:, 0].astype(F32), slots[:, 1].astype(F32), high, middle, low], axis=1)
+    return jnp.pad(parts, ((0, 0), (0, LANES - 5))).astype(BF16)
+
+
+def pick_kernel(tokens_ref, note_ref, out_ref):
+    note = note_ref[...].astype(F32)
+    slots = lax.broadcasted_iota(jnp.int32, (note.shape[0], out_ref.shape[1]), 1).astype(F32)
+    taken = (slots == note[:, 0:1]) | (slots == note[:, 1:2])
+    out_ref[0] = lax.dot_general(
+        jnp.where(taken, 1.0, 0.0).astype(BF16),
+        tokens_ref[...],
+        (((0,), (0,)), ((), ())),
+        preferred_element_type=F32,
+    ).astype(BF16)
+
+
+def pick_rows(tokens, slots, chunk):
+    count = tokens.shape[0]
+    return pl.pallas_call(
+        pick_kernel,
+        grid=(D // chunk,),
+        in_specs=[
+            pl.BlockSpec((count, chunk), lambda j: (0, j)),
+            pl.BlockSpec((count, LANES), lambda j: (0, D // LANES)),
+        ],
+        out_specs=pl.BlockSpec((1, slots, chunk), lambda j: (j, 0, 0)),
+        out_shape=jax.ShapeDtypeStruct((D // chunk, slots, chunk), BF16),
+        name="pick",
+    )(tokens, tokens)
+
+
+def combine_kernel(note_ref, rows_ref, out_ref):
+    note = note_ref[...].astype(F32)
+    share = note[:, 2:3] + note[:, 3:4] + note[:, 4:5]
+    slots = lax.broadcasted_iota(jnp.int32, (note.shape[0], rows_ref.shape[1]), 1).astype(F32)
+    weight = jnp.where(slots == note[:, 0:1], share, 0.0)
+    weight = weight + jnp.where(slots == note[:, 1:2], 1.0 - share, 0.0)
+    high = weight.astype(BF16)
+    low = (weight - high.astype(F32)).astype(BF16)
+    rows = rows_ref[0]
+    total = jnp.dot(high, rows, preferred_element_type=F32)
+    out_ref[...] = (total + jnp.dot(low, rows, preferred_element_type=F32)).astype(BF16)
+
+
+def combine_rows(note, rows):
+    count = note.shape[0]
+    chunks, slots, chunk = rows.shape
+    return pl.pallas_call(
+        combine_kernel,
+        grid=(chunks,),
+        in_specs=[
+            pl.BlockSpec((count, LANES), lambda j: (0, 0)),
+            pl.BlockSpec((1, slots, chunk), lambda j: (j, 0, 0)),
+        ],
+        out_specs=pl.BlockSpec((count, chunk), lambda j: (0, j)),
+        out_shape=jax.ShapeDtypeStruct((count, chunks * chunk), BF16),
+        name="combine",
+    )(note, rows)
 
 
 def layer(
@@ -82,8 +136,6 @@
     width = down.shape[-1]
     kept = lax.dynamic_index_in_dim(down, z_hi, 1, keepdims=False)
     sent = lax.dynamic_index_in_dim(down, 1 - z_hi, 1, keepdims=False)
-    swap = [(0, 1), (1, 0)]
-    other_a = lax.ppermute(sent[: xs // 2], "pair", swap)
 
     heads_out = attention(queries[0], keys[0], values[0], doc_lengths[0])
     tok_group = heads_out.shape[0]
@@ -105,53 +157,40 @@
     scale = lax.rsqrt(jnp.mean(attended * attended, axis=1, keepdims=True) + EPSILON)
     normed = (attended * scale * norm_gain).astype(BF16)
 
+    places = lax.axis_size(Z_AXES)
     chosen = expert_ids[0].reshape(2 * owned)
-    selector = slot_selector(chosen, experts, capacity)
-    picker = selector[:, 0::2] | selector[:, 1::2]
-    picked = jnp.dot(picker.astype(BF16), normed, preferred_element_type=F32).astype(BF16)
-    picked = picked.reshape(experts, 1, capacity, xs, chunk).transpose(0, 1, 3, 2, 4)
-    far = lax.axis_size(("pair", "ab"))
-    outgoing = jnp.broadcast_to(picked, (experts, far, xs, capacity, chunk))
-    rows = exchange(outgoing.reshape(-1, capacity, chunk), ROUTE).reshape(-1, chunk)
-    steps = ((1, 1), (-1, -1), (2, -2))
-    window = [rows] + [lax.ppermute(rows, Z_AXES, z_shift(d)) for d in steps]
-
-    rows = jnp.concatenate(window, axis=0)
+    slots = slot_numbers(chosen, lax.axis_index(Z_AXES), places, capacity).reshape(owned, 2)
+    logits = route_logits[0]
+    note = note_of(slots, jax.nn.sigmoid(logits[:, 0] - logits[:, 1]))
+    noted = jnp.concatenate([normed, note], axis=1)
+    tokens = exchange(jnp.broadcast_to(noted, (places, *noted.shape)), Z_AXES)
+    tokens = tokens.reshape(places * owned, D + LANES)
+    note = tokens[:, D:]
+
+    group_slots = experts * places * capacity
+    picked = pick_rows(tokens, group_slots, chunk)
+    picked, sent = lax.optimization_barrier((picked, sent))
+    other = lax.ppermute(sent, "pair", [(0, 1), (1, 0)])
+    rows = exchange(picked.reshape(xs * experts, -1, chunk), ROUTE).reshape(-1, chunk)
+
     partial = jnp.dot(rows, gate_up, preferred_element_type=F32).astype(BF16)
     partial = partial.reshape(xs, -1, partial.shape[1])
-    partial, sent_b = lax.optimization_barrier((partial, sent[xs // 2 :]))
-    other_b = lax.ppermute(sent_b, "pair", swap)
     summed = jnp.sum(exchange(partial, "hidden").astype(F32), axis=0)
     half = xs * unit
     activated = (jax.nn.silu(summed[:, :half]) * summed[:, half:]).astype(BF16)
     activated = exchange(jnp.broadcast_to(activated, (xs, *activated.shape)), "hidden")
     activated = activated.reshape(-1, half)
     kept = kept.reshape(half, width)
-    other = jnp.concatenate([other_a, other_b], axis=0).reshape(half, width)
+    other = other.reshape(half, width)
     down = jnp.concatenate(
         [jnp.where(z_hi == 0, kept, other), jnp.where(z_hi == 0, other, kept)], axis=1
     )
-    out = jnp.dot(activated, down, preferred_element_type=F32)
-    blocks = out.reshape(len(window), -1, chunk)
-    total = blocks[0]
-    for n, d in enumerate(steps):
-        back = lax.ppermute(blocks[n + 1].astype(BF16), Z_AXES, z_shift([-k for k in d]))
-        total = total + back.astype(F32)
-
-    total = total.astype(BF16).reshape(-1, capacity, chunk)
-    returned = exchange(total, ROUTE).reshape(experts, far, xs, capacity, chunk)
-    returned = jnp.sum(returned.astype(F32), axis=1).astype(BF16)
-    returned = returned.transpose(0, 2, 1, 3).reshape(experts * capacity, D)
-    per_row = jnp.einsum(
-        "sr,sd->rd", selector.astype(BF16), returned, preferred_element_type=F32
-    ).reshape(owned, 2, D)
-    logits = route_logits[0]
-    first_share = jax.nn.sigmoid(logits[:, 0] - logits[:, 1])
-    layer_out = (
-        attended
-        + first_share[:, None] * per_row[:, 0]
-        + (1.0 - first_share)[:, None] * per_row[:, 1]
-    )
+    out = jnp.dot(activated, down, preferred_element_type=F32).astype(BF16)
+
+    returned = exchange(out.reshape(xs * experts, -1, chunk), ROUTE)
+    returned = combine_rows(note, returned.reshape(xs, group_slots, chunk))
+    mixed = exchange(returned.reshape(places, owned, D), Z_AXES)
+    layer_out = attended + jnp.sum(mixed.astype(F32), axis=0)
     return layer_out.astype(BF16)[None]
 
 

time: 310 us -> 305 us (0.984); the launches traced: 308 us -> 300 us
  starting transfers between devices: 87.7 us -> 67.6 us
  Pallas kernels: 0 us -> 8.46 us
  waiting for transfers between devices: 139 us -> 134 us
  matrix products: 6.36 us -> 11.2 us
  blocking collectives: 45 us -> 49.2 us
    ppermute x8 -> x1, waiting for transfers between devices: 77.5 us -> 0.01 us  [layer(): other = lax.ppermute(sent, 'pair', [(0, 1), (1, 0)])]
    all_to_all x4 -> x7, waiting for transfers between devices: 62 us -> 105 us  [exchange(): return lax.all_to_all(value, axes, 0, 0, tiled=True)]
    ppermute x3, waiting for transfers between devices: 0.01 us -> 28.2 us  [layer(): lax.ppermute(block, 'hidden', [(i, (i + d) % xs) for i in range(xs)])]
    ppermute x8 -> x1, starting transfers between devices: 31.6 us -> 7.92 us  [layer(): other = lax.ppermute(sent, 'pair', [(0, 1), (1, 0)])]
    pallas_call x0 -> x2, Pallas kernels: none -> 8.46 us  [the longest x1 4.25 us: combine_rows(): pl.pallas_call(combine_kernel, grid=(chunks,), in_specs=[pl.BlockSpec((co...]
    all_to_all x2 -> x1, blocking collectives: 45 us -> 49.2 us  [exchange(): return lax.all_to_all(value, axes, 0, 0, tiled=True)]
    all_to_all x4 -> x7, starting transfers between devices: 45.5 us -> 49.1 us  [exchange(): return lax.all_to_all(value, axes, 0, 0, tiled=True)]
    unnamed x25 -> x31, local copies, waits for them, and re-layouts: 7.13 us -> 8.67 us
  transfers between devices with their start and end apart: 15 -> 11, of which waited for: 11 -> 8; matrix products, arithmetic and copies ran while one was open for 6% -> 6% of each run, Pallas kernels for 0% -> 0%
where the time goes in v2:
time: 305 us; the launch traced here: 300 us
  waiting for transfers between devices  134 us (44%)
  starting transfers between devices  67.6 us (22%)
  blocking collectives  49.2 us (16%)
  local copies, waits for them, and re-layouts  22.4 us (7%)
  matrix products  11.2 us (4%)
  Pallas kernels  8.46 us (3%)
  other arithmetic  6.63 us (2%)
    all_to_all x7, waiting for transfers between devices, exchange(): return lax.all_to_all(value, axes, 0, 0, tiled=True)  105 us
    all_to_all x1, blocking collectives, exchange(): return lax.all_to_all(value, axes, 0, 0, tiled=True)  49.2 us
    all_to_all x7, starting transfers between devices, exchange(): return lax.all_to_all(value, axes, 0, 0, tiled=True)  49.1 us
    ppermute x3, waiting for transfers between devices, layer(): lax.ppermute(block, 'hidden', [(i, (i + d) % xs) for i in range(xs)])  28.2 us
    ppermute x3, starting transfers between devices, layer(): lax.ppermute(block, 'hidden', [(i, (i + d) % xs) for i in range(xs)])  10.6 us
    unnamed x31, local copies, waits for them, and re-layouts  8.67 us
    ppermute x1, starting transfers between devices, layer(): other = lax.ppermute(sent, 'pair', [(0, 1), (1, 0)])  7.92 us
  transfers between devices with their start and end apart: 11, of which 8 were waited for; matrix products, arithmetic and copies ran while one was open for 6% of the time, Pallas kernels for 0%

profile of v2, /device:TPU:33, one launch (start us, length us, event | category | flops | bytes accessed | tf_op | source)
XLA Modules:
  0.0 299.6 jit_solution(18029577432998873099)
XLA Ops:
  2.0 1.4 convolution_convert_fusion
  3.8 1.4 copy.67
  5.2 4.1 %all-to-all-start = ((bf16[4,8,4,4096]{3,2,1,0:T(4,128)(2,1)}), bf16[4,8,4,4096]{3,2,1,0:T(4,128)(2,1)S(1)}, u32[]{:S(2)}, u32[]{:S(2)}) async-start(bf16[4,8,4,4096]{3,2,1,0:T(4,128)(2,1)} %bitcast.67), calls=%async_computation | async-start | bytes 2097152 | tf_op jit(solution)/shard_map/all_to_all | solution.py:23
  9.6 14.0 %all-to-all-done = bf16[4,8,4,4096]{3,2,1,0:T(4,128)(2,1)S(1)} async-done(((bf16[4,8,4,4096]{3,2,1,0:T(4,128)(2,1)}), bf16[4,8,4,4096]{3,2,1,0:T(4,128)(2,1)S(1)}, u32[]{:S(2)}, u32[]{:S(2)}) %all-to-all-start) | async-done | bytes 1048608 | tf_op jit(solution)/shard_map/all_to_all | solution.py:23
  23.6 1.4 reduce_sum.83
  25.0 12.1 %all-to-all-start.1 = ((bf16[8,4,4096]{2,1,0:T(4,128)(2,1)}), bf16[8,4,4096]{2,1,0:T(4,128)(2,1)S(1)}, u32[]{:S(2)}, u32[]{:S(2)}) async-start(bf16[8,4,4096]{2,1,0:T(4,128)(2,1)} %reduce_sum.83), calls=%async_computation.1 | async-start | bytes 524288 | tf_op jit(solution)/shard_map/all_to_all | solution.py:23
  37.8 12.4 %all-to-all-done.1 = bf16[8,4,4096]{2,1,0:T(4,128)(2,1)S(1)} async-done(((bf16[8,4,4096]{2,1,0:T(4,128)(2,1)}), bf16[8,4,4096]{2,1,0:T(4,128)(2,1)S(1)}, u32[]{:S(2)}, u32[]{:S(2)}) %all-to-all-start.1) | async-done | bytes 262176 | tf_op jit(solution)/shard_map/all_to_all | solution.py:23
  51.7 8.3 %all-to-all-start.2 = ((bf16[16,4,4224]{2,1,0:T(4,128)(2,1)}), bf16[16,4,4224]{2,1,0:T(4,128)(2,1)S(1)}, u32[]{:S(2)}, u32[]{:S(2)}) async-start(bf16[16,4,4224]{2,1,0:T(4,128)(2,1)} %broadcast_in_dim.40), calls=%async_computation.2 | async-start | bytes 1081344 | tf_op jit(solution)/shard_map/all_to_all | solution.py:23
  61.1 22.9 %all-to-all-done.2 = bf16[16,4,4224]{2,1,0:T(4,128)(2,1)S(1)} async-done(((bf16[16,4,4224]{2,1,0:T(4,128)(2,1)}), bf16[16,4,4224]{2,1,0:T(4,128)(2,1)S(1)}, u32[]{:S(2)}, u32[]{:S(2)}) %all-to-all-start.2) | async-done | bytes 540704 | tf_op jit(solution)/shard_map/all_to_all | solution.py:23
  84.9 4.2 %pick.1 = bf16[4,256,1024]{2,1,0:T(8,128)(2,1)} custom-call(bf16[64,4224]{1,0:T(8,128)(2,1)} %reshape.93.tokens_ref.note_ref, bf16[64,4224]{1,0:T(8,128)(2,1)} %reshape.93.tokens_ref.note_ref), custom_call_target="tpu_custom_call" | custom-call | tf_op jit(solution)/shard_map/pick/pallas_call | solution.py:71
  89.1 10.2 %all-to-all-start.3 = ((bf16[32,32,1024]{2,1,0:T(8,128)(2,1)}), bf16[32,32,1024]{2,1,0:T(8,128)(2,1)}, u32[]{:S(2)}, u32[]{:S(2)}) async-start(bf16[32,32,1024]{2,1,0:T(8,128)(2,1)} %bitcast.69), calls=%async_computation.3 | async-start | bytes 4194304 | tf_op jit(solution)/shard_map/all_to_all | solution.py:23
  99.4 1.4 constant_dynamic-slice_fusion.1
  100.8 2.1 copy.62
  102.9 3.3 %collective-permute-start = (bf16[2,1024,128]{1,2,0:T(8,128)(2,1)}, bf16[2,1024,128]{1,2,0:T(8,128)(2,1)}, u32[]{:S(2)}, u32[]{:S(2)}) collective-permute-start(bf16[2,1024,128]{1,2,0:T(8,128)(2,1)} %bitcast.16), channel_id=1, source_target_pairs={{0,2},{2,4},{4,6},{6,0},{1,3},{3,5},{5,7},{7,1},{8,10},{10,12},{12... | collective-permute-start | bytes 1572872 | tf_op jit(solution)/shard_map/ppermute | solution.py:152
  106.2 2.0 copy.63
  108.2 4.3 %collective-permute-start.1 = (bf16[2,1024,128]{1,2,0:T(8,128)(2,1)}, bf16[2,1024,128]{1,2,0:T(8,128)(2,1)}, u32[]{:S(2)}, u32[]{:S(2)}) collective-permute-start(bf16[2,1024,128]{1,2,0:T(8,128)(2,1)} %bitcast.18), channel_id=1, source_target_pairs={{0,4},{2,6},{4,0},{6,2},{1,5},{3,7},{5,1},{7,3},{8,12},{10,14},{12... | collective-permute-start | bytes 1572872 | tf_op jit(solution)/shard_map/ppermute | solution.py:152
  113.6 3.0 %collective-permute-start.2 = (bf16[2,1024,128]{1,2,0:T(8,128)(2,1)}, bf16[2,1024,128]{1,2,0:T(8,128)(2,1)}, u32[]{:S(2)}, u32[]{:S(2)}) collective-permute-start(bf16[2,1024,128]{1,2,0:T(8,128)(2,1)} %bitcast.20), channel_id=1, source_target_pairs={{0,6},{2,0},{4,2},{6,4},{1,7},{3,1},{5,3},{7,5},{8,14},{10,8},{12,... | collective-permute-start | bytes 1572872 | tf_op jit(solution)/shard_map/ppermute | solution.py:152
  118.8 17.6 %collective-permute-done = bf16[2,1024,128]{1,2,0:T(8,128)(2,1)} collective-permute-done((bf16[2,1024,128]{1,2,0:T(8,128)(2,1)}, bf16[2,1024,128]{1,2,0:T(8,128)(2,1)}, u32[]{:S(2)}, u32[]{:S(2)}) %collective-permute-start) | collective-permute-done | bytes 524320 | tf_op jit(solution)/shard_map/ppermute | solution.py:152
  137.5 10.6 %collective-permute-done.1 = bf16[2,1024,128]{1,2,0:T(8,128)(2,1)} collective-permute-done((bf16[2,1024,128]{1,2,0:T(8,128)(2,1)}, bf16[2,1024,128]{1,2,0:T(8,128)(2,1)}, u32[]{:S(2)}, u32[]{:S(2)}) %collective-permute-start.1) | collective-permute-done | bytes 524320 | tf_op jit(solution)/shard_map/ppermute | solution.py:152
  150.4 5.3 %convolution_convert_fusion.2 = bf16[1024,1024]{1,0:T(8,128)(2,1)} fusion(bf16[1024,1024]{1,0:T(8,128)(2,1)} %bitcast.13, bf16[1024,1024]{0,1:T(8,128)(2,1)S(1)} %bitcast.70), kind=kOutput, calls=%fused_computation.3 | convolution fusion | flops 2148532224 | bytes 6291456 | tf_op jit(solution)/shard_map/dot_general | solution.py:176
  155.6 3.6 %all-to-all-start.4 = ((bf16[4,256,1024]{2,1,0:T(8,128)(2,1)}), bf16[4,256,1024]{2,1,0:T(8,128)(2,1)S(1)}, u32[]{:S(2)}, u32[]{:S(2)}) async-start(bf16[4,256,1024]{2,1,0:T(8,128)(2,1)} %bitcast.71), calls=%async_computation.4 | async-start | bytes 4194304 | tf_op jit(solution)/shard_map/all_to_all | solution.py:23
  159.3 7.9 %collective-permute-start.3 = (bf16[4,128,512]{2,1,0:T(8,128)(2,1)}, bf16[4,128,512]{2,1,0:T(8,128)(2,1)}, u32[]{:S(2)}, u32[]{:S(2)}) collective-permute-start(bf16[4,128,512]{2,1,0:T(8,128)(2,1)} %get-tuple-element.8), channel_id=1, source_target_pairs={{0,1},{1,0},{2,3},{3,2},{4,5},{5,4},{6,7},{7,6},{8,9},{9,8},{10,11... | collective-permute-start | bytes 1572872 | tf_op jit(solution)/shard_map/ppermute | solution.py:173
  167.2 17.6 %all-to-all-done.4 = bf16[4,256,1024]{2,1,0:T(8,128)(2,1)S(1)} async-done(((bf16[4,256,1024]{2,1,0:T(8,128)(2,1)}), bf16[4,256,1024]{2,1,0:T(8,128)(2,1)S(1)}, u32[]{:S(2)}, u32[]{:S(2)}) %all-to-all-start.4) | async-done | bytes 2097184 | tf_op jit(solution)/shard_map/all_to_all | solution.py:23
  186.4 3.5 %all-to-all-start.5 = ((bf16[4,256,512]{2,1,0:T(8,128)(2,1)}), bf16[4,256,512]{2,1,0:T(8,128)(2,1)S(1)}, u32[]{:S(2)}, u32[]{:S(2)}) async-start(bf16[4,256,512]{2,1,0:T(8,128)(2,1)} %broadcast_in_dim.46), calls=%async_computation.5 | async-start | bytes 2097152 | tf_op jit(solution)/shard_map/all_to_all | solution.py:23
  189.9 1.9 bitcast_select_fusion.1
  191.9 11.5 %all-to-all-done.5 = bf16[4,256,512]{2,1,0:T(8,128)(2,1)S(1)} async-done(((bf16[4,256,512]{2,1,0:T(8,128)(2,1)}), bf16[4,256,512]{2,1,0:T(8,128)(2,1)S(1)}, u32[]{:S(2)}, u32[]{:S(2)}) %all-to-all-start.5) | async-done | bytes 1048608 | tf_op jit(solution)/shard_map/all_to_all | solution.py:23
  203.3 3.6 %convolution_convert_fusion.1 = bf16[1024,1024]{1,0:T(8,128)(2,1)} fusion(bf16[1024,512]{1,0:T(8,128)(2,1)S(1)} %bitcast.74, bf16[512,512]{1,0:T(8,128)(2,1)} %get-tuple-element.16, bf16[512,512]{1,0:T(8,128)(2,1)S(1)} %get-tuple-element.15), kind=kOutput, calls=%fused_computation.2 | convolution fusion | flops 1076887552 | bytes 4194304 | tf_op jit(solution)/shard_map/dot_general | solution.py:188
  207.0 7.4 %all-to-all-start.6 = ((bf16[32,32,1024]{2,1,0:T(8,128)(2,1)}), bf16[32,32,1024]{2,1,0:T(8,128)(2,1)S(1)}, u32[]{:S(2)}, u32[]{:S(2)}) async-start(bf16[32,32,1024]{2,1,0:T(8,128)(2,1)} %bitcast.72), calls=%async_computation.6 | async-start | bytes 4194304 | tf_op jit(solution)/shard_map/all_to_all | solution.py:23
  215.7 27.0 %all-to-all-done.6 = bf16[32,32,1024]{2,1,0:T(8,128)(2,1)S(1)} async-done(((bf16[32,32,1024]{2,1,0:T(8,128)(2,1)}), bf16[32,32,1024]{2,1,0:T(8,128)(2,1)S(1)}, u32[]{:S(2)}, u32[]{:S(2)}) %all-to-all-start.6) | async-done | bytes 2097184 | tf_op jit(solution)/shard_map/all_to_all | solution.py:23
  242.7 1.3 copy-done.1
  244.0 4.2 %combine.1 = bf16[64,4096]{1,0:T(8,128)(2,1)} custom-call(bf16[64,128]{1,0:T(8,128)(2,1)} %slice.28.note_ref, bf16[4,256,1024]{2,1,0:T(8,128)(2,1)} %bitcast.68), custom_call_target="tpu_custom_call" | custom-call | tf_op jit(solution)/shard_map/combine/pallas_call | solution.py:100
  249.5 49.2 %all_to_all.40 = bf16[16,4,4096]{2,1,0:T(4,128)(2,1)S(1)} all-to-all(bf16[16,4,4096]{2,1,0:T(4,128)(2,1)S(1)} %reshape.103), channel_id=1, replica_groups=mesh['ab'=2,'aa'=4,'y'=4,'core'=2,'hidden'=4,'pair'=2] {'pair','ab','aa'}, dimensions={0} | all-to-all | bytes 1048576 | tf_op jit(solution)/shard_map/all_to_all | solution.py:23
  (67 shorter events, 18.4 us)
Async XLA Ops:
  0.0 2.0 copy-start
  3.8 5.6 %copy-start.10 = (s32[1,4,2]{1,2,0:T(2,128)S(1)}, s32[1,4,2]{1,2,0:T(2,128)}, u32[]{:S(2)}) copy-start(s32[1,4,2]{1,2,0:T(2,128)} %param.18) | copy-start | bytes 100
  5.2 32.2 %copy-start.11 = (f32[1,4,2]{1,2,0:T(2,128)S(1)}, f32[1,4,2]{1,2,0:T(2,128)}, u32[]{:S(2)}) copy-start(f32[1,4,2]{1,2,0:T(2,128)} %param.17) | copy-start | bytes 100
  5.2 45.3 %copy-start.8 = (bf16[1,4,4096]{2,1,0:T(4,128)(2,1)S(1)}, bf16[1,4,4096]{2,1,0:T(4,128)(2,1)}, u32[]{:S(2)}) copy-start(bf16[1,4,4096]{2,1,0:T(4,128)(2,1)} %param.15) | copy-start | bytes 98308
  5.2 45.4 %copy-start.9 = (f32[4096]{0:T(1024)S(1)}, f32[4096]{0:T(1024)}, u32[]{:S(2)}) copy-start(f32[4096]{0:T(1024)} %param.16) | copy-start | bytes 49156
  5.2 18.4 %all-to-all-start = ((bf16[4,8,4,4096]{3,2,1,0:T(4,128)(2,1)}), bf16[4,8,4,4096]{3,2,1,0:T(4,128)(2,1)S(1)}, u32[]{:S(2)}, u32[]{:S(2)}) async-start(bf16[4,8,4,4096]{3,2,1,0:T(4,128)(2,1)} %bitcast.67), calls=%async_computation | async-start | bytes 2097152 | tf_op jit(solution)/shard_map/all_to_all | solution.py:23
  9.5 50.5 %copy-start.7 = (bf16[1,1024,512]{2,1,0:T(8,128)(2,1)S(1)}, bf16[1,1024,512]{2,1,0:T(8,128)(2,1)}, u32[]{:S(2)}) copy-start(bf16[1,1024,512]{2,1,0:T(8,128)(2,1)} %param.21) | copy-start | bytes 3145732
  25.0 25.2 %all-to-all-start.1 = ((bf16[8,4,4096]{2,1,0:T(4,128)(2,1)}), bf16[8,4,4096]{2,1,0:T(4,128)(2,1)S(1)}, u32[]{:S(2)}, u32[]{:S(2)}) async-start(bf16[8,4,4096]{2,1,0:T(4,128)(2,1)} %reduce_sum.83), calls=%async_computation.1 | async-start | bytes 524288 | tf_op jit(solution)/shard_map/all_to_all | solution.py:23
  51.7 32.2 %all-to-all-start.2 = ((bf16[16,4,4224]{2,1,0:T(4,128)(2,1)}), bf16[16,4,4224]{2,1,0:T(4,128)(2,1)S(1)}, u32[]{:S(2)}, u32[]{:S(2)}) async-start(bf16[16,4,4224]{2,1,0:T(4,128)(2,1)} %broadcast_in_dim.40), calls=%async_computation.2 | async-start | bytes 1081344 | tf_op jit(solution)/shard_map/all_to_all | solution.py:23
  89.1 10.2 %copy-start.4 = (bf16[1,2,4096,128]{3,2,1,0:T(8,128)(2,1)S(1)}, bf16[1,2,4096,128]{3,2,1,0:T(8,128)(2,1)}, u32[]{:S(2)}) copy-start(bf16[1,2,4096,128]{3,2,1,0:T(8,128)(2,1)} %param.20) | copy-start | bytes 6291460
  89.1 61.2 %all-to-all-start.3 = ((bf16[32,32,1024]{2,1,0:T(8,128)(2,1)}), bf16[32,32,1024]{2,1,0:T(8,128)(2,1)}, u32[]{:S(2)}, u32[]{:S(2)}) async-start(bf16[32,32,1024]{2,1,0:T(8,128)(2,1)} %bitcast.69), calls=%async_computation.3 | async-start | bytes 4194304 | tf_op jit(solution)/shard_map/all_to_all | solution.py:23
  100.8 11.8 %copy-start.6 = (bf16[2,1,1024,128]{3,2,1,0:T(8,128)(2,1)S(1)}, bf16[2,1,1024,128]{3,2,1,0:T(8,128)(2,1)}, u32[]{:S(2)}) copy-start(bf16[2,1,1024,128]{3,2,1,0:T(8,128)(2,1)} %get-tuple-element.11) | copy-start | bytes 1572868
  100.8 15.9 %copy-start.5 = (bf16[2,1,1024,128]{3,2,1,0:T(8,128)(2,1)S(1)}, bf16[2,1,1024,128]{3,2,1,0:T(8,128)(2,1)}, u32[]{:S(2)}) copy-start(bf16[2,1,1024,128]{3,2,1,0:T(8,128)(2,1)} %get-tuple-element.14) | copy-start | bytes 1572868
  102.9 33.5 %collective-permute-start = (bf16[2,1024,128]{1,2,0:T(8,128)(2,1)}, bf16[2,1024,128]{1,2,0:T(8,128)(2,1)}, u32[]{:S(2)}, u32[]{:S(2)}) collective-permute-start(bf16[2,1024,128]{1,2,0:T(8,128)(2,1)} %bitcast.16), channel_id=1, source_target_pairs={{0,2},{2,4},{4,6},{6,0},{1,3},{3,5},{5,7},{7,1},{8,10},{10,12},{12... | collective-permute-start | bytes 1572872 | tf_op jit(solution)/shard_map/ppermute | solution.py:152
  108.2 40.0 %collective-permute-start.1 = (bf16[2,1024,128]{1,2,0:T(8,128)(2,1)}, bf16[2,1024,128]{1,2,0:T(8,128)(2,1)}, u32[]{:S(2)}, u32[]{:S(2)}) collective-permute-start(bf16[2,1024,128]{1,2,0:T(8,128)(2,1)} %bitcast.18), channel_id=1, source_target_pairs={{0,4},{2,6},{4,0},{6,2},{1,5},{3,7},{5,1},{7,3},{8,12},{10,14},{12... | collective-permute-start | bytes 1572872 | tf_op jit(solution)/shard_map/ppermute | solution.py:152
  113.6 35.6 %collective-permute-start.2 = (bf16[2,1024,128]{1,2,0:T(8,128)(2,1)}, bf16[2,1024,128]{1,2,0:T(8,128)(2,1)}, u32[]{:S(2)}, u32[]{:S(2)}) collective-permute-start(bf16[2,1024,128]{1,2,0:T(8,128)(2,1)} %bitcast.20), channel_id=1, source_target_pairs={{0,6},{2,0},{4,2},{6,4},{1,7},{3,1},{5,3},{7,5},{8,14},{10,8},{12,... | collective-permute-start | bytes 1572872 | tf_op jit(solution)/shard_map/ppermute | solution.py:152
  117.7 1.0 copy-start.3
  155.6 29.1 %all-to-all-start.4 = ((bf16[4,256,1024]{2,1,0:T(8,128)(2,1)}), bf16[4,256,1024]{2,1,0:T(8,128)(2,1)S(1)}, u32[]{:S(2)}, u32[]{:S(2)}) async-start(bf16[4,256,1024]{2,1,0:T(8,128)(2,1)} %bitcast.71), calls=%async_computation.4 | async-start | bytes 4194304 | tf_op jit(solution)/shard_map/all_to_all | solution.py:23
  159.3 30.7 %collective-permute-start.3 = (bf16[4,128,512]{2,1,0:T(8,128)(2,1)}, bf16[4,128,512]{2,1,0:T(8,128)(2,1)}, u32[]{:S(2)}, u32[]{:S(2)}) collective-permute-start(bf16[4,128,512]{2,1,0:T(8,128)(2,1)} %get-tuple-element.8), channel_id=1, source_target_pairs={{0,1},{1,0},{2,3},{3,2},{4,5},{5,4},{6,7},{7,6},{8,9},{9,8},{10,11... | collective-permute-start | bytes 1572872 | tf_op jit(solution)/shard_map/ppermute | solution.py:173
  185.2 4.8 %copy-start.2 = (bf16[4,1,128,512]{3,2,1,0:T(8,128)(2,1)S(1)}, bf16[4,1,128,512]{3,2,1,0:T(8,128)(2,1)}, u32[]{:S(2)}) copy-start(bf16[4,1,128,512]{3,2,1,0:T(8,128)(2,1)} %get-tuple-element.17) | copy-start | bytes 1572868
  186.4 17.0 %all-to-all-start.5 = ((bf16[4,256,512]{2,1,0:T(8,128)(2,1)}), bf16[4,256,512]{2,1,0:T(8,128)(2,1)S(1)}, u32[]{:S(2)}, u32[]{:S(2)}) async-start(bf16[4,256,512]{2,1,0:T(8,128)(2,1)} %broadcast_in_dim.46), calls=%async_computation.5 | async-start | bytes 2097152 | tf_op jit(solution)/shard_map/all_to_all | solution.py:23
  207.0 35.7 %all-to-all-start.6 = ((bf16[32,32,1024]{2,1,0:T(8,128)(2,1)}), bf16[32,32,1024]{2,1,0:T(8,128)(2,1)S(1)}, u32[]{:S(2)}, u32[]{:S(2)}) async-start(bf16[32,32,1024]{2,1,0:T(8,128)(2,1)} %bitcast.72), calls=%async_computation.6 | async-start | bytes 4194304 | tf_op jit(solution)/shard_map/all_to_all | solution.py:23
  242.7 1.3 copy-start.1

commit v3 on v2

v3 whole, which is shorter than its diff:
```python
import jax
import jax.numpy as jnp
from jax import lax
from jax.experimental import pallas as pl
from jax.sharding import Mesh
from jax.sharding import PartitionSpec as P


D = 4096
HD = 128
EPSILON = 1e-05
BF16 = jnp.bfloat16
F32 = jnp.float32


ATTN = ("ab", "am", "al")
HIDDEN = ("xh", "xl")
QUAD = ("al", "xl")
Z_AXES = ("pair", "ab", "am", "al")
ROUTE = ("xh", "xl", "y", "core")
LANES = 128


def exchange(value, axes):
    return lax.all_to_all(value, axes, 0, 0, tiled=True)


def attention(queries, keys, values, doc_lengths):
    tok_group = queries.shape[0]
    doc_ends = jnp.cumsum(doc_lengths)
    positions = jnp.arange(tok_group, dtype=jnp.int32)
    document = jnp.sum((positions[:, None] >= doc_ends[None, :]).astype(jnp.int32), axis=1)
    allowed = (document[:, None] == document[None, :]) & (positions[None, :] <= positions[:, None])
    scores = jnp.dot(queries, keys.T, preferred_element_type=F32) * HD ** (-0.5)
    scores = jnp.where(allowed, scores, -1e30)
    row_top = jnp.max(scores, axis=1, keepdims=True)
    weights = jnp.exp(scores - row_top)
    probabilities = (weights / jnp.sum(weights, axis=1, keepdims=True)).astype(BF16)
    return jnp.dot(probabilities, values, preferred_element_type=F32).astype(BF16)


def slot_numbers(chosen, place, places, capacity):
    rows = chosen.shape[0]
    row_ids = jnp.arange(rows, dtype=jnp.int32)
    earlier = row_ids[None, :] < row_ids[:, None]
    same = chosen[:, None] == chosen[None, :]
    ranking = jnp.sum((same & earlier).astype(jnp.int32), axis=-1)
    return (chosen * places + place) * capacity + ranking


def note_of(slots, share):
    high = lax.reduce_precision(share, 8, 7)
    middle = lax.reduce_precision(share - high, 8, 7)
    low = share - high - middle
    parts = jnp.stack([slots[:, 0].astype(F32), slots[:, 1].astype(F32), high, middle, low], axis=1)
    return jnp.pad(parts, ((0, 0), (0, LANES - 5))).astype(BF16)


def pick_kernel(tokens_ref, note_ref, out_ref):
    note = note_ref[...].astype(F32)
    slots = lax.broadcasted_iota(jnp.int32, (note.shape[0], out_ref.shape[1]), 1).astype(F32)
    taken = (slots == note[:, 0:1]) | (slots == note[:, 1:2])
    out_ref[0] = lax.dot_general(
        jnp.where(taken, 1.0, 0.0).astype(BF16),
        tokens_ref[...],
        (((0,), (0,)), ((), ())),
        preferred_element_type=F32,
    ).astype(BF16)


def pick_rows(tokens, slots, chunk, copies):
    count = tokens.shape[0]
    width = tokens.shape[1] - LANES
    parts = width // chunk
    return pl.pallas_call(
        pick_kernel,
        grid=(copies * parts,),
        in_specs=[
            pl.BlockSpec((count, chunk), lambda j: (0, j % parts)),
            pl.BlockSpec((count, LANES), lambda j: (0, width // LANES)),
        ],
        out_specs=pl.BlockSpec((1, slots, chunk), lambda j: (j, 0, 0)),
        out_shape=jax.ShapeDtypeStruct((copies * parts, slots, chunk), BF16),
        name="pick",
    )(tokens, tokens)


def combine_kernel(note_ref, rows_ref, out_ref):
    note = note_ref[...].astype(F32)
    share = note[:, 2:3] + note[:, 3:4] + note[:, 4:5]
    slots = lax.broadcasted_iota(jnp.int32, (note.shape[0], rows_ref.shape[2]), 1).astype(F32)
    weight = jnp.where(slots == note[:, 0:1], share, 0.0)
    weight = weight + jnp.where(slots == note[:, 1:2], 1.0 - share, 0.0)
    high = weight.astype(BF16)
    low = (weight - high.astype(F32)).astype(BF16)
    total = jnp.zeros(out_ref.shape, F32)
    for k in range(rows_ref.shape[0]):
        rows = rows_ref[k, 0]
        total += jnp.dot(high, rows, preferred_element_type=F32)
        total += jnp.dot(low, rows, preferred_element_type=F32)
    out_ref[...] = total.astype(BF16)


def combine_rows(note, rows):
    count = note.shape[0]
    sums, chunks, slots, chunk = rows.shape
    return pl.pallas_call(
        combine_kernel,
        grid=(chunks,),
        in_specs=[
            pl.BlockSpec((count, LANES), lambda j: (0, 0)),
            pl.BlockSpec((sums, 1, slots, chunk), lambda j: (0, j, 0, 0)),
        ],
        out_specs=pl.BlockSpec((count, chunk), lambda j: (0, j)),
        out_shape=jax.ShapeDtypeStruct((count, chunks * chunk), BF16),
        name="combine",
    )(note, rows)


def down_moves(i, j):
    moves = []
    for high in range(4):
        for n in range(16):
            al, xh, xl, pair = n >> 3, (n >> 2) & 1, (n >> 1) & 1, n & 1
            moves.append((high * 16 + n, high * 16 + xh * 8 + (al ^ i) * 4 + xl * 2 + (pair ^ j)))
    return moves


def layer(
    queries,
    keys,
    values,
    out_weight,
    residual,
    norm_gain,
    route_logits,
    expert_ids,
    doc_lengths,
    gate_up_weight,
    down_weight,
):
    xs = lax.axis_size(HIDDEN)
    zl = lax.axis_size(ATTN)
    pairs = lax.axis_size("pair")
    experts = lax.axis_size(("y", "core"))
    quad = lax.axis_size(QUAD)
    capacity = 2
    chunk = D // quad
    unit = gate_up_weight.shape[-1]
    half = quad * unit

    heads_out = attention(queries[0], keys[0], values[0], doc_lengths[0])
    tok_group = heads_out.shape[0]
    owned = tok_group // (zl * xs)
    projected = jnp.dot(heads_out, out_weight, preferred_element_type=F32).astype(BF16)
    projected = projected.reshape(zl, xs, owned, D).transpose(1, 0, 2, 3)
    projected = jnp.sum(exchange(projected, HIDDEN).astype(F32), axis=0).astype(BF16)
    me = lax.axis_index(QUAD)
    gate_up = gate_up_weight[0].reshape(2, quad, chunk, unit)
    gathered = jnp.zeros((quad, 2, chunk, unit), BF16)
    for d in range(quad):
        block = lax.dynamic_index_in_dim(gate_up, me ^ d, 1, keepdims=False)
        if d > 0:
            block = lax.ppermute(block, QUAD, [(i, i ^ d) for i in range(quad)])
        gathered = lax.dynamic_update_index_in_dim(gathered, block, me ^ d, 0)
    projected = jnp.sum(exchange(projected, ATTN).astype(F32), axis=0)
    gate_up = gathered.transpose(2, 1, 0, 3).reshape(chunk, 2 * half)
    attended = residual[0].astype(F32) + projected
    scale = lax.rsqrt(jnp.mean(attended * attended, axis=1, keepdims=True) + EPSILON)
    normed = (attended * scale * norm_gain).astype(BF16)

    places = lax.axis_size(Z_AXES)
    chosen = expert_ids[0].reshape(2 * owned)
    slots = slot_numbers(chosen, lax.axis_index(Z_AXES), places, capacity).reshape(owned, 2)
    logits = route_logits[0]
    note = note_of(slots, jax.nn.sigmoid(logits[:, 0] - logits[:, 1]))
    parity = lax.axis_size("al")
    width = D // parity
    noted = jnp.stack(
        [jnp.concatenate([normed[:, k * width : (k + 1) * width], note], axis=1) for k in range(parity)]
    )
    noted = jnp.broadcast_to(noted, (places // parity, *noted.shape))
    tokens = exchange(noted.reshape(places, owned, width + LANES), Z_AXES)
    tokens = tokens.reshape(places * owned, width + LANES)
    note = tokens[:, width:]

    group_slots = experts * places * capacity
    picked = pick_rows(tokens, group_slots, chunk, lax.axis_size("xh"))
    blocks = down_weight[0].reshape(2, 2, pairs, unit, -1)
    part = blocks.shape[-1]
    picked, blocks = lax.optimization_barrier((picked, blocks))
    al, xh, z_hi = lax.axis_index("al"), lax.axis_index("xh"), lax.axis_index("pair")
    down = jnp.zeros((parity, 2 * unit, pairs * part), BF16)
    for i, j in ((0, 1), (1, 1), (0, 0), (1, 0)):
        sent = lax.dynamic_slice(
            blocks, (al ^ i, 0, z_hi ^ j, 0, 0), (1, 2, 1, unit, part)
        ).reshape(2 * unit, part)
        sent = lax.ppermute(sent, ("ab", "am", "al", "xh", "xl", "pair"), down_moves(i, j))
        down = lax.dynamic_update_slice(down, sent[None], (xh ^ i, 0, (z_hi ^ j) * part))
    down = down.reshape(half, chunk)
    rows = exchange(picked.reshape(xs * experts, -1, chunk), ROUTE).reshape(-1, chunk)

    partial = jnp.dot(rows, gate_up, preferred_element_type=F32).astype(BF16)
    partial = partial.reshape(quad, -1, partial.shape[1])
    summed = jnp.sum(exchange(partial, QUAD).astype(F32), axis=0)
    activated = (jax.nn.silu(summed[:, :half]) * summed[:, half:]).astype(BF16)
    activated = exchange(jnp.broadcast_to(activated, (quad, *activated.shape)), QUAD)
    activated = activated.reshape(-1, half)
    out = jnp.dot(activated, down, preferred_element_type=F32).astype(BF16)

    returned = exchange(out.reshape(xs * experts, -1, chunk), ROUTE)
    returned = combine_rows(note, returned.reshape(2, 2, group_slots, chunk))
    mixed = exchange(returned.reshape(places, owned, width), Z_AXES)
    mixed = jnp.sum(mixed.reshape(-1, parity, owned, width).astype(F32), axis=0)
    layer_out = attended + jnp.concatenate([mixed[k] for k in range(parity)], axis=1)
    return layer_out.astype(BF16)[None]


def solution(mesh):
    cut = Mesh(
        mesh.devices.reshape(2, 2, 2, 4, 2, 2, 2, 2),
        ("ab", "am", "al", "y", "core", "xh", "xl", "pair"),
    )
    expert = ("y", "core")
    group = ("y", "core", "pair")
    owner = (*ATTN, *HIDDEN)
    in_specs = (
        P(group, None, owner),
        P(group, None, ATTN),
        P(group, None, ATTN),
        P(owner, None),
        P(group, owner, None),
        P(),
        P(group, owner, None),
        P(group, owner, None),
        P(group, None),
        P(expert, None, None, (*owner, "pair")),
        P(expert, ATTN, (*HIDDEN, "pair")),
    )
    return jax.shard_map(
        layer, mesh=cut, in_specs=in_specs, out_specs=P(group, owner, None), check_vma=False
    )
```

time: 305 us -> 351 us (1.15)
  blocking collectives: 49.2 us -> 99.7 us
  starting transfers between devices: 67.6 us -> 81 us
  waiting for transfers between devices: 134 us -> 124 us
    all_to_all x7 -> x5, waiting for transfers between devices: 105 us -> 53.4 us  [exchange(): return lax.all_to_all(value, axes, 0, 0, tiled=True)]
    all_to_all x1 -> x3, blocking collectives: 49.2 us -> 99.7 us  [exchange(): return lax.all_to_all(value, axes, 0, 0, tiled=True)]
    ppermute x4 -> x7, waiting for transfers between devices: 28.2 us -> 70.4 us  [the longest x4 40 us: layer(): lax.ppermute(sent, ('ab', 'am', 'al', 'xh', 'xl', 'pair'), down_moves(i, j))]
    ppermute x4 -> x7, starting transfers between devices: 18.5 us -> 28.6 us  [the longest x4 20.2 us: layer(): lax.ppermute(sent, ('ab', 'am', 'al', 'xh', 'xl', 'pair'), down_moves(i, j))]
    all_to_all x7 -> x5, starting transfers between devices: 49.1 us -> 52.4 us  [exchange(): return lax.all_to_all(value, axes, 0, 0, tiled=True)]
    unnamed x31 -> x29, local copies, waits for them, and re-layouts: 8.67 us -> 8.69 us
  transfers between devices with their start and end apart: 11 -> 12, of which waited for: 8 -> 5; matrix products, arithmetic and copies ran while one was open for 6% -> 5% of each run, Pallas kernels for 0% -> 0%
where the time goes in v3:
time: 351 us; the launch traced here: 349 us
  waiting for transfers between devices  124 us (35%)
  blocking collectives  99.7 us (28%)
  starting transfers between devices  81 us (23%)
  local copies, waits for them, and re-layouts  23.1 us (7%)
  matrix products  8.87 us (3%)
  Pallas kernels  7.3 us (2%)
  other arithmetic  4.66 us (1%)
    all_to_all x3, blocking collectives, exchange(): return lax.all_to_all(value, axes, 0, 0, tiled=True)  99.7 us
    all_to_all x5, waiting for transfers between devices, exchange(): return lax.all_to_all(value, axes, 0, 0, tiled=True)  53.4 us
    all_to_all x5, starting transfers between devices, exchange(): return lax.all_to_all(value, axes, 0, 0, tiled=True)  52.4 us
    ppermute x4, waiting for transfers between devices, layer(): lax.ppermute(sent, ('ab', 'am', 'al', 'xh', 'xl', 'pair'), down_moves(i, j))  40 us
    ppermute x3, waiting for transfers between devices, layer(): block = lax.ppermute(block, QUAD, [(i, i ^ d) for i in range(quad)])  30.4 us
    ppermute x4, starting transfers between devices, layer(): lax.ppermute(sent, ('ab', 'am', 'al', 'xh', 'xl', 'pair'), down_moves(i, j))  20.2 us
    unnamed x29, local copies, waits for them, and re-layouts  8.69 us
    ppermute x3, starting transfers between devices, layer(): block = lax.ppermute(block, QUAD, [(i, i ^ d) for i in range(quad)])  8.34 us
  transfers between devices with their start and end apart: 12, of which 5 were waited for; matrix products, arithmetic and copies ran while one was open for 5% of the time, Pallas kernels for 0%

profile of v3, /device:TPU:33, one launch (start us, length us, event | category | flops | bytes accessed | tf_op | source)
XLA Modules:
  0.0 348.8 jit_solution(15586620768912282936)
XLA Ops:
  2.0 1.4 convolution_convert_fusion
  3.8 1.4 copy.70
  5.2 4.1 %all-to-all-start = ((bf16[4,8,4,4096]{3,2,1,0:T(4,128)(2,1)}), bf16[4,8,4,4096]{3,2,1,0:T(4,128)(2,1)S(1)}, u32[]{:S(2)}, u32[]{:S(2)}) async-start(bf16[4,8,4,4096]{3,2,1,0:T(4,128)(2,1)} %bitcast.78), calls=%async_computation | async-start | bytes 2097152 | tf_op jit(solution)/shard_map/all_to_all | solution.py:25
  9.5 14.0 %all-to-all-done = bf16[4,8,4,4096]{3,2,1,0:T(4,128)(2,1)S(1)} async-done(((bf16[4,8,4,4096]{3,2,1,0:T(4,128)(2,1)}), bf16[4,8,4,4096]{3,2,1,0:T(4,128)(2,1)S(1)}, u32[]{:S(2)}, u32[]{:S(2)}) %all-to-all-start) | async-done | bytes 1048608 | tf_op jit(solution)/shard_map/all_to_all | solution.py:25
  23.6 1.4 reduce_sum.81
  25.0 12.1 %all-to-all-start.1 = ((bf16[8,4,4096]{2,1,0:T(4,128)(2,1)}), bf16[8,4,4096]{2,1,0:T(4,128)(2,1)S(1)}, u32[]{:S(2)}, u32[]{:S(2)}) async-start(bf16[8,4,4096]{2,1,0:T(4,128)(2,1)} %reduce_sum.81), calls=%async_computation.1 | async-start | bytes 524288 | tf_op jit(solution)/shard_map/all_to_all | solution.py:25
  37.8 12.4 %all-to-all-done.1 = bf16[8,4,4096]{2,1,0:T(4,128)(2,1)S(1)} async-done(((bf16[8,4,4096]{2,1,0:T(4,128)(2,1)}), bf16[8,4,4096]{2,1,0:T(4,128)(2,1)S(1)}, u32[]{:S(2)}, u32[]{:S(2)}) %all-to-all-start.1) | async-done | bytes 262176 | tf_op jit(solution)/shard_map/all_to_all | solution.py:25
  50.9 23.5 %all_to_all.40 = bf16[16,4,2176]{2,1,0:T(4,128)(2,1)S(1)} all-to-all(bf16[16,4,2176]{2,1,0:T(4,128)(2,1)S(1)} %bitcast.85), channel_id=1, replica_groups=mesh['ab'=2,'am'=2,'al'=2,'y'=4,'core'=2,'xh'=2,'xl'=2,'pair'=2] {'pair'..., dimensions={0} | all-to-all | bytes 557056 | tf_op jit(solution)/shard_map/all_to_all | solution.py:25
  75.3 4.2 %pick.1 = bf16[4,256,1024]{2,1,0:T(8,128)(2,1)} custom-call(bf16[64,2176]{1,0:T(8,128)(2,1)} %reshape.111.tokens_ref.note_ref, bf16[64,2176]{1,0:T(8,128)(2,1)} %reshape.111.tokens_ref.note_ref), custom_call_target="tpu_custom_call" | custom-call | tf_op jit(solution)/shard_map/pick/pallas_call | solution.py:75
  79.5 10.4 %all-to-all-start.3 = ((bf16[32,32,1024]{2,1,0:T(8,128)(2,1)}), bf16[32,32,1024]{2,1,0:T(8,128)(2,1)}, u32[]{:S(2)}, u32[]{:S(2)}) async-start(bf16[32,32,1024]{2,1,0:T(8,128)(2,1)} %bitcast.79), calls=%async_computation.3 | async-start | bytes 4194304 | tf_op jit(solution)/shard_map/all_to_all | solution.py:25
  89.9 1.3 constant_dynamic-slice_fusion.4
  91.3 2.1 copy.65
  93.4 3.3 collective-permute-start
  96.7 2.1 copy.66
  98.8 2.0 collective-permute-start.1
  101.8 3.1 collective-permute-start.2
  107.0 30.4 %collective-permute-done = bf16[2,1024,128]{1,2,0:T(8,128)(2,1)} collective-permute-done((bf16[2,1024,128]{1,2,0:T(8,128)(2,1)}, bf16[2,1024,128]{1,2,0:T(8,128)(2,1)}, u32[]{:S(2)}, u32[]{:S(2)}) %collective-permute-start) | collective-permute-done | bytes 524320 | tf_op jit(solution)/shard_map/ppermute | solution.py:164
  140.7 4.0 %convolution_convert_fusion.2 = bf16[1024,1024]{1,0:T(8,128)(2,1)S(1)} fusion(bf16[1024,1024]{1,0:T(8,128)(2,1)} %bitcast.15, bf16[1024,1024]{0,1:T(8,128)(2,1)S(1)} %bitcast.81), kind=kOutput, calls=%fused_computation.3 | convolution fusion | flops 2148532224 | bytes 6291456 | tf_op jit(solution)/shard_map/dot_general | solution.py:203
  144.7 26.3 %all_to_all.41 = bf16[4,256,1024]{2,1,0:T(8,128)(2,1)S(1)} all-to-all(bf16[4,256,1024]{2,1,0:T(8,128)(2,1)S(1)} %bitcast.83), channel_id=1, replica_groups=mesh['ab'=2,'am'=2,'al'=2,'y'=4,'core'=2,'xh'=2,'xl'=2,'pair'=2] {'al','..., dimensions={0} | all-to-all | bytes 4194304 | tf_op jit(solution)/shard_map/all_to_all | solution.py:25
  172.5 3.7 %all-to-all-start.5 = ((bf16[4,256,512]{2,1,0:T(8,128)(2,1)}), bf16[4,256,512]{2,1,0:T(8,128)(2,1)S(1)}, u32[]{:S(2)}, u32[]{:S(2)}) async-start(bf16[4,256,512]{2,1,0:T(8,128)(2,1)} %broadcast_in_dim.61), calls=%async_computation.5 | async-start | bytes 2097152 | tf_op jit(solution)/shard_map/all_to_all | solution.py:25
  177.2 6.6 %collective-permute-start.3 = (bf16[256,512]{1,0:T(8,128)(2,1)}, bf16[256,512]{1,0:T(8,128)(2,1)}, u32[]{:S(2)}, u32[]{:S(2)}) collective-permute-start(bf16[256,512]{1,0:T(8,128)(2,1)} %bitcast.28), channel_id=1, source_target_pairs={{0,1},{1,0},{2,3},{3,2},{4,65},{5,64},{6,67},{7,66},{64,5},{65,4},... | collective-permute-start | bytes 786440 | tf_op jit(solution)/shard_map/ppermute | solution.py:198
  183.7 6.3 %collective-permute-start.4 = (bf16[256,512]{1,0:T(8,128)(2,1)}, bf16[256,512]{1,0:T(8,128)(2,1)}, u32[]{:S(2)}, u32[]{:S(2)}) collective-permute-start(bf16[256,512]{1,0:T(8,128)(2,1)} %bitcast.30), channel_id=1, source_target_pairs={{0,5},{1,4},{2,7},{3,6},{4,69},{5,68},{6,71},{7,70},{64,1},{65,0},... | collective-permute-start | bytes 786440 | tf_op jit(solution)/shard_map/ppermute | solution.py:198
  190.1 5.4 %collective-permute-start.5 = (bf16[256,512]{1,0:T(8,128)(2,1)}, bf16[256,512]{1,0:T(8,128)(2,1)S(1)}, u32[]{:S(2)}, u32[]{:S(2)}) collective-permute-start(bf16[256,512]{1,0:T(8,128)(2,1)} %bitcast.91), channel_id=1, source_target_pairs={{0,0},{1,1},{2,2},{3,3},{4,64},{5,65},{6,66},{7,67},{64,4},{65,5},... | collective-permute-start | bytes 786440 | tf_op jit(solution)/shard_map/ppermute | solution.py:198
  195.5 1.9 collective-permute-start.6
  197.5 40.0 %collective-permute-done.3 = bf16[256,512]{1,0:T(8,128)(2,1)} collective-permute-done((bf16[256,512]{1,0:T(8,128)(2,1)}, bf16[256,512]{1,0:T(8,128)(2,1)}, u32[]{:S(2)}, u32[]{:S(2)}) %collective-permute-start.3) | collective-permute-done | bytes 262176 | tf_op jit(solution)/shard_map/ppermute | solution.py:198
  239.7 2.6 convolution_convert_fusion.1
  242.3 22.1 %all-to-all-start.6 = ((bf16[32,32,1024]{2,1,0:T(8,128)(2,1)}), bf16[32,32,1024]{2,1,0:T(8,128)(2,1)S(1)}, u32[]{:S(2)}, u32[]{:S(2)}) async-start(bf16[32,32,1024]{2,1,0:T(8,128)(2,1)} %bitcast.82), calls=%async_computation.6 | async-start | bytes 4194304 | tf_op jit(solution)/shard_map/all_to_all | solution.py:25
  264.4 1.3 slice.46.note_ref
  265.7 27.0 %all-to-all-done.6 = bf16[32,32,1024]{2,1,0:T(8,128)(2,1)S(1)} async-done(((bf16[32,32,1024]{2,1,0:T(8,128)(2,1)}), bf16[32,32,1024]{2,1,0:T(8,128)(2,1)S(1)}, u32[]{:S(2)}, u32[]{:S(2)}) %all-to-all-start.6) | async-done | bytes 2097184 | tf_op jit(solution)/shard_map/all_to_all | solution.py:25
  292.7 1.3 copy-done.1
  294.0 3.1 combine.1
  298.2 49.8 %all_to_all.42 = bf16[16,4,2048]{2,1,0:T(4,128)(2,1)S(1)} all-to-all(bf16[16,4,2048]{2,1,0:T(4,128)(2,1)S(1)} %reshape.124), channel_id=1, replica_groups=mesh['ab'=2,'am'=2,'al'=2,'y'=4,'core'=2,'xh'=2,'xl'=2,'pair'=2] {'pair'..., dimensions={0} | all-to-all | bytes 524288 | tf_op jit(solution)/shard_map/all_to_all | solution.py:25
  (76 shorter events, 17.7 us)
Async XLA Ops:
  0.0 2.0 copy-start
  3.8 5.6 %copy-start.9 = (s32[1,4,2]{1,2,0:T(2,128)S(1)}, s32[1,4,2]{1,2,0:T(2,128)}, u32[]{:S(2)}) copy-start(s32[1,4,2]{1,2,0:T(2,128)} %param.18) | copy-start | bytes 100
  5.2 32.2 %copy-start.10 = (f32[1,4,2]{1,2,0:T(2,128)S(1)}, f32[1,4,2]{1,2,0:T(2,128)}, u32[]{:S(2)}) copy-start(f32[1,4,2]{1,2,0:T(2,128)} %param.17) | copy-start | bytes 100
  5.2 45.3 %copy-start.7 = (bf16[1,4,4096]{2,1,0:T(4,128)(2,1)S(1)}, bf16[1,4,4096]{2,1,0:T(4,128)(2,1)}, u32[]{:S(2)}) copy-start(bf16[1,4,4096]{2,1,0:T(4,128)(2,1)} %param.15) | copy-start | bytes 98308
  5.2 45.4 %copy-start.8 = (f32[4096]{0:T(1024)S(1)}, f32[4096]{0:T(1024)}, u32[]{:S(2)}) copy-start(f32[4096]{0:T(1024)} %param.16) | copy-start | bytes 49156
  5.2 18.4 %all-to-all-start = ((bf16[4,8,4,4096]{3,2,1,0:T(4,128)(2,1)}), bf16[4,8,4,4096]{3,2,1,0:T(4,128)(2,1)S(1)}, u32[]{:S(2)}, u32[]{:S(2)}) async-start(bf16[4,8,4,4096]{3,2,1,0:T(4,128)(2,1)} %bitcast.78), calls=%async_computation | async-start | bytes 2097152 | tf_op jit(solution)/shard_map/all_to_all | solution.py:25
  25.0 25.2 %all-to-all-start.1 = ((bf16[8,4,4096]{2,1,0:T(4,128)(2,1)}), bf16[8,4,4096]{2,1,0:T(4,128)(2,1)S(1)}, u32[]{:S(2)}, u32[]{:S(2)}) async-start(bf16[8,4,4096]{2,1,0:T(4,128)(2,1)} %reduce_sum.81), calls=%async_computation.1 | async-start | bytes 524288 | tf_op jit(solution)/shard_map/all_to_all | solution.py:25
  79.5 10.5 %copy-start.3 = (bf16[1,2,4096,128]{3,2,1,0:T(8,128)(2,1)S(1)}, bf16[1,2,4096,128]{3,2,1,0:T(8,128)(2,1)}, u32[]{:S(2)}) copy-start(bf16[1,2,4096,128]{3,2,1,0:T(8,128)(2,1)} %param.20) | copy-start | bytes 6291460
  79.5 61.2 %all-to-all-start.3 = ((bf16[32,32,1024]{2,1,0:T(8,128)(2,1)}), bf16[32,32,1024]{2,1,0:T(8,128)(2,1)}, u32[]{:S(2)}, u32[]{:S(2)}) async-start(bf16[32,32,1024]{2,1,0:T(8,128)(2,1)} %bitcast.79), calls=%async_computation.3 | async-start | bytes 4194304 | tf_op jit(solution)/shard_map/all_to_all | solution.py:25
  91.3 9.5 %copy-start.5 = (bf16[2,1,1024,128]{3,2,1,0:T(8,128)(2,1)S(1)}, bf16[2,1,1024,128]{3,2,1,0:T(8,128)(2,1)}, u32[]{:S(2)}) copy-start(bf16[2,1,1024,128]{3,2,1,0:T(8,128)(2,1)} %get-tuple-element.11) | copy-start | bytes 1572868
  91.3 13.6 %copy-start.4 = (bf16[2,1,1024,128]{3,2,1,0:T(8,128)(2,1)S(1)}, bf16[2,1,1024,128]{3,2,1,0:T(8,128)(2,1)}, u32[]{:S(2)}) copy-start(bf16[2,1,1024,128]{3,2,1,0:T(8,128)(2,1)} %get-tuple-element.14) | copy-start | bytes 1572868
  93.4 44.0 %collective-permute-start = (bf16[2,1024,128]{1,2,0:T(8,128)(2,1)}, bf16[2,1024,128]{1,2,0:T(8,128)(2,1)}, u32[]{:S(2)}, u32[]{:S(2)}) collective-permute-start(bf16[2,1024,128]{1,2,0:T(8,128)(2,1)} %bitcast.18), channel_id=1, source_target_pairs={{0,2},{2,0},{64,66},{66,64},{1,3},{3,1},{65,67},{67,65},{4,6},{6,4... | collective-permute-start | bytes 1572872 | tf_op jit(solution)/shard_map/ppermute | solution.py:164
  98.8 39.7 %collective-permute-start.1 = (bf16[2,1024,128]{1,2,0:T(8,128)(2,1)}, bf16[2,1024,128]{1,2,0:T(8,128)(2,1)}, u32[]{:S(2)}, u32[]{:S(2)}) collective-permute-start(bf16[2,1024,128]{1,2,0:T(8,128)(2,1)} %bitcast.20), channel_id=1, source_target_pairs={{0,64},{2,66},{64,0},{66,2},{1,65},{3,67},{65,1},{67,3},{4,68},{6,... | collective-permute-start | bytes 1572872 | tf_op jit(solution)/shard_map/ppermute | solution.py:164
  101.8 37.8 %collective-permute-start.2 = (bf16[2,1024,128]{1,2,0:T(8,128)(2,1)}, bf16[2,1024,128]{1,2,0:T(8,128)(2,1)}, u32[]{:S(2)}, u32[]{:S(2)}) collective-permute-start(bf16[2,1024,128]{1,2,0:T(8,128)(2,1)} %bitcast.22), channel_id=1, source_target_pairs={{0,66},{2,64},{64,2},{66,0},{1,67},{3,65},{65,3},{67,1},{4,70},{6,... | collective-permute-start | bytes 1572872 | tf_op jit(solution)/shard_map/ppermute | solution.py:164
  105.9 1.0 copy-start.2
  171.3 4.9 %copy-start.6 = (bf16[1,1024,512]{2,1,0:T(8,128)(2,1)S(1)}, bf16[1,1024,512]{2,1,0:T(8,128)(2,1)}, u32[]{:S(2)}) copy-start(bf16[1,1024,512]{2,1,0:T(8,128)(2,1)} %param.21) | copy-start | bytes 3145732
  172.5 67.1 %all-to-all-start.5 = ((bf16[4,256,512]{2,1,0:T(8,128)(2,1)}), bf16[4,256,512]{2,1,0:T(8,128)(2,1)S(1)}, u32[]{:S(2)}, u32[]{:S(2)}) async-start(bf16[4,256,512]{2,1,0:T(8,128)(2,1)} %broadcast_in_dim.61), calls=%async_computation.5 | async-start | bytes 2097152 | tf_op jit(solution)/shard_map/all_to_all | solution.py:25
  177.2 60.3 %collective-permute-start.3 = (bf16[256,512]{1,0:T(8,128)(2,1)}, bf16[256,512]{1,0:T(8,128)(2,1)}, u32[]{:S(2)}, u32[]{:S(2)}) collective-permute-start(bf16[256,512]{1,0:T(8,128)(2,1)} %bitcast.28), channel_id=1, source_target_pairs={{0,1},{1,0},{2,3},{3,2},{4,65},{5,64},{6,67},{7,66},{64,5},{65,4},... | collective-permute-start | bytes 786440 | tf_op jit(solution)/shard_map/ppermute | solution.py:198
  183.7 54.9 %collective-permute-start.4 = (bf16[256,512]{1,0:T(8,128)(2,1)}, bf16[256,512]{1,0:T(8,128)(2,1)}, u32[]{:S(2)}, u32[]{:S(2)}) collective-permute-start(bf16[256,512]{1,0:T(8,128)(2,1)} %bitcast.30), channel_id=1, source_target_pairs={{0,5},{1,4},{2,7},{3,6},{4,69},{5,68},{6,71},{7,70},{64,1},{65,0},... | collective-permute-start | bytes 786440 | tf_op jit(solution)/shard_map/ppermute | solution.py:198
  190.1 49.5 %collective-permute-start.5 = (bf16[256,512]{1,0:T(8,128)(2,1)}, bf16[256,512]{1,0:T(8,128)(2,1)S(1)}, u32[]{:S(2)}, u32[]{:S(2)}) collective-permute-start(bf16[256,512]{1,0:T(8,128)(2,1)} %bitcast.91), channel_id=1, source_target_pairs={{0,0},{1,1},{2,2},{3,3},{4,64},{5,65},{6,66},{7,67},{64,4},{65,5},... | collective-permute-start | bytes 786440 | tf_op jit(solution)/shard_map/ppermute | solution.py:198
  195.5 44.1 %collective-permute-start.6 = (bf16[256,512]{1,0:T(8,128)(2,1)S(1)}, bf16[256,512]{1,0:T(8,128)(2,1)S(1)}, u32[]{:S(2)}, u32[]{:S(2)}) collective-permute-start(bf16[256,512]{1,0:T(8,128)(2,1)S(1)} %bitcast.90), channel_id=1, source_target_pairs={{0,4},{1,5},{2,6},{3,7},{4,68},{5,69},{6,70},{7,71},{64,0},{65,1},... | collective-permute-start | bytes 786440 | tf_op jit(solution)/shard_map/ppermute | solution.py:198
  242.3 50.4 %all-to-all-start.6 = ((bf16[32,32,1024]{2,1,0:T(8,128)(2,1)}), bf16[32,32,1024]{2,1,0:T(8,128)(2,1)S(1)}, u32[]{:S(2)}, u32[]{:S(2)}) async-start(bf16[32,32,1024]{2,1,0:T(8,128)(2,1)} %bitcast.82), calls=%async_computation.6 | async-start | bytes 4194304 | tf_op jit(solution)/shard_map/all_to_all | solution.py:25
  292.7 1.3 copy-start.1

commit v4 on v3

--- a/solution.py
+++ b/solution.py
@@ -15,7 +15,6 @@
 
 ATTN = ("ab", "am", "al")
 HIDDEN = ("xh", "xl")
-QUAD = ("al", "xl")
 Z_AXES = ("pair", "ab", "am", "al")
 ROUTE = ("xh", "xl", "y", "core")
 LANES = 128
@@ -68,19 +67,17 @@
     ).astype(BF16)
 
 
-def pick_rows(tokens, slots, chunk, copies):
+def pick_rows(tokens, slots, chunk):
     count = tokens.shape[0]
-    width = tokens.shape[1] - LANES
-    parts = width // chunk
     return pl.pallas_call(
         pick_kernel,
-        grid=(copies * parts,),
+        grid=(D // chunk,),
         in_specs=[
-            pl.BlockSpec((count, chunk), lambda j: (0, j % parts)),
-            pl.BlockSpec((count, LANES), lambda j: (0, width // LANES)),
+            pl.BlockSpec((count, chunk), lambda j: (0, j)),
+            pl.BlockSpec((count, LANES), lambda j: (0, D // LANES)),
         ],
         out_specs=pl.BlockSpec((1, slots, chunk), lambda j: (j, 0, 0)),
-        out_shape=jax.ShapeDtypeStruct((copies * parts, slots, chunk), BF16),
+        out_shape=jax.ShapeDtypeStruct((D // chunk, slots, chunk), BF16),
         name="pick",
     )(tokens, tokens)
 
@@ -143,11 +140,10 @@
     zl = lax.axis_size(ATTN)
     pairs = lax.axis_size("pair")
     experts = lax.axis_size(("y", "core"))
-    quad = lax.axis_size(QUAD)
     capacity = 2
-    chunk = D // quad
+    chunk = D // xs
     unit = gate_up_weight.shape[-1]
-    half = quad * unit
+    half = xs * unit
 
     heads_out = attention(queries[0], keys[0], values[0], doc_lengths[0])
     tok_group = heads_out.shape[0]
@@ -155,13 +151,13 @@
     projected = jnp.dot(heads_out, out_weight, preferred_element_type=F32).astype(BF16)
     projected = projected.reshape(zl, xs, owned, D).transpose(1, 0, 2, 3)
     projected = jnp.sum(exchange(projected, HIDDEN).astype(F32), axis=0).astype(BF16)
-    me = lax.axis_index(QUAD)
-    gate_up = gate_up_weight[0].reshape(2, quad, chunk, unit)
-    gathered = jnp.zeros((quad, 2, chunk, unit), BF16)
-    for d in range(quad):
+    me = lax.axis_index(HIDDEN)
+    gate_up = gate_up_weight[0].reshape(2, xs, chunk, unit)
+    gathered = jnp.zeros((xs, 2, chunk, unit), BF16)
+    for d in range(xs):
         block = lax.dynamic_index_in_dim(gate_up, me ^ d, 1, keepdims=False)
         if d > 0:
-            block = lax.ppermute(block, QUAD, [(i, i ^ d) for i in range(quad)])
+            block = lax.ppermute(block, HIDDEN, [(i, i ^ d) for i in range(xs)])
         gathered = lax.dynamic_update_index_in_dim(gathered, block, me ^ d, 0)
     projected = jnp.sum(exchange(projected, ATTN).astype(F32), axis=0)
     gate_up = gathered.transpose(2, 1, 0, 3).reshape(chunk, 2 * half)
@@ -174,18 +170,14 @@
     slots = slot_numbers(chosen, lax.axis_index(Z_AXES), places, capacity).reshape(owned, 2)
     logits = route_logits[0]
     note = note_of(slots, jax.nn.sigmoid(logits[:, 0] - logits[:, 1]))
+    noted = jnp.concatenate([normed, note], axis=1)
+    tokens = exchange(jnp.broadcast_to(noted, (places, *noted.shape)), Z_AXES)
+    tokens = tokens.reshape(places * owned, D + LANES)
+    note = tokens[:, D:]
+
+    group_slots = experts * places * capacity
+    picked = pick_rows(tokens, group_slots, chunk)
     parity = lax.axis_size("al")
-    width = D // parity
-    noted = jnp.stack(
-        [jnp.concatenate([normed[:, k * width : (k + 1) * width], note], axis=1) for k in range(parity)]
-    )
-    noted = jnp.broadcast_to(noted, (places // parity, *noted.shape))
-    tokens = exchange(noted.reshape(places, owned, width + LANES), Z_AXES)
-    tokens = tokens.reshape(places * owned, width + LANES)
-    note = tokens[:, width:]
-
-    group_slots = experts * places * capacity
-    picked = pick_rows(tokens, group_slots, chunk, lax.axis_size("xh"))
     blocks = down_weight[0].reshape(2, 2, pairs, unit, -1)
     part = blocks.shape[-1]
     picked, blocks = lax.optimization_barrier((picked, blocks))
@@ -197,19 +189,22 @@
         ).reshape(2 * unit, part)
         sent = lax.ppermute(sent, ("ab", "am", "al", "xh", "xl", "pair"), down_moves(i, j))
         down = lax.dynamic_update_slice(down, sent[None], (xh ^ i, 0, (z_hi ^ j) * part))
-    down = down.reshape(half, chunk)
     rows = exchange(picked.reshape(xs * experts, -1, chunk), ROUTE).reshape(-1, chunk)
 
     partial = jnp.dot(rows, gate_up, preferred_element_type=F32).astype(BF16)
-    partial = partial.reshape(quad, -1, partial.shape[1])
-    summed = jnp.sum(exchange(partial, QUAD).astype(F32), axis=0)
+    partial = partial.reshape(xs, -1, partial.shape[1])
+    summed = jnp.sum(exchange(partial, HIDDEN).astype(F32), axis=0)
     activated = (jax.nn.silu(summed[:, :half]) * summed[:, half:]).astype(BF16)
-    activated = exchange(jnp.broadcast_to(activated, (quad, *activated.shape)), QUAD)
-    activated = activated.reshape(-1, half)
-    out = jnp.dot(activated, down, preferred_element_type=F32).astype(BF16)
+    activated = jnp.stack([activated[:, : half // 2], activated[:, half // 2 :]])[None, :, None]
+    activated = jnp.broadcast_to(activated, (parity, 2, 2, *activated.shape[3:]))
+    activated = activated.reshape(parity * xs, *activated.shape[3:])
+    activated = exchange(activated, ("al", *HIDDEN)).reshape(parity, -1, half // 2)
+    activated = jnp.concatenate([activated[k] for k in range(parity)], axis=1)
+    out = jnp.dot(activated, down.reshape(half, chunk), preferred_element_type=F32).astype(BF16)
 
     returned = exchange(out.reshape(xs * experts, -1, chunk), ROUTE)
     returned = combine_rows(note, returned.reshape(2, 2, group_slots, chunk))
+    width = D // parity
     mixed = exchange(returned.reshape(places, owned, width), Z_AXES)
     mixed = jnp.sum(mixed.reshape(-1, parity, owned, width).astype(F32), axis=0)
     layer_out = attended + jnp.concatenate([mixed[k] for k in range(parity)], axis=1)

time: 351 us -> 366 us (1.043)
  waiting for transfers between devices: 124 us -> 139 us
    ppermute x4, waiting for transfers between devices: 40 us -> 56.1 us  [layer(): lax.ppermute(sent, ('ab', 'am', 'al', 'xh', 'xl', 'pair'), down_moves(i, j))]
  transfers between devices with their start and end apart: 12 -> 12, of which waited for: 5 -> 6; matrix products, arithmetic and copies ran while one was open for 5% -> 5% of each run, Pallas kernels for 0% -> 0%
where the time goes in v4:
time: 366 us; the launch traced here: 363 us
  waiting for transfers between devices  139 us (38%)
  blocking collectives  97.3 us (27%)
  starting transfers between devices  82.2 us (22%)
  local copies, waits for them, and re-layouts  23.4 us (6%)
  matrix products  8.89 us (2%)
  Pallas kernels  7.3 us (2%)
  other arithmetic  4.65 us (1%)
    all_to_all x3, blocking collectives, exchange(): return lax.all_to_all(value, axes, 0, 0, tiled=True)  97.3 us
    ppermute x4, waiting for transfers between devices, layer(): lax.ppermute(sent, ('ab', 'am', 'al', 'xh', 'xl', 'pair'), down_moves(i, j))  56.1 us
    all_to_all x5, waiting for transfers between devices, exchange(): return lax.all_to_all(value, axes, 0, 0, tiled=True)  53.4 us
    all_to_all x5, starting transfers between devices, exchange(): return lax.all_to_all(value, axes, 0, 0, tiled=True)  52.1 us
    ppermute x3, waiting for transfers between devices, layer(): block = lax.ppermute(block, HIDDEN, [(i, i ^ d) for i in range(xs)])  29.5 us
    ppermute x4, starting transfers between devices, layer(): lax.ppermute(sent, ('ab', 'am', 'al', 'xh', 'xl', 'pair'), down_moves(i, j))  20.5 us
    ppermute x3, starting transfers between devices, layer(): block = lax.ppermute(block, HIDDEN, [(i, i ^ d) for i in range(xs)])  9.55 us
    unnamed x29, local copies, waits for them, and re-layouts  8.64 us
  transfers between devices with their start and end apart: 12, of which 6 were waited for; matrix products, arithmetic and copies ran while one was open for 5% of the time, Pallas kernels for 0%

profile of v4, /device:TPU:33, one launch (start us, length us, event | category | flops | bytes accessed | tf_op | source)
XLA Modules:
  0.0 363.1 jit_solution(1593289447620034166)
XLA Ops:
  2.0 1.4 convolution_convert_fusion
  3.8 1.4 copy.67
  5.2 4.1 %all-to-all-start = ((bf16[4,8,4,4096]{3,2,1,0:T(4,128)(2,1)}), bf16[4,8,4,4096]{3,2,1,0:T(4,128)(2,1)S(1)}, u32[]{:S(2)}, u32[]{:S(2)}) async-start(bf16[4,8,4,4096]{3,2,1,0:T(4,128)(2,1)} %bitcast.78), calls=%async_computation | async-start | bytes 2097152 | tf_op jit(solution)/shard_map/all_to_all | solution.py:24
  9.5 14.0 %all-to-all-done = bf16[4,8,4,4096]{3,2,1,0:T(4,128)(2,1)S(1)} async-done(((bf16[4,8,4,4096]{3,2,1,0:T(4,128)(2,1)}), bf16[4,8,4,4096]{3,2,1,0:T(4,128)(2,1)S(1)}, u32[]{:S(2)}, u32[]{:S(2)}) %all-to-all-start) | async-done | bytes 1048608 | tf_op jit(solution)/shard_map/all_to_all | solution.py:24
  23.6 1.4 reduce_sum.81
  25.0 12.1 %all-to-all-start.1 = ((bf16[8,4,4096]{2,1,0:T(4,128)(2,1)}), bf16[8,4,4096]{2,1,0:T(4,128)(2,1)S(1)}, u32[]{:S(2)}, u32[]{:S(2)}) async-start(bf16[8,4,4096]{2,1,0:T(4,128)(2,1)} %reduce_sum.81), calls=%async_computation.1 | async-start | bytes 524288 | tf_op jit(solution)/shard_map/all_to_all | solution.py:24
  37.8 12.4 %all-to-all-done.1 = bf16[8,4,4096]{2,1,0:T(4,128)(2,1)S(1)} async-done(((bf16[8,4,4096]{2,1,0:T(4,128)(2,1)}), bf16[8,4,4096]{2,1,0:T(4,128)(2,1)S(1)}, u32[]{:S(2)}, u32[]{:S(2)}) %all-to-all-start.1) | async-done | bytes 262176 | tf_op jit(solution)/shard_map/all_to_all | solution.py:24
  51.0 40.0 %all_to_all.40 = bf16[16,4,4224]{2,1,0:T(4,128)(2,1)S(1)} all-to-all(bf16[16,4,4224]{2,1,0:T(4,128)(2,1)S(1)} %broadcast_in_dim.58), channel_id=1, replica_groups=mesh['ab'=2,'am'=2,'al'=2,'y'=4,'core'=2,'xh'=2,'xl'=2,'pair'=2] {'pair'..., dimensions={0} | all-to-all | bytes 1081344 | tf_op jit(solution)/shard_map/all_to_all | solution.py:24
  91.9 4.2 %pick.1 = bf16[4,256,1024]{2,1,0:T(8,128)(2,1)} custom-call(bf16[64,4224]{1,0:T(8,128)(2,1)} %reshape.113.tokens_ref.note_ref, bf16[64,4224]{1,0:T(8,128)(2,1)} %reshape.113.tokens_ref.note_ref), custom_call_target="tpu_custom_call" | custom-call | tf_op jit(solution)/shard_map/pick/pallas_call | solution.py:72
  96.1 7.3 %all-to-all-start.3 = ((bf16[32,32,1024]{2,1,0:T(8,128)(2,1)}), bf16[32,32,1024]{2,1,0:T(8,128)(2,1)}, u32[]{:S(2)}, u32[]{:S(2)}) async-start(bf16[32,32,1024]{2,1,0:T(8,128)(2,1)} %bitcast.79), calls=%async_computation.3 | async-start | bytes 4194304 | tf_op jit(solution)/shard_map/all_to_all | solution.py:24
  103.5 1.4 constant_dynamic-slice_fusion.4
  104.9 2.1 copy.62
  107.0 3.3 collective-permute-start
  110.3 2.0 copy.63
  112.3 4.3 %collective-permute-start.1 = (bf16[2,1024,128]{1,2,0:T(8,128)(2,1)}, bf16[2,1024,128]{1,2,0:T(8,128)(2,1)}, u32[]{:S(2)}, u32[]{:S(2)}) collective-permute-start(bf16[2,1024,128]{1,2,0:T(8,128)(2,1)} %bitcast.17), channel_id=1, source_target_pairs={{0,4},{2,6},{4,0},{6,2},{1,5},{3,7},{5,1},{7,3},{8,12},{10,14},{12... | collective-permute-start | bytes 1572872 | tf_op jit(solution)/shard_map/ppermute | solution.py:160
  117.7 2.0 collective-permute-start.2
  121.8 18.0 %collective-permute-done = bf16[2,1024,128]{1,2,0:T(8,128)(2,1)} collective-permute-done((bf16[2,1024,128]{1,2,0:T(8,128)(2,1)}, bf16[2,1024,128]{1,2,0:T(8,128)(2,1)}, u32[]{:S(2)}, u32[]{:S(2)}) %collective-permute-start) | collective-permute-done | bytes 524320 | tf_op jit(solution)/shard_map/ppermute | solution.py:160
  140.8 11.5 %collective-permute-done.1 = bf16[2,1024,128]{1,2,0:T(8,128)(2,1)} collective-permute-done((bf16[2,1024,128]{1,2,0:T(8,128)(2,1)}, bf16[2,1024,128]{1,2,0:T(8,128)(2,1)}, u32[]{:S(2)}, u32[]{:S(2)}) %collective-permute-start.1) | collective-permute-done | bytes 524320 | tf_op jit(solution)/shard_map/ppermute | solution.py:160
  154.5 4.0 %convolution_convert_fusion.2 = bf16[1024,1024]{1,0:T(8,128)(2,1)S(1)} fusion(bf16[1024,1024]{1,0:T(8,128)(2,1)} %bitcast.12, bf16[1024,1024]{0,1:T(8,128)(2,1)S(1)} %bitcast.81), kind=kOutput, calls=%fused_computation.3 | convolution fusion | flops 2148532224 | bytes 6291456 | tf_op jit(solution)/shard_map/dot_general | solution.py:194
  158.5 27.9 %all_to_all.41 = bf16[4,256,1024]{2,1,0:T(8,128)(2,1)S(1)} all-to-all(bf16[4,256,1024]{2,1,0:T(8,128)(2,1)S(1)} %bitcast.83), channel_id=1, replica_groups=mesh['ab'=2,'am'=2,'al'=2,'y'=4,'core'=2,'xh'=2,'xl'=2,'pair'=2] {'xh','..., dimensions={0} | all-to-all | bytes 4194304 | tf_op jit(solution)/shard_map/all_to_all | solution.py:24
  188.1 4.6 %all-to-all-start.5 = ((bf16[8,256,256]{2,1,0:T(8,128)(2,1)}), bf16[8,256,256]{2,1,0:T(8,128)(2,1)S(1)}, u32[]{:S(2)}, u32[]{:S(2)}) async-start(bf16[8,256,256]{2,1,0:T(8,128)(2,1)} %bitcast.26), calls=%async_computation.5 | async-start | bytes 2097152 | tf_op jit(solution)/shard_map/all_to_all | solution.py:24
  193.6 4.0 %collective-permute-start.3 = (bf16[256,512]{1,0:T(8,128)(2,1)}, bf16[256,512]{1,0:T(8,128)(2,1)}, u32[]{:S(2)}, u32[]{:S(2)}) collective-permute-start(bf16[256,512]{1,0:T(8,128)(2,1)} %bitcast.29), channel_id=1, source_target_pairs={{0,1},{1,0},{2,3},{3,2},{4,65},{5,64},{6,67},{7,66},{64,5},{65,4},... | collective-permute-start | bytes 786440 | tf_op jit(solution)/shard_map/ppermute | solution.py:190
  197.5 9.0 %collective-permute-start.4 = (bf16[256,512]{1,0:T(8,128)(2,1)}, bf16[256,512]{1,0:T(8,128)(2,1)}, u32[]{:S(2)}, u32[]{:S(2)}) collective-permute-start(bf16[256,512]{1,0:T(8,128)(2,1)} %bitcast.31), channel_id=1, source_target_pairs={{0,5},{1,4},{2,7},{3,6},{4,69},{5,68},{6,71},{7,70},{64,1},{65,0},... | collective-permute-start | bytes 786440 | tf_op jit(solution)/shard_map/ppermute | solution.py:190
  206.5 5.7 %collective-permute-start.5 = (bf16[256,512]{1,0:T(8,128)(2,1)}, bf16[256,512]{1,0:T(8,128)(2,1)S(1)}, u32[]{:S(2)}, u32[]{:S(2)}) collective-permute-start(bf16[256,512]{1,0:T(8,128)(2,1)} %bitcast.91), channel_id=1, source_target_pairs={{0,0},{1,1},{2,2},{3,3},{4,64},{5,65},{6,66},{7,67},{64,4},{65,5},... | collective-permute-start | bytes 786440 | tf_op jit(solution)/shard_map/ppermute | solution.py:190
  212.2 1.9 collective-permute-start.6
  214.1 56.1 %collective-permute-done.3 = bf16[256,512]{1,0:T(8,128)(2,1)} collective-permute-done((bf16[256,512]{1,0:T(8,128)(2,1)}, bf16[256,512]{1,0:T(8,128)(2,1)}, u32[]{:S(2)}, u32[]{:S(2)}) %collective-permute-start.3) | collective-permute-done | bytes 262176 | tf_op jit(solution)/shard_map/ppermute | solution.py:190
  272.5 2.6 convolution_convert_fusion.1
  275.1 24.0 %all-to-all-start.6 = ((bf16[32,32,1024]{2,1,0:T(8,128)(2,1)}), bf16[32,32,1024]{2,1,0:T(8,128)(2,1)S(1)}, u32[]{:S(2)}, u32[]{:S(2)}) async-start(bf16[32,32,1024]{2,1,0:T(8,128)(2,1)} %bitcast.82), calls=%async_computation.6 | async-start | bytes 4194304 | tf_op jit(solution)/shard_map/all_to_all | solution.py:24
  300.5 27.0 %all-to-all-done.6 = bf16[32,32,1024]{2,1,0:T(8,128)(2,1)S(1)} async-done(((bf16[32,32,1024]{2,1,0:T(8,128)(2,1)}), bf16[32,32,1024]{2,1,0:T(8,128)(2,1)S(1)}, u32[]{:S(2)}, u32[]{:S(2)}) %all-to-all-start.6) | async-done | bytes 2097184 | tf_op jit(solution)/shard_map/all_to_all | solution.py:24
  327.5 1.3 copy-done.1
  328.8 3.1 combine.1
  333.0 29.4 %all_to_all.42 = bf16[16,4,2048]{2,1,0:T(4,128)(2,1)S(1)} all-to-all(bf16[16,4,2048]{2,1,0:T(4,128)(2,1)S(1)} %reshape.126), channel_id=1, replica_groups=mesh['ab'=2,'am'=2,'al'=2,'y'=4,'core'=2,'xh'=2,'xl'=2,'pair'=2] {'pair'..., dimensions={0} | all-to-all | bytes 524288 | tf_op jit(solution)/shard_map/all_to_all | solution.py:24
  (77 shorter events, 19.3 us)
Async XLA Ops:
  0.0 2.0 copy-start
  3.8 5.6 %copy-start.9 = (s32[1,4,2]{1,2,0:T(2,128)S(1)}, s32[1,4,2]{1,2,0:T(2,128)}, u32[]{:S(2)}) copy-start(s32[1,4,2]{1,2,0:T(2,128)} %param.18) | copy-start | bytes 100
  5.2 32.2 %copy-start.10 = (f32[1,4,2]{1,2,0:T(2,128)S(1)}, f32[1,4,2]{1,2,0:T(2,128)}, u32[]{:S(2)}) copy-start(f32[1,4,2]{1,2,0:T(2,128)} %param.17) | copy-start | bytes 100
  5.2 45.3 %copy-start.7 = (bf16[1,4,4096]{2,1,0:T(4,128)(2,1)S(1)}, bf16[1,4,4096]{2,1,0:T(4,128)(2,1)}, u32[]{:S(2)}) copy-start(bf16[1,4,4096]{2,1,0:T(4,128)(2,1)} %param.15) | copy-start | bytes 98308
  5.2 45.4 %copy-start.8 = (f32[4096]{0:T(1024)S(1)}, f32[4096]{0:T(1024)}, u32[]{:S(2)}) copy-start(f32[4096]{0:T(1024)} %param.16) | copy-start | bytes 49156
  5.2 18.4 %all-to-all-start = ((bf16[4,8,4,4096]{3,2,1,0:T(4,128)(2,1)}), bf16[4,8,4,4096]{3,2,1,0:T(4,128)(2,1)S(1)}, u32[]{:S(2)}, u32[]{:S(2)}) async-start(bf16[4,8,4,4096]{3,2,1,0:T(4,128)(2,1)} %bitcast.78), calls=%async_computation | async-start | bytes 2097152 | tf_op jit(solution)/shard_map/all_to_all | solution.py:24
  25.0 25.2 %all-to-all-start.1 = ((bf16[8,4,4096]{2,1,0:T(4,128)(2,1)}), bf16[8,4,4096]{2,1,0:T(4,128)(2,1)S(1)}, u32[]{:S(2)}, u32[]{:S(2)}) async-start(bf16[8,4,4096]{2,1,0:T(4,128)(2,1)} %reduce_sum.81), calls=%async_computation.1 | async-start | bytes 524288 | tf_op jit(solution)/shard_map/all_to_all | solution.py:24
  96.1 7.4 %copy-start.3 = (bf16[1,2,4096,128]{3,2,1,0:T(8,128)(2,1)S(1)}, bf16[1,2,4096,128]{3,2,1,0:T(8,128)(2,1)}, u32[]{:S(2)}) copy-start(bf16[1,2,4096,128]{3,2,1,0:T(8,128)(2,1)} %param.20) | copy-start | bytes 6291460
  96.1 58.4 %all-to-all-start.3 = ((bf16[32,32,1024]{2,1,0:T(8,128)(2,1)}), bf16[32,32,1024]{2,1,0:T(8,128)(2,1)}, u32[]{:S(2)}, u32[]{:S(2)}) async-start(bf16[32,32,1024]{2,1,0:T(8,128)(2,1)} %bitcast.79), calls=%async_computation.3 | async-start | bytes 4194304 | tf_op jit(solution)/shard_map/all_to_all | solution.py:24
  104.9 11.8 %copy-start.5 = (bf16[2,1,1024,128]{3,2,1,0:T(8,128)(2,1)S(1)}, bf16[2,1,1024,128]{3,2,1,0:T(8,128)(2,1)}, u32[]{:S(2)}) copy-start(bf16[2,1,1024,128]{3,2,1,0:T(8,128)(2,1)} %get-tuple-element.11) | copy-start | bytes 1572868
  104.9 14.8 %copy-start.4 = (bf16[2,1,1024,128]{3,2,1,0:T(8,128)(2,1)S(1)}, bf16[2,1,1024,128]{3,2,1,0:T(8,128)(2,1)}, u32[]{:S(2)}) copy-start(bf16[2,1,1024,128]{3,2,1,0:T(8,128)(2,1)} %get-tuple-element.14) | copy-start | bytes 1572868
  107.0 32.7 %collective-permute-start = (bf16[2,1024,128]{1,2,0:T(8,128)(2,1)}, bf16[2,1024,128]{1,2,0:T(8,128)(2,1)}, u32[]{:S(2)}, u32[]{:S(2)}) collective-permute-start(bf16[2,1024,128]{1,2,0:T(8,128)(2,1)} %bitcast.15), channel_id=1, source_target_pairs={{0,2},{2,0},{4,6},{6,4},{1,3},{3,1},{5,7},{7,5},{8,10},{10,8},{12,... | collective-permute-start | bytes 1572872 | tf_op jit(solution)/shard_map/ppermute | solution.py:160
  112.3 40.0 %collective-permute-start.1 = (bf16[2,1024,128]{1,2,0:T(8,128)(2,1)}, bf16[2,1024,128]{1,2,0:T(8,128)(2,1)}, u32[]{:S(2)}, u32[]{:S(2)}) collective-permute-start(bf16[2,1024,128]{1,2,0:T(8,128)(2,1)} %bitcast.17), channel_id=1, source_target_pairs={{0,4},{2,6},{4,0},{6,2},{1,5},{3,7},{5,1},{7,3},{8,12},{10,14},{12... | collective-permute-start | bytes 1572872 | tf_op jit(solution)/shard_map/ppermute | solution.py:160
  117.7 35.7 %collective-permute-start.2 = (bf16[2,1024,128]{1,2,0:T(8,128)(2,1)}, bf16[2,1024,128]{1,2,0:T(8,128)(2,1)}, u32[]{:S(2)}, u32[]{:S(2)}) collective-permute-start(bf16[2,1024,128]{1,2,0:T(8,128)(2,1)} %bitcast.19), channel_id=1, source_target_pairs={{0,6},{2,4},{4,2},{6,0},{1,7},{3,5},{5,3},{7,1},{8,14},{10,12},{12... | collective-permute-start | bytes 1572872 | tf_op jit(solution)/shard_map/ppermute | solution.py:160
  120.7 1.0 copy-start.2
  187.0 5.7 %copy-start.6 = (bf16[1,1024,512]{2,1,0:T(8,128)(2,1)S(1)}, bf16[1,1024,512]{2,1,0:T(8,128)(2,1)}, u32[]{:S(2)}) copy-start(bf16[1,1024,512]{2,1,0:T(8,128)(2,1)} %param.21) | copy-start | bytes 3145732
  188.1 84.3 %all-to-all-start.5 = ((bf16[8,256,256]{2,1,0:T(8,128)(2,1)}), bf16[8,256,256]{2,1,0:T(8,128)(2,1)S(1)}, u32[]{:S(2)}, u32[]{:S(2)}) async-start(bf16[8,256,256]{2,1,0:T(8,128)(2,1)} %bitcast.26), calls=%async_computation.5 | async-start | bytes 2097152 | tf_op jit(solution)/shard_map/all_to_all | solution.py:24
  193.6 76.6 %collective-permute-start.3 = (bf16[256,512]{1,0:T(8,128)(2,1)}, bf16[256,512]{1,0:T(8,128)(2,1)}, u32[]{:S(2)}, u32[]{:S(2)}) collective-permute-start(bf16[256,512]{1,0:T(8,128)(2,1)} %bitcast.29), channel_id=1, source_target_pairs={{0,1},{1,0},{2,3},{3,2},{4,65},{5,64},{6,67},{7,66},{64,5},{65,4},... | collective-permute-start | bytes 786440 | tf_op jit(solution)/shard_map/ppermute | solution.py:190
  197.5 73.8 %collective-permute-start.4 = (bf16[256,512]{1,0:T(8,128)(2,1)}, bf16[256,512]{1,0:T(8,128)(2,1)}, u32[]{:S(2)}, u32[]{:S(2)}) collective-permute-start(bf16[256,512]{1,0:T(8,128)(2,1)} %bitcast.31), channel_id=1, source_target_pairs={{0,5},{1,4},{2,7},{3,6},{4,69},{5,68},{6,71},{7,70},{64,1},{65,0},... | collective-permute-start | bytes 786440 | tf_op jit(solution)/shard_map/ppermute | solution.py:190
  206.5 65.8 %collective-permute-start.5 = (bf16[256,512]{1,0:T(8,128)(2,1)}, bf16[256,512]{1,0:T(8,128)(2,1)S(1)}, u32[]{:S(2)}, u32[]{:S(2)}) collective-permute-start(bf16[256,512]{1,0:T(8,128)(2,1)} %bitcast.91), channel_id=1, source_target_pairs={{0,0},{1,1},{2,2},{3,3},{4,64},{5,65},{6,66},{7,67},{64,4},{65,5},... | collective-permute-start | bytes 786440 | tf_op jit(solution)/shard_map/ppermute | solution.py:190
  212.2 60.2 %collective-permute-start.6 = (bf16[256,512]{1,0:T(8,128)(2,1)S(1)}, bf16[256,512]{1,0:T(8,128)(2,1)S(1)}, u32[]{:S(2)}, u32[]{:S(2)}) collective-permute-start(bf16[256,512]{1,0:T(8,128)(2,1)S(1)} %bitcast.90), channel_id=1, source_target_pairs={{0,4},{1,5},{2,6},{3,7},{4,68},{5,69},{6,70},{7,71},{64,0},{65,1},... | collective-permute-start | bytes 786440 | tf_op jit(solution)/shard_map/ppermute | solution.py:190
  275.1 52.4 %all-to-all-start.6 = ((bf16[32,32,1024]{2,1,0:T(8,128)(2,1)}), bf16[32,32,1024]{2,1,0:T(8,128)(2,1)S(1)}, u32[]{:S(2)}, u32[]{:S(2)}) async-start(bf16[32,32,1024]{2,1,0:T(8,128)(2,1)} %bitcast.82), calls=%async_computation.6 | async-start | bytes 4194304 | tf_op jit(solution)/shard_map/all_to_all | solution.py:24
  327.5 1.3 copy-start.1

commit v5 on v2

--- a/solution.py
+++ b/solution.py
@@ -13,9 +13,9 @@
 F32 = jnp.float32
 
 
-ATTN = ("ab", "aa")
-Z_AXES = ("pair", "ab", "aa")
-ROUTE = ("hidden", "y", "core")
+ATTN = ("ab", "am", "al")
+Z_AXES = ("pair", "ab", "am")
+ROUTE = ("al", "hidden", "y", "core")
 LANES = 128
 
 
@@ -66,17 +66,18 @@
     ).astype(BF16)
 
 
-def pick_rows(tokens, slots, chunk):
+def pick_rows(tokens, slots, chunk, copies):
     count = tokens.shape[0]
+    parts = D // chunk
     return pl.pallas_call(
         pick_kernel,
-        grid=(D // chunk,),
+        grid=(copies * parts,),
         in_specs=[
-            pl.BlockSpec((count, chunk), lambda j: (0, j)),
+            pl.BlockSpec((count, chunk), lambda j: (0, j % parts)),
             pl.BlockSpec((count, LANES), lambda j: (0, D // LANES)),
         ],
         out_specs=pl.BlockSpec((1, slots, chunk), lambda j: (j, 0, 0)),
-        out_shape=jax.ShapeDtypeStruct((D // chunk, slots, chunk), BF16),
+        out_shape=jax.ShapeDtypeStruct((copies * parts, slots, chunk), BF16),
         name="pick",
     )(tokens, tokens)
 
@@ -84,25 +85,28 @@
 def combine_kernel(note_ref, rows_ref, out_ref):
     note = note_ref[...].astype(F32)
     share = note[:, 2:3] + note[:, 3:4] + note[:, 4:5]
-    slots = lax.broadcasted_iota(jnp.int32, (note.shape[0], rows_ref.shape[1]), 1).astype(F32)
+    slots = lax.broadcasted_iota(jnp.int32, (note.shape[0], rows_ref.shape[2]), 1).astype(F32)
     weight = jnp.where(slots == note[:, 0:1], share, 0.0)
     weight = weight + jnp.where(slots == note[:, 1:2], 1.0 - share, 0.0)
     high = weight.astype(BF16)
     low = (weight - high.astype(F32)).astype(BF16)
-    rows = rows_ref[0]
-    total = jnp.dot(high, rows, preferred_element_type=F32)
-    out_ref[...] = (total + jnp.dot(low, rows, preferred_element_type=F32)).astype(BF16)
+    total = jnp.zeros(out_ref.shape, F32)
+    for k in range(rows_ref.shape[0]):
+        rows = rows_ref[k, 0]
+        total += jnp.dot(high, rows, preferred_element_type=F32)
+        total += jnp.dot(low, rows, preferred_element_type=F32)
+    out_ref[...] = total.astype(BF16)
 
 
 def combine_rows(note, rows):
     count = note.shape[0]
-    chunks, slots, chunk = rows.shape
+    sums, chunks, slots, chunk = rows.shape
     return pl.pallas_call(
         combine_kernel,
         grid=(chunks,),
         in_specs=[
             pl.BlockSpec((count, LANES), lambda j: (0, 0)),
-            pl.BlockSpec((1, slots, chunk), lambda j: (j, 0, 0)),
+            pl.BlockSpec((sums, 1, slots, chunk), lambda j: (0, j, 0, 0)),
         ],
         out_specs=pl.BlockSpec((count, chunk), lambda j: (0, j)),
         out_shape=jax.ShapeDtypeStruct((count, chunks * chunk), BF16),
@@ -168,10 +172,11 @@
     note = tokens[:, D:]
 
     group_slots = experts * places * capacity
-    picked = pick_rows(tokens, group_slots, chunk)
+    parities = lax.axis_size("al")
+    picked = pick_rows(tokens, group_slots, chunk, parities)
     picked, sent = lax.optimization_barrier((picked, sent))
     other = lax.ppermute(sent, "pair", [(0, 1), (1, 0)])
-    rows = exchange(picked.reshape(xs * experts, -1, chunk), ROUTE).reshape(-1, chunk)
+    rows = exchange(picked.reshape(parities * xs * experts, -1, chunk), ROUTE).reshape(-1, chunk)
 
     partial = jnp.dot(rows, gate_up, preferred_element_type=F32).astype(BF16)
     partial = partial.reshape(xs, -1, partial.shape[1])
@@ -187,8 +192,8 @@
     )
     out = jnp.dot(activated, down, preferred_element_type=F32).astype(BF16)
 
-    returned = exchange(out.reshape(xs * experts, -1, chunk), ROUTE)
-    returned = combine_rows(note, returned.reshape(xs, group_slots, chunk))
+    returned = exchange(out.reshape(parities * xs * experts, -1, chunk), ROUTE)
+    returned = combine_rows(note, returned.reshape(parities, xs, group_slots, chunk))
     mixed = exchange(returned.reshape(places, owned, D), Z_AXES)
     layer_out = attended + jnp.sum(mixed.astype(F32), axis=0)
     return layer_out.astype(BF16)[None]
@@ -196,11 +201,12 @@
 
 def solution(mesh):
     cut = Mesh(
-        mesh.devices.reshape(2, 4, 4, 2, 4, 2), ("ab", "aa", "y", "core", "hidden", "pair")
+        mesh.devices.reshape(2, 2, 2, 4, 2, 4, 2),
+        ("ab", "am", "al", "y", "core", "hidden", "pair"),
     )
     expert = ("y", "core")
     group = ("y", "core", "pair")
-    owner = ("ab", "aa", "hidden")
+    owner = (*ATTN, "hidden")
     in_specs = (
         P(group, None, owner),
         P(group, None, ATTN),
@@ -211,7 +217,7 @@
         P(group, owner, None),
         P(group, owner, None),
         P(group, None),
-        P(expert, None, None, ("ab", "aa", "hidden", "pair")),
+        P(expert, None, None, (*owner, "pair")),
         P(expert, ATTN, ("hidden", "pair")),
     )
     return jax.shard_map(

time: 305 us -> 288 us (0.944)
  the two profiles are of different devices: /device:TPU:33 before, /device:TPU:3 now
where the time goes in v5:
time: 288 us; the launch traced here: 286 us
  waiting for transfers between devices  126 us (44%)
  starting transfers between devices  85.1 us (30%)
  blocking collectives  24.6 us (9%)
  local copies, waits for them, and re-layouts  21.9 us (8%)
  matrix products  11.2 us (4%)
  Pallas kernels  10.5 us (4%)
  other arithmetic  6.52 us (2%)
    all_to_all x7, waiting for transfers between devices, exchange(): return lax.all_to_all(value, axes, 0, 0, tiled=True)  80.8 us
    all_to_all x7, starting transfers between devices, exchange(): return lax.all_to_all(value, axes, 0, 0, tiled=True)  71.7 us
    ppermute x3, waiting for transfers between devices, layer(): lax.ppermute(block, 'hidden', [(i, (i + d) % xs) for i in range(xs)])  25.9 us
    all_to_all x1, blocking collectives, exchange(): return lax.all_to_all(value, axes, 0, 0, tiled=True)  24.6 us
    ppermute x1, waiting for transfers between devices, layer(): other = lax.ppermute(sent, 'pair', [(0, 1), (1, 0)])  19.5 us
    ppermute x3, starting transfers between devices, layer(): lax.ppermute(block, 'hidden', [(i, (i + d) % xs) for i in range(xs)])  9.6 us
    unnamed x31, local copies, waits for them, and re-layouts  8.75 us
    pallas_call x1, Pallas kernels, pick_rows(): pl.pallas_call(pick_kernel, grid=(copies * parts,), in_specs=[pl.BlockSpe...  6.31 us
  transfers between devices with their start and end apart: 11, of which 9 were waited for; matrix products, arithmetic and copies ran while one was open for 6% of the time, Pallas kernels for 0%

profile of v5, /device:TPU:3, one launch (start us, length us, event | category | flops | bytes accessed | tf_op | source)
XLA Modules:
  0.0 286.3 jit_solution(6073083342392141179)
XLA Ops:
  2.0 1.4 convolution_convert_fusion
  3.8 1.4 copy.67
  5.2 4.4 %all-to-all-start = ((bf16[4,8,4,4096]{3,2,1,0:T(4,128)(2,1)}), bf16[4,8,4,4096]{3,2,1,0:T(4,128)(2,1)S(1)}, u32[]{:S(2)}, u32[]{:S(2)}) async-start(bf16[4,8,4,4096]{3,2,1,0:T(4,128)(2,1)} %bitcast.67), calls=%async_computation | async-start | bytes 2097152 | tf_op jit(solution)/shard_map/all_to_all | solution.py:23
  9.8 8.4 %all-to-all-done = bf16[4,8,4,4096]{3,2,1,0:T(4,128)(2,1)S(1)} async-done(((bf16[4,8,4,4096]{3,2,1,0:T(4,128)(2,1)}), bf16[4,8,4,4096]{3,2,1,0:T(4,128)(2,1)S(1)}, u32[]{:S(2)}, u32[]{:S(2)}) %all-to-all-start) | async-done | bytes 1048608 | tf_op jit(solution)/shard_map/all_to_all | solution.py:23
  18.2 1.4 reduce_sum.83
  19.6 16.7 %all-to-all-start.1 = ((bf16[8,4,4096]{2,1,0:T(4,128)(2,1)}), bf16[8,4,4096]{2,1,0:T(4,128)(2,1)S(1)}, u32[]{:S(2)}, u32[]{:S(2)}) async-start(bf16[8,4,4096]{2,1,0:T(4,128)(2,1)} %reduce_sum.83), calls=%async_computation.1 | async-start | bytes 524288 | tf_op jit(solution)/shard_map/all_to_all | solution.py:23
  37.1 11.2 %all-to-all-done.1 = bf16[8,4,4096]{2,1,0:T(4,128)(2,1)S(1)} async-done(((bf16[8,4,4096]{2,1,0:T(4,128)(2,1)}), bf16[8,4,4096]{2,1,0:T(4,128)(2,1)S(1)}, u32[]{:S(2)}, u32[]{:S(2)}) %all-to-all-start.1) | async-done | bytes 262176 | tf_op jit(solution)/shard_map/all_to_all | solution.py:23
  49.7 9.0 %all-to-all-start.2 = ((bf16[8,4,4224]{2,1,0:T(4,128)(2,1)}), bf16[8,4,4224]{2,1,0:T(4,128)(2,1)S(1)}, u32[]{:S(2)}, u32[]{:S(2)}) async-start(bf16[8,4,4224]{2,1,0:T(4,128)(2,1)} %broadcast_in_dim.40), calls=%async_computation.2 | async-start | bytes 540672 | tf_op jit(solution)/shard_map/all_to_all | solution.py:23
  59.8 14.5 %all-to-all-done.2 = bf16[8,4,4224]{2,1,0:T(4,128)(2,1)S(1)} async-done(((bf16[8,4,4224]{2,1,0:T(4,128)(2,1)}), bf16[8,4,4224]{2,1,0:T(4,128)(2,1)S(1)}, u32[]{:S(2)}, u32[]{:S(2)}) %all-to-all-start.2) | async-done | bytes 270368 | tf_op jit(solution)/shard_map/all_to_all | solution.py:23
  75.1 6.3 %pick.1 = bf16[8,128,1024]{2,1,0:T(8,128)(2,1)} custom-call(bf16[32,4224]{1,0:T(8,128)(2,1)} %reshape.93.tokens_ref.note_ref, bf16[32,4224]{1,0:T(8,128)(2,1)} %reshape.93.tokens_ref.note_ref), custom_call_target="tpu_custom_call" | custom-call | tf_op jit(solution)/shard_map/pick/pallas_call | solution.py:72
  81.4 14.1 %all-to-all-start.3 = ((bf16[64,16,1024]{2,1,0:T(8,128)(2,1)}), bf16[64,16,1024]{2,1,0:T(8,128)(2,1)}, u32[]{:S(2)}, u32[]{:S(2)}) async-start(bf16[64,16,1024]{2,1,0:T(8,128)(2,1)} %bitcast.68), calls=%async_computation.3 | async-start | bytes 4194304 | tf_op jit(solution)/shard_map/all_to_all | solution.py:23
  95.6 1.4 constant_dynamic-slice_fusion.1
  97.0 2.2 copy.62
  99.1 3.1 %collective-permute-start = (bf16[2,1024,128]{1,2,0:T(8,128)(2,1)}, bf16[2,1024,128]{1,2,0:T(8,128)(2,1)}, u32[]{:S(2)}, u32[]{:S(2)}) collective-permute-start(bf16[2,1024,128]{1,2,0:T(8,128)(2,1)} %bitcast.16), channel_id=1, source_target_pairs={{0,2},{2,4},{4,6},{6,0},{1,3},{3,5},{5,7},{7,1},{8,10},{10,12},{12... | collective-permute-start | bytes 1572872 | tf_op jit(solution)/shard_map/ppermute | solution.py:156
  102.2 2.1 copy.63
  104.3 2.6 collective-permute-start.1
  108.0 3.9 %collective-permute-start.2 = (bf16[2,1024,128]{1,2,0:T(8,128)(2,1)}, bf16[2,1024,128]{1,2,0:T(8,128)(2,1)}, u32[]{:S(2)}, u32[]{:S(2)}) collective-permute-start(bf16[2,1024,128]{1,2,0:T(8,128)(2,1)} %bitcast.20), channel_id=1, source_target_pairs={{0,6},{2,0},{4,2},{6,4},{1,7},{3,1},{5,3},{7,5},{8,14},{10,8},{12,... | collective-permute-start | bytes 1572872 | tf_op jit(solution)/shard_map/ppermute | solution.py:156
  114.1 16.0 %collective-permute-done = bf16[2,1024,128]{1,2,0:T(8,128)(2,1)} collective-permute-done((bf16[2,1024,128]{1,2,0:T(8,128)(2,1)}, bf16[2,1024,128]{1,2,0:T(8,128)(2,1)}, u32[]{:S(2)}, u32[]{:S(2)}) %collective-permute-start) | collective-permute-done | bytes 524320 | tf_op jit(solution)/shard_map/ppermute | solution.py:156
  132.7 9.4 %collective-permute-done.2 = bf16[2,1024,128]{1,2,0:T(8,128)(2,1)} collective-permute-done((bf16[2,1024,128]{1,2,0:T(8,128)(2,1)}, bf16[2,1024,128]{1,2,0:T(8,128)(2,1)}, u32[]{:S(2)}, u32[]{:S(2)}) %collective-permute-start.2) | collective-permute-done | bytes 524320 | tf_op jit(solution)/shard_map/ppermute | solution.py:156
  143.2 5.3 %convolution_convert_fusion.2 = bf16[1024,1024]{1,0:T(8,128)(2,1)} fusion(bf16[1024,1024]{1,0:T(8,128)(2,1)} %bitcast.13, bf16[1024,1024]{0,1:T(8,128)(2,1)S(1)} %bitcast.70), kind=kOutput, calls=%fused_computation.3 | convolution fusion | flops 2148532224 | bytes 6291456 | tf_op jit(solution)/shard_map/dot_general | solution.py:181
  148.5 6.4 %all-to-all-start.4 = ((bf16[4,256,1024]{2,1,0:T(8,128)(2,1)}), bf16[4,256,1024]{2,1,0:T(8,128)(2,1)S(1)}, u32[]{:S(2)}, u32[]{:S(2)}) async-start(bf16[4,256,1024]{2,1,0:T(8,128)(2,1)} %bitcast.71), calls=%async_computation.4 | async-start | bytes 4194304 | tf_op jit(solution)/shard_map/all_to_all | solution.py:23
  154.9 3.8 %collective-permute-start.3 = (bf16[4,128,512]{2,1,0:T(8,128)(2,1)}, bf16[4,128,512]{2,1,0:T(8,128)(2,1)}, u32[]{:S(2)}, u32[]{:S(2)}) collective-permute-start(bf16[4,128,512]{2,1,0:T(8,128)(2,1)} %get-tuple-element.8), channel_id=1, source_target_pairs={{0,1},{1,0},{2,3},{3,2},{4,5},{5,4},{6,7},{7,6},{8,9},{9,8},{10,11... | collective-permute-start | bytes 1572872 | tf_op jit(solution)/shard_map/ppermute | solution.py:178
  158.6 20.6 %all-to-all-done.4 = bf16[4,256,1024]{2,1,0:T(8,128)(2,1)S(1)} async-done(((bf16[4,256,1024]{2,1,0:T(8,128)(2,1)}), bf16[4,256,1024]{2,1,0:T(8,128)(2,1)S(1)}, u32[]{:S(2)}, u32[]{:S(2)}) %all-to-all-start.4) | async-done | bytes 2097184 | tf_op jit(solution)/shard_map/all_to_all | solution.py:23
  180.9 4.7 %all-to-all-start.5 = ((bf16[4,256,512]{2,1,0:T(8,128)(2,1)}), bf16[4,256,512]{2,1,0:T(8,128)(2,1)S(1)}, u32[]{:S(2)}, u32[]{:S(2)}) async-start(bf16[4,256,512]{2,1,0:T(8,128)(2,1)} %broadcast_in_dim.46), calls=%async_computation.5 | async-start | bytes 2097152 | tf_op jit(solution)/shard_map/all_to_all | solution.py:23
  185.5 19.5 %collective-permute-done.3 = bf16[4,128,512]{2,1,0:T(8,128)(2,1)} collective-permute-done((bf16[4,128,512]{2,1,0:T(8,128)(2,1)}, bf16[4,128,512]{2,1,0:T(8,128)(2,1)}, u32[]{:S(2)}, u32[]{:S(2)}) %collective-permute-start.3) | collective-permute-done | bytes 524320 | tf_op jit(solution)/shard_map/ppermute | solution.py:178
  205.1 1.9 bitcast_select_fusion.1
  207.0 3.6 %convolution_convert_fusion.1 = bf16[1024,1024]{1,0:T(8,128)(2,1)} fusion(bf16[1024,512]{1,0:T(8,128)(2,1)S(1)} %bitcast.74, bf16[512,512]{1,0:T(8,128)(2,1)} %get-tuple-element.16, bf16[512,512]{1,0:T(8,128)(2,1)S(1)} %get-tuple-element.15), kind=kOutput, calls=%fused_computation.2 | convolution fusion | flops 1076887552 | bytes 4194304 | tf_op jit(solution)/shard_map/dot_general | solution.py:193
  210.6 16.5 %all-to-all-start.6 = ((bf16[64,16,1024]{2,1,0:T(8,128)(2,1)}), bf16[64,16,1024]{2,1,0:T(8,128)(2,1)S(1)}, u32[]{:S(2)}, u32[]{:S(2)}) async-start(bf16[64,16,1024]{2,1,0:T(8,128)(2,1)} %bitcast.72), calls=%async_computation.6 | async-start | bytes 4194304 | tf_op jit(solution)/shard_map/all_to_all | solution.py:23
  228.4 26.0 %all-to-all-done.6 = bf16[64,16,1024]{2,1,0:T(8,128)(2,1)S(1)} async-done(((bf16[64,16,1024]{2,1,0:T(8,128)(2,1)}), bf16[64,16,1024]{2,1,0:T(8,128)(2,1)S(1)}, u32[]{:S(2)}, u32[]{:S(2)}) %all-to-all-start.6) | async-done | bytes 2097184 | tf_op jit(solution)/shard_map/all_to_all | solution.py:23
  254.4 1.3 copy-done.1
  255.8 4.2 %combine.1 = bf16[32,4096]{1,0:T(8,128)(2,1)} custom-call(bf16[32,128]{1,0:T(8,128)(2,1)} %slice.28.note_ref, bf16[2,4,128,1024]{3,2,1,0:T(8,128)(2,1)} %bitcast.69), custom_call_target="tpu_custom_call" | custom-call | tf_op jit(solution)/shard_map/combine/pallas_call | solution.py:104
  261.0 24.6 %all_to_all.40 = bf16[8,4,4096]{2,1,0:T(4,128)(2,1)S(1)} all-to-all(bf16[8,4,4096]{2,1,0:T(4,128)(2,1)S(1)} %reshape.103), channel_id=1, replica_groups=mesh['ab'=2,'am'=2,'al'=2,'y'=4,'core'=2,'hidden'=4,'pair'=2] {'pair','a..., dimensions={0} | all-to-all | bytes 524288 | tf_op jit(solution)/shard_map/all_to_all | solution.py:23
  (67 shorter events, 18.2 us)
Async XLA Ops:
  0.0 2.0 copy-start
  3.8 5.8 %copy-start.10 = (s32[1,4,2]{1,2,0:T(2,128)S(1)}, s32[1,4,2]{1,2,0:T(2,128)}, u32[]{:S(2)}) copy-start(s32[1,4,2]{1,2,0:T(2,128)} %param.18) | copy-start | bytes 100
  5.2 31.5 %copy-start.11 = (f32[1,4,2]{1,2,0:T(2,128)S(1)}, f32[1,4,2]{1,2,0:T(2,128)}, u32[]{:S(2)}) copy-start(f32[1,4,2]{1,2,0:T(2,128)} %param.17) | copy-start | bytes 100
  5.2 43.4 %copy-start.8 = (bf16[1,4,4096]{2,1,0:T(4,128)(2,1)S(1)}, bf16[1,4,4096]{2,1,0:T(4,128)(2,1)}, u32[]{:S(2)}) copy-start(bf16[1,4,4096]{2,1,0:T(4,128)(2,1)} %param.15) | copy-start | bytes 98308
  5.2 43.6 %copy-start.9 = (f32[4096]{0:T(1024)S(1)}, f32[4096]{0:T(1024)}, u32[]{:S(2)}) copy-start(f32[4096]{0:T(1024)} %param.16) | copy-start | bytes 49156
  5.2 13.0 %all-to-all-start = ((bf16[4,8,4,4096]{3,2,1,0:T(4,128)(2,1)}), bf16[4,8,4,4096]{3,2,1,0:T(4,128)(2,1)S(1)}, u32[]{:S(2)}, u32[]{:S(2)}) async-start(bf16[4,8,4,4096]{3,2,1,0:T(4,128)(2,1)} %bitcast.67), calls=%async_computation | async-start | bytes 2097152 | tf_op jit(solution)/shard_map/all_to_all | solution.py:23
  9.6 49.1 %copy-start.7 = (bf16[1,1024,512]{2,1,0:T(8,128)(2,1)S(1)}, bf16[1,1024,512]{2,1,0:T(8,128)(2,1)}, u32[]{:S(2)}) copy-start(bf16[1,1024,512]{2,1,0:T(8,128)(2,1)} %param.21) | copy-start | bytes 3145732
  19.6 28.7 %all-to-all-start.1 = ((bf16[8,4,4096]{2,1,0:T(4,128)(2,1)}), bf16[8,4,4096]{2,1,0:T(4,128)(2,1)S(1)}, u32[]{:S(2)}, u32[]{:S(2)}) async-start(bf16[8,4,4096]{2,1,0:T(4,128)(2,1)} %reduce_sum.83), calls=%async_computation.1 | async-start | bytes 524288 | tf_op jit(solution)/shard_map/all_to_all | solution.py:23
  49.7 24.6 %all-to-all-start.2 = ((bf16[8,4,4224]{2,1,0:T(4,128)(2,1)}), bf16[8,4,4224]{2,1,0:T(4,128)(2,1)S(1)}, u32[]{:S(2)}, u32[]{:S(2)}) async-start(bf16[8,4,4224]{2,1,0:T(4,128)(2,1)} %broadcast_in_dim.40), calls=%async_computation.2 | async-start | bytes 540672 | tf_op jit(solution)/shard_map/all_to_all | solution.py:23
  81.4 14.1 %copy-start.4 = (bf16[1,2,4096,128]{3,2,1,0:T(8,128)(2,1)S(1)}, bf16[1,2,4096,128]{3,2,1,0:T(8,128)(2,1)}, u32[]{:S(2)}) copy-start(bf16[1,2,4096,128]{3,2,1,0:T(8,128)(2,1)} %param.20) | copy-start | bytes 6291460
  81.4 61.8 %all-to-all-start.3 = ((bf16[64,16,1024]{2,1,0:T(8,128)(2,1)}), bf16[64,16,1024]{2,1,0:T(8,128)(2,1)}, u32[]{:S(2)}, u32[]{:S(2)}) async-start(bf16[64,16,1024]{2,1,0:T(8,128)(2,1)} %bitcast.68), calls=%async_computation.3 | async-start | bytes 4194304 | tf_op jit(solution)/shard_map/all_to_all | solution.py:23
  97.0 9.9 %copy-start.6 = (bf16[2,1,1024,128]{3,2,1,0:T(8,128)(2,1)S(1)}, bf16[2,1,1024,128]{3,2,1,0:T(8,128)(2,1)}, u32[]{:S(2)}) copy-start(bf16[2,1,1024,128]{3,2,1,0:T(8,128)(2,1)} %get-tuple-element.11) | copy-start | bytes 1572868
  97.0 14.9 %copy-start.5 = (bf16[2,1,1024,128]{3,2,1,0:T(8,128)(2,1)S(1)}, bf16[2,1,1024,128]{3,2,1,0:T(8,128)(2,1)}, u32[]{:S(2)}) copy-start(bf16[2,1,1024,128]{3,2,1,0:T(8,128)(2,1)} %get-tuple-element.14) | copy-start | bytes 1572868
  99.1 30.9 %collective-permute-start = (bf16[2,1024,128]{1,2,0:T(8,128)(2,1)}, bf16[2,1024,128]{1,2,0:T(8,128)(2,1)}, u32[]{:S(2)}, u32[]{:S(2)}) collective-permute-start(bf16[2,1024,128]{1,2,0:T(8,128)(2,1)} %bitcast.16), channel_id=1, source_target_pairs={{0,2},{2,4},{4,6},{6,0},{1,3},{3,5},{5,7},{7,1},{8,10},{10,12},{12... | collective-permute-start | bytes 1572872 | tf_op jit(solution)/shard_map/ppermute | solution.py:156
  104.3 27.3 %collective-permute-start.1 = (bf16[2,1024,128]{1,2,0:T(8,128)(2,1)}, bf16[2,1024,128]{1,2,0:T(8,128)(2,1)}, u32[]{:S(2)}, u32[]{:S(2)}) collective-permute-start(bf16[2,1024,128]{1,2,0:T(8,128)(2,1)} %bitcast.18), channel_id=1, source_target_pairs={{0,4},{2,6},{4,0},{6,2},{1,5},{3,7},{5,1},{7,3},{8,12},{10,14},{12... | collective-permute-start | bytes 1572872 | tf_op jit(solution)/shard_map/ppermute | solution.py:156
  108.0 34.1 %collective-permute-start.2 = (bf16[2,1024,128]{1,2,0:T(8,128)(2,1)}, bf16[2,1024,128]{1,2,0:T(8,128)(2,1)}, u32[]{:S(2)}, u32[]{:S(2)}) collective-permute-start(bf16[2,1024,128]{1,2,0:T(8,128)(2,1)} %bitcast.20), channel_id=1, source_target_pairs={{0,6},{2,0},{4,2},{6,4},{1,7},{3,1},{5,3},{7,5},{8,14},{10,8},{12,... | collective-permute-start | bytes 1572872 | tf_op jit(solution)/shard_map/ppermute | solution.py:156
  112.9 1.0 copy-start.3
  148.5 30.8 %all-to-all-start.4 = ((bf16[4,256,1024]{2,1,0:T(8,128)(2,1)}), bf16[4,256,1024]{2,1,0:T(8,128)(2,1)S(1)}, u32[]{:S(2)}, u32[]{:S(2)}) async-start(bf16[4,256,1024]{2,1,0:T(8,128)(2,1)} %bitcast.71), calls=%async_computation.4 | async-start | bytes 4194304 | tf_op jit(solution)/shard_map/all_to_all | solution.py:23
  154.9 50.2 %collective-permute-start.3 = (bf16[4,128,512]{2,1,0:T(8,128)(2,1)}, bf16[4,128,512]{2,1,0:T(8,128)(2,1)}, u32[]{:S(2)}, u32[]{:S(2)}) collective-permute-start(bf16[4,128,512]{2,1,0:T(8,128)(2,1)} %get-tuple-element.8), channel_id=1, source_target_pairs={{0,1},{1,0},{2,3},{3,2},{4,5},{5,4},{6,7},{7,6},{8,9},{9,8},{10,11... | collective-permute-start | bytes 1572872 | tf_op jit(solution)/shard_map/ppermute | solution.py:178
  179.6 25.4 %copy-start.2 = (bf16[4,1,128,512]{3,2,1,0:T(8,128)(2,1)S(1)}, bf16[4,1,128,512]{3,2,1,0:T(8,128)(2,1)}, u32[]{:S(2)}) copy-start(bf16[4,1,128,512]{3,2,1,0:T(8,128)(2,1)} %get-tuple-element.17) | copy-start | bytes 1572868
  180.9 26.1 %all-to-all-start.5 = ((bf16[4,256,512]{2,1,0:T(8,128)(2,1)}), bf16[4,256,512]{2,1,0:T(8,128)(2,1)S(1)}, u32[]{:S(2)}, u32[]{:S(2)}) async-start(bf16[4,256,512]{2,1,0:T(8,128)(2,1)} %broadcast_in_dim.46), calls=%async_computation.5 | async-start | bytes 2097152 | tf_op jit(solution)/shard_map/all_to_all | solution.py:23
  210.6 43.8 %all-to-all-start.6 = ((bf16[64,16,1024]{2,1,0:T(8,128)(2,1)}), bf16[64,16,1024]{2,1,0:T(8,128)(2,1)S(1)}, u32[]{:S(2)}, u32[]{:S(2)}) async-start(bf16[64,16,1024]{2,1,0:T(8,128)(2,1)} %bitcast.72), calls=%async_computation.6 | async-start | bytes 4194304 | tf_op jit(solution)/shard_map/all_to_all | solution.py:23
  254.4 1.3 copy-start.1

commit v6 on v5

--- a/solution.py
+++ b/solution.py
@@ -2,6 +2,7 @@
 import jax.numpy as jnp
 from jax import lax
 from jax.experimental import pallas as pl
+from jax.experimental.pallas import tpu as pltpu
 from jax.sharding import Mesh
 from jax.sharding import PartitionSpec as P
 
@@ -23,18 +24,44 @@
     return lax.all_to_all(value, axes, 0, 0, tiled=True)
 
 
-def attention(queries, keys, values, doc_lengths):
-    tok_group = queries.shape[0]
-    doc_ends = jnp.cumsum(doc_lengths)
-    positions = jnp.arange(tok_group, dtype=jnp.int32)
-    document = jnp.sum((positions[:, None] >= doc_ends[None, :]).astype(jnp.int32), axis=1)
-    allowed = (document[:, None] == document[None, :]) & (positions[None, :] <= positions[:, None])
-    scores = jnp.dot(queries, keys.T, preferred_element_type=F32) * HD ** (-0.5)
-    scores = jnp.where(allowed, scores, -1e30)
-    row_top = jnp.max(scores, axis=1, keepdims=True)
-    weights = jnp.exp(scores - row_top)
+def attention_kernel(doc_ref, queries_ref, keys_ref, values_ref, weight_ref, out_ref):
+    count = queries_ref.shape[0]
+    first_end = doc_ref[0]
+    second_end = first_end + doc_ref[1]
+    rows = lax.broadcasted_iota(jnp.int32, (count, count), 0)
+    cols = lax.broadcasted_iota(jnp.int32, (count, count), 1)
+    row_doc = (rows >= first_end).astype(jnp.int32) + (rows >= second_end).astype(jnp.int32)
+    col_doc = (cols >= first_end).astype(jnp.int32) + (cols >= second_end).astype(jnp.int32)
+    allowed = (row_doc == col_doc) & (cols <= rows)
+    scores = lax.dot_general(
+        queries_ref[...],
+        keys_ref[...],
+        (((1,), (1,)), ((), ())),
+        preferred_element_type=F32,
+    )
+    scores = jnp.where(allowed, scores * HD ** (-0.5), -1e30)
+    weights = jnp.exp(scores - jnp.max(scores, axis=1, keepdims=True))
     probabilities = (weights / jnp.sum(weights, axis=1, keepdims=True)).astype(BF16)
-    return jnp.dot(probabilities, values, preferred_element_type=F32).astype(BF16)
+    heads_out = jnp.dot(probabilities, values_ref[...], preferred_element_type=F32).astype(BF16)
+    total = jnp.dot(heads_out, weight_ref[...], preferred_element_type=F32)
+    parts, groups, owned, _ = out_ref.shape
+    places = parts // 2
+    for group in range(groups):
+        for part in range(parts):
+            start = ((group * 2 + part // places) * places + part % places) * owned
+            out_ref[part, group] = total[start : start + owned].astype(BF16)
+
+
+def attention(doc_lengths, queries, keys, values, out_weight, parts, owned):
+    count = queries.shape[0]
+    vmem = pl.BlockSpec(memory_space=pltpu.VMEM)
+    return pl.pallas_call(
+        attention_kernel,
+        in_specs=[pl.BlockSpec(memory_space=pltpu.SMEM), vmem, vmem, vmem, vmem],
+        out_specs=vmem,
+        out_shape=jax.ShapeDtypeStruct((parts, count // (parts * owned), owned, D), BF16),
+        name="attention",
+    )(doc_lengths, queries, keys, values, out_weight)
 
 
 def slot_numbers(chosen, place, places, capacity):
@@ -56,28 +83,29 @@
 
 def pick_kernel(tokens_ref, note_ref, out_ref):
     note = note_ref[...].astype(F32)
-    slots = lax.broadcasted_iota(jnp.int32, (note.shape[0], out_ref.shape[1]), 1).astype(F32)
+    slots = lax.broadcasted_iota(jnp.int32, (note.shape[0], out_ref.shape[2]), 1).astype(F32)
     taken = (slots == note[:, 0:1]) | (slots == note[:, 1:2])
-    out_ref[0] = lax.dot_general(
+    rows = lax.dot_general(
         jnp.where(taken, 1.0, 0.0).astype(BF16),
         tokens_ref[...],
         (((0,), (0,)), ((), ())),
         preferred_element_type=F32,
     ).astype(BF16)
+    for copy in range(out_ref.shape[0]):
+        out_ref[copy, 0] = rows
 
 
 def pick_rows(tokens, slots, chunk, copies):
     count = tokens.shape[0]
-    parts = D // chunk
     return pl.pallas_call(
         pick_kernel,
-        grid=(copies * parts,),
+        grid=(D // chunk,),
         in_specs=[
-            pl.BlockSpec((count, chunk), lambda j: (0, j % parts)),
+            pl.BlockSpec((count, chunk), lambda j: (0, j)),
             pl.BlockSpec((count, LANES), lambda j: (0, D // LANES)),
         ],
-        out_specs=pl.BlockSpec((1, slots, chunk), lambda j: (j, 0, 0)),
-        out_shape=jax.ShapeDtypeStruct((copies * parts, slots, chunk), BF16),
+        out_specs=pl.BlockSpec((copies, 1, slots, chunk), lambda j: (0, j, 0, 0)),
+        out_shape=jax.ShapeDtypeStruct((copies, D // chunk, slots, chunk), BF16),
         name="pick",
     )(tokens, tokens)
 
@@ -90,17 +118,20 @@
     weight = weight + jnp.where(slots == note[:, 1:2], 1.0 - share, 0.0)
     high = weight.astype(BF16)
     low = (weight - high.astype(F32)).astype(BF16)
-    total = jnp.zeros(out_ref.shape, F32)
+    both = jnp.concatenate([high, low], axis=0)
+    total = jnp.zeros((2 * note.shape[0], out_ref.shape[2]), F32)
     for k in range(rows_ref.shape[0]):
-        rows = rows_ref[k, 0]
-        total += jnp.dot(high, rows, preferred_element_type=F32)
-        total += jnp.dot(low, rows, preferred_element_type=F32)
-    out_ref[...] = total.astype(BF16)
-
-
-def combine_rows(note, rows):
+        total += jnp.dot(both, rows_ref[k, 0], preferred_element_type=F32)
+    total = total[: note.shape[0]] + total[note.shape[0] :]
+    places, owned, _ = out_ref.shape
+    for place in range(places):
+        out_ref[place] = total[place * owned : (place + 1) * owned].astype(BF16)
+
+
+def combine_rows(note, rows, owned):
     count = note.shape[0]
     sums, chunks, slots, chunk = rows.shape
+    places = count // owned
     return pl.pallas_call(
         combine_kernel,
         grid=(chunks,),
@@ -108,8 +139,8 @@
             pl.BlockSpec((count, LANES), lambda j: (0, 0)),
             pl.BlockSpec((sums, 1, slots, chunk), lambda j: (0, j, 0, 0)),
         ],
-        out_specs=pl.BlockSpec((count, chunk), lambda j: (0, j)),
-        out_shape=jax.ShapeDtypeStruct((count, chunks * chunk), BF16),
+        out_specs=pl.BlockSpec((places, owned, chunk), lambda j: (0, 0, j)),
+        out_shape=jax.ShapeDtypeStruct((places, owned, chunks * chunk), BF16),
         name="combine",
     )(note, rows)
 
@@ -129,6 +160,7 @@
 ):
     xs = lax.axis_size("hidden")
     zl = lax.axis_size(ATTN)
+    parities = lax.axis_size("al")
     pairs = lax.axis_size("pair")
     experts = lax.axis_size(("y", "core"))
     capacity = 2
@@ -141,12 +173,13 @@
     kept = lax.dynamic_index_in_dim(down, z_hi, 1, keepdims=False)
     sent = lax.dynamic_index_in_dim(down, 1 - z_hi, 1, keepdims=False)
 
-    heads_out = attention(queries[0], keys[0], values[0], doc_lengths[0])
-    tok_group = heads_out.shape[0]
+    tok_group = queries.shape[1]
     owned = tok_group // (zl * xs)
-    projected = jnp.dot(heads_out, out_weight, preferred_element_type=F32).astype(BF16)
-    projected = projected.reshape(zl, xs, owned, D).transpose(1, 0, 2, 3)
-    projected = jnp.sum(exchange(projected, "hidden").astype(F32), axis=0).astype(BF16)
+    projected = attention(
+        doc_lengths[0], queries[0], keys[0], values[0], out_weight, parities * xs, owned
+    )
+    projected = exchange(projected, ("al", "hidden"))
+    projected = jnp.sum(projected.astype(F32), axis=0).astype(BF16)
     gate_up = gate_up_weight[0].reshape(2, xs, chunk, unit)
     me = lax.axis_index("hidden")
     gathered = jnp.zeros((xs, 2, chunk, unit), BF16)
@@ -155,7 +188,7 @@
         if d > 0:
             block = lax.ppermute(block, "hidden", [(i, (i + d) % xs) for i in range(xs)])
         gathered = lax.dynamic_update_index_in_dim(gathered, block, (me - d) % xs, 0)
-    projected = jnp.sum(exchange(projected, ATTN).astype(F32), axis=0)
+    projected = jnp.sum(exchange(projected, ("ab", "am")).astype(F32), axis=0)
     gate_up = gathered.transpose(2, 1, 0, 3).reshape(chunk, 2 * xs * unit)
     attended = residual[0].astype(F32) + projected
     scale = lax.rsqrt(jnp.mean(attended * attended, axis=1, keepdims=True) + EPSILON)
@@ -172,7 +205,6 @@
     note = tokens[:, D:]
 
     group_slots = experts * places * capacity
-    parities = lax.axis_size("al")
     picked = pick_rows(tokens, group_slots, chunk, parities)
     picked, sent = lax.optimization_barrier((picked, sent))
     other = lax.ppermute(sent, "pair", [(0, 1), (1, 0)])
@@ -193,8 +225,10 @@
     out = jnp.dot(activated, down, preferred_element_type=F32).astype(BF16)
 
     returned = exchange(out.reshape(parities * xs * experts, -1, chunk), ROUTE)
-    returned = combine_rows(note, returned.reshape(parities, xs, group_slots, chunk))
-    mixed = exchange(returned.reshape(places, owned, D), Z_AXES)
+    returned = combine_rows(
+        note, returned.reshape(parities, xs, group_slots, chunk), owned
+    )
+    mixed = exchange(returned, Z_AXES)
     layer_out = attended + jnp.sum(mixed.astype(F32), axis=0)
     return layer_out.astype(BF16)[None]
 

time: 288 us -> 277 us (0.962)
  waiting for transfers between devices: 126 us -> 132 us
  starting transfers between devices: 85.1 us -> 79.3 us
  local copies, waits for them, and re-layouts: 21.9 us -> 17 us
  matrix products: 11.2 us -> 7.86 us
  other arithmetic: 6.52 us -> 3.26 us
    all_to_all x7, starting transfers between devices: 71.7 us -> 66.1 us  [exchange(): return lax.all_to_all(value, axes, 0, 0, tiled=True)]
    ppermute x1, waiting for transfers between devices: 19.5 us -> 23.9 us  [layer(): other = lax.ppermute(sent, 'pair', [(0, 1), (1, 0)])]
    reshape x3 -> x0, local copies, waits for them, and re-layouts: 2.88 us -> none  [the longest x2 1.83 us: layer(): projected = projected.reshape(zl, xs, owned, D).transpose(1, 0, 2, 3)]
    unnamed x31 -> x23, local copies, waits for them, and re-layouts: 8.75 us -> 7.05 us
    pallas_call x1 -> x2, Pallas kernels: 6.31 us -> 7.12 us  [the longest x1 3.97 us: pick_rows(): pl.pallas_call(pick_kernel, grid=(D // chunk,), in_specs=[pl.BlockSpec((c...]
  transfers between devices with their start and end apart: 11 -> 11, of which waited for: 9 -> 9; matrix products, arithmetic and copies ran while one was open for 6% -> 5% of each run, Pallas kernels for 0% -> 0%
where the time goes in v6:
time: 277 us; the launch traced here: 275 us
  waiting for transfers between devices  132 us (48%)
  starting transfers between devices  79.3 us (29%)
  blocking collectives  25 us (9%)
  local copies, waits for them, and re-layouts  17 us (6%)
  Pallas kernels  11.2 us (4%)
  matrix products  7.86 us (3%)
  other arithmetic  3.26 us (1%)
    all_to_all x7, waiting for transfers between devices, exchange(): return lax.all_to_all(value, axes, 0, 0, tiled=True)  79.9 us
    all_to_all x7, starting transfers between devices, exchange(): return lax.all_to_all(value, axes, 0, 0, tiled=True)  66.1 us
    ppermute x3, waiting for transfers between devices, layer(): lax.ppermute(block, 'hidden', [(i, (i + d) % xs) for i in range(xs)])  27.7 us
    all_to_all x1, blocking collectives, exchange(): return lax.all_to_all(value, axes, 0, 0, tiled=True)  25 us
    ppermute x1, waiting for transfers between devices, layer(): other = lax.ppermute(sent, 'pair', [(0, 1), (1, 0)])  23.9 us
    ppermute x3, starting transfers between devices, layer(): lax.ppermute(block, 'hidden', [(i, (i + d) % xs) for i in range(xs)])  9.6 us
    unnamed x23, local copies, waits for them, and re-layouts  7.05 us
  transfers between devices with their start and end apart: 11, of which 9 were waited for; matrix products, arithmetic and copies ran while one was open for 5% of the time, Pallas kernels for 0%

profile of v6, /device:TPU:3, one launch (start us, length us, event | category | flops | bytes accessed | tf_op | source)
XLA Modules:
  0.0 275.4 jit_solution(14443127382509985589)
XLA Ops:
  0.0 3.1 %attention.1 = bf16[8,4,4,4096]{3,2,1,0:T(4,128)(2,1)} custom-call(s32[2]{0:T(128)} %bitcast.64, bf16[128,128]{1,0:T(8,128)(2,1)} %bitcast.60, bf16[128,128]{1,0:T(8,128)(2,1)} %bitcast.61, bf16[128,128]{1,0:T(8,128)(2,1)} %bitcast.62, bf16[128,4096]{1,0:T(8,128)(2,1)} %weight_ref.1), custom_call_target="tpu_custom_call" | custom-call | tf_op jit(solution)/shard_map/attention/pallas_call | solution.py:58
  3.2 5.8 %all-to-all-start = ((bf16[8,4,4,4096]{3,2,1,0:T(4,128)(2,1)}), bf16[8,4,4,4096]{3,2,1,0:T(4,128)(2,1)S(1)}, u32[]{:S(2)}, u32[]{:S(2)}) async-start(bf16[8,4,4,4096]{3,2,1,0:T(4,128)(2,1)} %attention.1), calls=%async_computation | async-start | bytes 2097152 | tf_op jit(solution)/shard_map/all_to_all | solution.py:24
  9.7 10.0 %all-to-all-done = bf16[8,4,4,4096]{3,2,1,0:T(4,128)(2,1)S(1)} async-done(((bf16[8,4,4,4096]{3,2,1,0:T(4,128)(2,1)}), bf16[8,4,4,4096]{3,2,1,0:T(4,128)(2,1)S(1)}, u32[]{:S(2)}, u32[]{:S(2)}) %all-to-all-start) | async-done | bytes 1048608 | tf_op jit(solution)/shard_map/all_to_all | solution.py:24
  19.7 1.2 reduce_sum.63
  20.9 13.6 %all-to-all-start.1 = ((bf16[4,4,4096]{2,1,0:T(4,128)(2,1)}), bf16[4,4,4096]{2,1,0:T(4,128)(2,1)S(1)}, u32[]{:S(2)}, u32[]{:S(2)}) async-start(bf16[4,4,4096]{2,1,0:T(4,128)(2,1)} %reduce_sum.63), calls=%async_computation.1 | async-start | bytes 262144 | tf_op jit(solution)/shard_map/all_to_all | solution.py:24
  34.7 8.5 %all-to-all-done.1 = bf16[4,4,4096]{2,1,0:T(4,128)(2,1)S(1)} async-done(((bf16[4,4,4096]{2,1,0:T(4,128)(2,1)}), bf16[4,4,4096]{2,1,0:T(4,128)(2,1)S(1)}, u32[]{:S(2)}, u32[]{:S(2)}) %all-to-all-start.1) | async-done | bytes 131104 | tf_op jit(solution)/shard_map/all_to_all | solution.py:24
  44.4 7.3 %all-to-all-start.2 = ((bf16[8,4,4224]{2,1,0:T(4,128)(2,1)}), bf16[8,4,4224]{2,1,0:T(4,128)(2,1)S(1)}, u32[]{:S(2)}, u32[]{:S(2)}) async-start(bf16[8,4,4224]{2,1,0:T(4,128)(2,1)} %broadcast_in_dim.27), calls=%async_computation.2 | async-start | bytes 540672 | tf_op jit(solution)/shard_map/all_to_all | solution.py:24
  52.6 14.6 %all-to-all-done.2 = bf16[8,4,4224]{2,1,0:T(4,128)(2,1)S(1)} async-done(((bf16[8,4,4224]{2,1,0:T(4,128)(2,1)}), bf16[8,4,4224]{2,1,0:T(4,128)(2,1)S(1)}, u32[]{:S(2)}, u32[]{:S(2)}) %all-to-all-start.2) | async-done | bytes 270368 | tf_op jit(solution)/shard_map/all_to_all | solution.py:24
  68.0 4.0 %pick.1 = bf16[2,4,128,1024]{3,2,1,0:T(8,128)(2,1)} custom-call(bf16[32,4224]{1,0:T(8,128)(2,1)} %reshape.56.tokens_ref.note_ref, bf16[32,4224]{1,0:T(8,128)(2,1)} %reshape.56.tokens_ref.note_ref), custom_call_target="tpu_custom_call" | custom-call | tf_op jit(solution)/shard_map/pick/pallas_call | solution.py:100
  72.0 15.3 %all-to-all-start.3 = ((bf16[64,16,1024]{2,1,0:T(8,128)(2,1)}), bf16[64,16,1024]{2,1,0:T(8,128)(2,1)}, u32[]{:S(2)}, u32[]{:S(2)}) async-start(bf16[64,16,1024]{2,1,0:T(8,128)(2,1)} %bitcast.52), calls=%async_computation.3 | async-start | bytes 4194304 | tf_op jit(solution)/shard_map/all_to_all | solution.py:24
  87.4 1.2 constant_dynamic-slice_fusion.1
  88.6 2.1 copy.33
  90.7 3.1 %collective-permute-start = (bf16[2,1024,128]{1,2,0:T(8,128)(2,1)}, bf16[2,1024,128]{1,2,0:T(8,128)(2,1)}, u32[]{:S(2)}, u32[]{:S(2)}) collective-permute-start(bf16[2,1024,128]{1,2,0:T(8,128)(2,1)} %bitcast.14), channel_id=1, source_target_pairs={{0,2},{2,4},{4,6},{6,0},{1,3},{3,5},{5,7},{7,1},{8,10},{10,12},{12... | collective-permute-start | bytes 1572872 | tf_op jit(solution)/shard_map/ppermute | solution.py:189
  93.8 2.1 copy.34
  95.9 2.6 collective-permute-start.1
  99.5 3.9 %collective-permute-start.2 = (bf16[2,1024,128]{1,2,0:T(8,128)(2,1)}, bf16[2,1024,128]{1,2,0:T(8,128)(2,1)}, u32[]{:S(2)}, u32[]{:S(2)}) collective-permute-start(bf16[2,1024,128]{1,2,0:T(8,128)(2,1)} %bitcast.18), channel_id=1, source_target_pairs={{0,6},{2,0},{4,2},{6,4},{1,7},{3,1},{5,3},{7,5},{8,14},{10,8},{12,... | collective-permute-start | bytes 1572872 | tf_op jit(solution)/shard_map/ppermute | solution.py:189
  104.0 17.8 %collective-permute-done = bf16[2,1024,128]{1,2,0:T(8,128)(2,1)} collective-permute-done((bf16[2,1024,128]{1,2,0:T(8,128)(2,1)}, bf16[2,1024,128]{1,2,0:T(8,128)(2,1)}, u32[]{:S(2)}, u32[]{:S(2)}) %collective-permute-start) | collective-permute-done | bytes 524320 | tf_op jit(solution)/shard_map/ppermute | solution.py:189
  121.9 1.1 bitcast_dynamic-update-slice_fusion.2
  124.5 9.4 %collective-permute-done.2 = bf16[2,1024,128]{1,2,0:T(8,128)(2,1)} collective-permute-done((bf16[2,1024,128]{1,2,0:T(8,128)(2,1)}, bf16[2,1024,128]{1,2,0:T(8,128)(2,1)}, u32[]{:S(2)}, u32[]{:S(2)}) %collective-permute-start.2) | collective-permute-done | bytes 524320 | tf_op jit(solution)/shard_map/ppermute | solution.py:189
  135.0 5.3 %convolution_convert_fusion.1 = bf16[1024,1024]{1,0:T(8,128)(2,1)} fusion(bf16[1024,1024]{1,0:T(8,128)(2,1)} %bitcast.11, bf16[1024,1024]{0,1:T(8,128)(2,1)S(1)} %bitcast.54), kind=kOutput, calls=%fused_computation.2 | convolution fusion | flops 2148532224 | bytes 6291456 | tf_op jit(solution)/shard_map/dot_general | solution.py:213
  140.3 6.4 %all-to-all-start.4 = ((bf16[4,256,1024]{2,1,0:T(8,128)(2,1)}), bf16[4,256,1024]{2,1,0:T(8,128)(2,1)S(1)}, u32[]{:S(2)}, u32[]{:S(2)}) async-start(bf16[4,256,1024]{2,1,0:T(8,128)(2,1)} %bitcast.55), calls=%async_computation.4 | async-start | bytes 4194304 | tf_op jit(solution)/shard_map/all_to_all | solution.py:24
  146.7 3.6 %collective-permute-start.3 = (bf16[4,128,512]{2,1,0:T(8,128)(2,1)}, bf16[4,128,512]{2,1,0:T(8,128)(2,1)S(1)}, u32[]{:S(2)}, u32[]{:S(2)}) collective-permute-start(bf16[4,128,512]{2,1,0:T(8,128)(2,1)} %get-tuple-element.8), channel_id=1, source_target_pairs={{0,1},{1,0},{2,3},{3,2},{4,5},{5,4},{6,7},{7,6},{8,9},{9,8},{10,11... | collective-permute-start | bytes 1572872 | tf_op jit(solution)/shard_map/ppermute | solution.py:210
  150.3 20.7 %all-to-all-done.4 = bf16[4,256,1024]{2,1,0:T(8,128)(2,1)S(1)} async-done(((bf16[4,256,1024]{2,1,0:T(8,128)(2,1)}), bf16[4,256,1024]{2,1,0:T(8,128)(2,1)S(1)}, u32[]{:S(2)}, u32[]{:S(2)}) %all-to-all-start.4) | async-done | bytes 2097184 | tf_op jit(solution)/shard_map/all_to_all | solution.py:24
  172.6 4.7 %all-to-all-start.5 = ((bf16[4,256,512]{2,1,0:T(8,128)(2,1)}), bf16[4,256,512]{2,1,0:T(8,128)(2,1)S(1)}, u32[]{:S(2)}, u32[]{:S(2)}) async-start(bf16[4,256,512]{2,1,0:T(8,128)(2,1)} %broadcast_in_dim.33), calls=%async_computation.5 | async-start | bytes 2097152 | tf_op jit(solution)/shard_map/all_to_all | solution.py:24
  177.2 23.9 %collective-permute-done.3 = bf16[4,128,512]{2,1,0:T(8,128)(2,1)S(1)} collective-permute-done((bf16[4,128,512]{2,1,0:T(8,128)(2,1)}, bf16[4,128,512]{2,1,0:T(8,128)(2,1)S(1)}, u32[]{:S(2)}, u32[]{:S(2)}) %collective-permute-start.3) | collective-permute-done | bytes 524320 | tf_op jit(solution)/shard_map/ppermute | solution.py:210
  201.2 2.6 convolution_convert_fusion
  203.8 13.1 %all-to-all-start.6 = ((bf16[64,16,1024]{2,1,0:T(8,128)(2,1)}), bf16[64,16,1024]{2,1,0:T(8,128)(2,1)S(1)}, u32[]{:S(2)}, u32[]{:S(2)}) async-start(bf16[64,16,1024]{2,1,0:T(8,128)(2,1)} %bitcast.56), calls=%async_computation.6 | async-start | bytes 4194304 | tf_op jit(solution)/shard_map/all_to_all | solution.py:24
  216.9 1.3 slice.28.note_ref
  218.2 26.1 %all-to-all-done.6 = bf16[64,16,1024]{2,1,0:T(8,128)(2,1)S(1)} async-done(((bf16[64,16,1024]{2,1,0:T(8,128)(2,1)}), bf16[64,16,1024]{2,1,0:T(8,128)(2,1)S(1)}, u32[]{:S(2)}, u32[]{:S(2)}) %all-to-all-start.6) | async-done | bytes 2097184 | tf_op jit(solution)/shard_map/all_to_all | solution.py:24
  244.3 1.3 copy-done
  245.6 4.1 %combine.1 = bf16[8,4,4096]{2,1,0:T(4,128)(2,1)} custom-call(bf16[32,128]{1,0:T(8,128)(2,1)} %slice.28.note_ref, bf16[2,4,128,1024]{3,2,1,0:T(8,128)(2,1)} %bitcast.53), custom_call_target="tpu_custom_call" | custom-call | tf_op jit(solution)/shard_map/combine/pallas_call | solution.py:135
  249.7 25.0 %all_to_all.40 = bf16[8,4,4096]{2,1,0:T(4,128)(2,1)S(1)} all-to-all(bf16[8,4,4096]{2,1,0:T(4,128)(2,1)} %combine.1), channel_id=1, replica_groups=mesh['ab'=2,'am'=2,'al'=2,'y'=4,'core'=2,'hidden'=4,'pair'=2] {'pair','a..., dimensions={0} | all-to-all | bytes 524288 | tf_op jit(solution)/shard_map/all_to_all | solution.py:24
  (52 shorter events, 10.4 us)
Async XLA Ops:
  0.0 8.9 %copy-start.6 = (s32[1,4,2]{1,2,0:T(2,128)S(1)}, s32[1,4,2]{1,2,0:T(2,128)}, u32[]{:S(2)}) copy-start(s32[1,4,2]{1,2,0:T(2,128)} %param.18) | copy-start | bytes 100
  0.0 9.5 %copy-start.7 = (f32[1,4,2]{1,2,0:T(2,128)S(1)}, f32[1,4,2]{1,2,0:T(2,128)}, u32[]{:S(2)}) copy-start(f32[1,4,2]{1,2,0:T(2,128)} %param.17) | copy-start | bytes 100
  3.2 40.1 %copy-start.4 = (bf16[1,4,4096]{2,1,0:T(4,128)(2,1)S(1)}, bf16[1,4,4096]{2,1,0:T(4,128)(2,1)}, u32[]{:S(2)}) copy-start(bf16[1,4,4096]{2,1,0:T(4,128)(2,1)} %param.15) | copy-start | bytes 98308
  3.2 40.3 %copy-start.5 = (f32[4096]{0:T(1024)S(1)}, f32[4096]{0:T(1024)}, u32[]{:S(2)}) copy-start(f32[4096]{0:T(1024)} %param.16) | copy-start | bytes 49156
  3.2 48.5 %copy-start.3 = (bf16[1,1024,512]{2,1,0:T(8,128)(2,1)S(1)}, bf16[1,1024,512]{2,1,0:T(8,128)(2,1)}, u32[]{:S(2)}) copy-start(bf16[1,1024,512]{2,1,0:T(8,128)(2,1)} %param.21) | copy-start | bytes 3145732
  3.2 16.5 %all-to-all-start = ((bf16[8,4,4,4096]{3,2,1,0:T(4,128)(2,1)}), bf16[8,4,4,4096]{3,2,1,0:T(4,128)(2,1)S(1)}, u32[]{:S(2)}, u32[]{:S(2)}) async-start(bf16[8,4,4,4096]{3,2,1,0:T(4,128)(2,1)} %attention.1), calls=%async_computation | async-start | bytes 2097152 | tf_op jit(solution)/shard_map/all_to_all | solution.py:24
  20.9 22.3 %all-to-all-start.1 = ((bf16[4,4,4096]{2,1,0:T(4,128)(2,1)}), bf16[4,4,4096]{2,1,0:T(4,128)(2,1)S(1)}, u32[]{:S(2)}, u32[]{:S(2)}) async-start(bf16[4,4,4096]{2,1,0:T(4,128)(2,1)} %reduce_sum.63), calls=%async_computation.1 | async-start | bytes 262144 | tf_op jit(solution)/shard_map/all_to_all | solution.py:24
  44.4 22.9 %all-to-all-start.2 = ((bf16[8,4,4224]{2,1,0:T(4,128)(2,1)}), bf16[8,4,4224]{2,1,0:T(4,128)(2,1)S(1)}, u32[]{:S(2)}, u32[]{:S(2)}) async-start(bf16[8,4,4224]{2,1,0:T(4,128)(2,1)} %broadcast_in_dim.27), calls=%async_computation.2 | async-start | bytes 540672 | tf_op jit(solution)/shard_map/all_to_all | solution.py:24
  72.0 15.4 %copy-start.1 = (bf16[1,2,4096,128]{3,2,1,0:T(8,128)(2,1)S(1)}, bf16[1,2,4096,128]{3,2,1,0:T(8,128)(2,1)}, u32[]{:S(2)}) copy-start(bf16[1,2,4096,128]{3,2,1,0:T(8,128)(2,1)} %param.20) | copy-start | bytes 6291460
  72.0 63.0 %all-to-all-start.3 = ((bf16[64,16,1024]{2,1,0:T(8,128)(2,1)}), bf16[64,16,1024]{2,1,0:T(8,128)(2,1)}, u32[]{:S(2)}, u32[]{:S(2)}) async-start(bf16[64,16,1024]{2,1,0:T(8,128)(2,1)} %bitcast.52), calls=%async_computation.3 | async-start | bytes 4194304 | tf_op jit(solution)/shard_map/all_to_all | solution.py:24
  88.6 14.8 %copy-start.2 = (bf16[2,1,1024,128]{3,2,1,0:T(8,128)(2,1)S(1)}, bf16[2,1,1024,128]{3,2,1,0:T(8,128)(2,1)}, u32[]{:S(2)}) copy-start(bf16[2,1,1024,128]{3,2,1,0:T(8,128)(2,1)} %get-tuple-element.14) | copy-start | bytes 1572868
  90.7 31.1 %collective-permute-start = (bf16[2,1024,128]{1,2,0:T(8,128)(2,1)}, bf16[2,1024,128]{1,2,0:T(8,128)(2,1)}, u32[]{:S(2)}, u32[]{:S(2)}) collective-permute-start(bf16[2,1024,128]{1,2,0:T(8,128)(2,1)} %bitcast.14), channel_id=1, source_target_pairs={{0,2},{2,4},{4,6},{6,0},{1,3},{3,5},{5,7},{7,1},{8,10},{10,12},{12... | collective-permute-start | bytes 1572872 | tf_op jit(solution)/shard_map/ppermute | solution.py:189
  95.9 27.6 %collective-permute-start.1 = (bf16[2,1024,128]{1,2,0:T(8,128)(2,1)}, bf16[2,1024,128]{1,2,0:T(8,128)(2,1)}, u32[]{:S(2)}, u32[]{:S(2)}) collective-permute-start(bf16[2,1024,128]{1,2,0:T(8,128)(2,1)} %bitcast.16), channel_id=1, source_target_pairs={{0,4},{2,6},{4,0},{6,2},{1,5},{3,7},{5,1},{7,3},{8,12},{10,14},{12... | collective-permute-start | bytes 1572872 | tf_op jit(solution)/shard_map/ppermute | solution.py:189
  99.5 34.4 %collective-permute-start.2 = (bf16[2,1024,128]{1,2,0:T(8,128)(2,1)}, bf16[2,1024,128]{1,2,0:T(8,128)(2,1)}, u32[]{:S(2)}, u32[]{:S(2)}) collective-permute-start(bf16[2,1024,128]{1,2,0:T(8,128)(2,1)} %bitcast.18), channel_id=1, source_target_pairs={{0,6},{2,0},{4,2},{6,4},{1,7},{3,1},{5,3},{7,5},{8,14},{10,8},{12,... | collective-permute-start | bytes 1572872 | tf_op jit(solution)/shard_map/ppermute | solution.py:189
  140.3 30.7 %all-to-all-start.4 = ((bf16[4,256,1024]{2,1,0:T(8,128)(2,1)}), bf16[4,256,1024]{2,1,0:T(8,128)(2,1)S(1)}, u32[]{:S(2)}, u32[]{:S(2)}) async-start(bf16[4,256,1024]{2,1,0:T(8,128)(2,1)} %bitcast.55), calls=%async_computation.4 | async-start | bytes 4194304 | tf_op jit(solution)/shard_map/all_to_all | solution.py:24
  146.7 54.4 %collective-permute-start.3 = (bf16[4,128,512]{2,1,0:T(8,128)(2,1)}, bf16[4,128,512]{2,1,0:T(8,128)(2,1)S(1)}, u32[]{:S(2)}, u32[]{:S(2)}) collective-permute-start(bf16[4,128,512]{2,1,0:T(8,128)(2,1)} %get-tuple-element.8), channel_id=1, source_target_pairs={{0,1},{1,0},{2,3},{3,2},{4,5},{5,4},{6,7},{7,6},{8,9},{9,8},{10,11... | collective-permute-start | bytes 1572872 | tf_op jit(solution)/shard_map/ppermute | solution.py:210
  172.6 28.7 %all-to-all-start.5 = ((bf16[4,256,512]{2,1,0:T(8,128)(2,1)}), bf16[4,256,512]{2,1,0:T(8,128)(2,1)S(1)}, u32[]{:S(2)}, u32[]{:S(2)}) async-start(bf16[4,256,512]{2,1,0:T(8,128)(2,1)} %broadcast_in_dim.33), calls=%async_computation.5 | async-start | bytes 2097152 | tf_op jit(solution)/shard_map/all_to_all | solution.py:24
  203.8 40.4 %all-to-all-start.6 = ((bf16[64,16,1024]{2,1,0:T(8,128)(2,1)}), bf16[64,16,1024]{2,1,0:T(8,128)(2,1)S(1)}, u32[]{:S(2)}, u32[]{:S(2)}) async-start(bf16[64,16,1024]{2,1,0:T(8,128)(2,1)} %bitcast.56), calls=%async_computation.6 | async-start | bytes 4194304 | tf_op jit(solution)/shard_map/all_to_all | solution.py:24
  244.3 1.3 copy-start

commit v7 on v6

--- a/solution.py
+++ b/solution.py
@@ -81,13 +81,17 @@
     return jnp.pad(parts, ((0, 0), (0, LANES - 5))).astype(BF16)
 
 
+def stacked(ref):
+    return jnp.concatenate([ref[k].astype(F32) for k in range(ref.shape[0])], axis=0)
+
+
 def pick_kernel(tokens_ref, note_ref, out_ref):
-    note = note_ref[...].astype(F32)
+    note = stacked(note_ref)
     slots = lax.broadcasted_iota(jnp.int32, (note.shape[0], out_ref.shape[2]), 1).astype(F32)
     taken = (slots == note[:, 0:1]) | (slots == note[:, 1:2])
     rows = lax.dot_general(
         jnp.where(taken, 1.0, 0.0).astype(BF16),
-        tokens_ref[...],
+        stacked(tokens_ref).astype(BF16),
         (((0,), (0,)), ((), ())),
         preferred_element_type=F32,
     ).astype(BF16)
@@ -96,13 +100,13 @@
 
 
 def pick_rows(tokens, slots, chunk, copies):
-    count = tokens.shape[0]
+    places, owned, _ = tokens.shape
     return pl.pallas_call(
         pick_kernel,
         grid=(D // chunk,),
         in_specs=[
-            pl.BlockSpec((count, chunk), lambda j: (0, j)),
-            pl.BlockSpec((count, LANES), lambda j: (0, D // LANES)),
+            pl.BlockSpec((places, owned, chunk), lambda j: (0, 0, j)),
+            pl.BlockSpec((places, owned, LANES), lambda j: (0, 0, D // LANES)),
         ],
         out_specs=pl.BlockSpec((copies, 1, slots, chunk), lambda j: (0, j, 0, 0)),
         out_shape=jax.ShapeDtypeStruct((copies, D // chunk, slots, chunk), BF16),
@@ -111,7 +115,7 @@
 
 
 def combine_kernel(note_ref, rows_ref, out_ref):
-    note = note_ref[...].astype(F32)
+    note = stacked(note_ref)
     share = note[:, 2:3] + note[:, 3:4] + note[:, 4:5]
     slots = lax.broadcasted_iota(jnp.int32, (note.shape[0], rows_ref.shape[2]), 1).astype(F32)
     weight = jnp.where(slots == note[:, 0:1], share, 0.0)
@@ -128,21 +132,20 @@
         out_ref[place] = total[place * owned : (place + 1) * owned].astype(BF16)
 
 
-def combine_rows(note, rows, owned):
-    count = note.shape[0]
+def combine_rows(tokens, rows):
+    places, owned, _ = tokens.shape
     sums, chunks, slots, chunk = rows.shape
-    places = count // owned
     return pl.pallas_call(
         combine_kernel,
         grid=(chunks,),
         in_specs=[
-            pl.BlockSpec((count, LANES), lambda j: (0, 0)),
+            pl.BlockSpec((places, owned, LANES), lambda j: (0, 0, D // LANES)),
             pl.BlockSpec((sums, 1, slots, chunk), lambda j: (0, j, 0, 0)),
         ],
         out_specs=pl.BlockSpec((places, owned, chunk), lambda j: (0, 0, j)),
         out_shape=jax.ShapeDtypeStruct((places, owned, chunks * chunk), BF16),
         name="combine",
-    )(note, rows)
+    )(tokens, rows)
 
 
 def layer(
@@ -201,8 +204,6 @@
     note = note_of(slots, jax.nn.sigmoid(logits[:, 0] - logits[:, 1]))
     noted = jnp.concatenate([normed, note], axis=1)
     tokens = exchange(jnp.broadcast_to(noted, (places, *noted.shape)), Z_AXES)
-    tokens = tokens.reshape(places * owned, D + LANES)
-    note = tokens[:, D:]
 
     group_slots = experts * places * capacity
     picked = pick_rows(tokens, group_slots, chunk, parities)
@@ -225,9 +226,7 @@
     out = jnp.dot(activated, down, preferred_element_type=F32).astype(BF16)
 
     returned = exchange(out.reshape(parities * xs * experts, -1, chunk), ROUTE)
-    returned = combine_rows(
-        note, returned.reshape(parities, xs, group_slots, chunk), owned
-    )
+    returned = combine_rows(tokens, returned.reshape(parities, xs, group_slots, chunk))
     mixed = exchange(returned, Z_AXES)
     layer_out = attended + jnp.sum(mixed.astype(F32), axis=0)
     return layer_out.astype(BF16)[None]

time: 277 us -> 274 us (0.989)
  blocking collectives: 25 us -> 63.1 us
  waiting for transfers between devices: 132 us -> 108 us
  starting transfers between devices: 79.3 us -> 66.2 us
    all_to_all x1 -> x2, blocking collectives: 25 us -> 63.1 us  [exchange(): return lax.all_to_all(value, axes, 0, 0, tiled=True)]
    all_to_all x7 -> x6, waiting for transfers between devices: 79.9 us -> 53.9 us  [exchange(): return lax.all_to_all(value, axes, 0, 0, tiled=True)]
    all_to_all x7 -> x6, starting transfers between devices: 66.1 us -> 53.1 us  [exchange(): return lax.all_to_all(value, axes, 0, 0, tiled=True)]
  transfers between devices with their start and end apart: 11 -> 10, of which waited for: 9 -> 8; matrix products, arithmetic and copies ran while one was open for 5% -> 5% of each run, Pallas kernels for 0% -> 0%
where the time goes in v7:
time: 274 us; the launch traced here: 273 us
  waiting for transfers between devices  108 us (39%)
  starting transfers between devices  66.2 us (24%)
  blocking collectives  63.1 us (23%)
  local copies, waits for them, and re-layouts  14.3 us (5%)
  Pallas kernels  11.2 us (4%)
  matrix products  6.52 us (2%)
  other arithmetic  3.25 us (1%)
    all_to_all x2, blocking collectives, exchange(): return lax.all_to_all(value, axes, 0, 0, tiled=True)  63.1 us
    all_to_all x6, waiting for transfers between devices, exchange(): return lax.all_to_all(value, axes, 0, 0, tiled=True)  53.9 us
    all_to_all x6, starting transfers between devices, exchange(): return lax.all_to_all(value, axes, 0, 0, tiled=True)  53.1 us
    ppermute x3, waiting for transfers between devices, layer(): lax.ppermute(block, 'hidden', [(i, (i + d) % xs) for i in range(xs)])  27.8 us
    ppermute x1, waiting for transfers between devices, layer(): other = lax.ppermute(sent, 'pair', [(0, 1), (1, 0)])  26.1 us
    ppermute x3, starting transfers between devices, layer(): lax.ppermute(block, 'hidden', [(i, (i + d) % xs) for i in range(xs)])  9.6 us
    unnamed x23, local copies, waits for them, and re-layouts  6.44 us
  transfers between devices with their start and end apart: 10, of which 8 were waited for; matrix products, arithmetic and copies ran while one was open for 5% of the time, Pallas kernels for 0%

profile of v7, /device:TPU:3, one launch (start us, length us, event | category | flops | bytes accessed | tf_op | source)
XLA Modules:
  0.0 272.6 jit_solution(1336718816690130925)
XLA Ops:
  0.0 3.1 %attention.1 = bf16[8,4,4,4096]{3,2,1,0:T(4,128)(2,1)} custom-call(s32[2]{0:T(128)} %bitcast.64, bf16[128,128]{1,0:T(8,128)(2,1)} %bitcast.60, bf16[128,128]{1,0:T(8,128)(2,1)} %bitcast.61, bf16[128,128]{1,0:T(8,128)(2,1)} %bitcast.62, bf16[128,4096]{1,0:T(8,128)(2,1)} %weight_ref.1), custom_call_target="tpu_custom_call" | custom-call | tf_op jit(solution)/shard_map/attention/pallas_call | solution.py:58
  3.2 5.8 %all-to-all-start = ((bf16[8,4,4,4096]{3,2,1,0:T(4,128)(2,1)}), bf16[8,4,4,4096]{3,2,1,0:T(4,128)(2,1)S(1)}, u32[]{:S(2)}, u32[]{:S(2)}) async-start(bf16[8,4,4,4096]{3,2,1,0:T(4,128)(2,1)} %attention.1), calls=%async_computation | async-start | bytes 2097152 | tf_op jit(solution)/shard_map/all_to_all | solution.py:24
  9.7 10.0 %all-to-all-done = bf16[8,4,4,4096]{3,2,1,0:T(4,128)(2,1)S(1)} async-done(((bf16[8,4,4,4096]{3,2,1,0:T(4,128)(2,1)}), bf16[8,4,4,4096]{3,2,1,0:T(4,128)(2,1)S(1)}, u32[]{:S(2)}, u32[]{:S(2)}) %all-to-all-start) | async-done | bytes 1048608 | tf_op jit(solution)/shard_map/all_to_all | solution.py:24
  19.7 1.2 reduce_sum.63
  20.9 13.6 %all-to-all-start.1 = ((bf16[4,4,4096]{2,1,0:T(4,128)(2,1)}), bf16[4,4,4096]{2,1,0:T(4,128)(2,1)S(1)}, u32[]{:S(2)}, u32[]{:S(2)}) async-start(bf16[4,4,4096]{2,1,0:T(4,128)(2,1)} %reduce_sum.63), calls=%async_computation.1 | async-start | bytes 262144 | tf_op jit(solution)/shard_map/all_to_all | solution.py:24
  34.7 8.5 %all-to-all-done.1 = bf16[4,4,4096]{2,1,0:T(4,128)(2,1)S(1)} async-done(((bf16[4,4,4096]{2,1,0:T(4,128)(2,1)}), bf16[4,4,4096]{2,1,0:T(4,128)(2,1)S(1)}, u32[]{:S(2)}, u32[]{:S(2)}) %all-to-all-start.1) | async-done | bytes 131104 | tf_op jit(solution)/shard_map/all_to_all | solution.py:24
  44.3 7.3 %all-to-all-start.2 = ((bf16[8,4,4224]{2,1,0:T(4,128)(2,1)}), bf16[8,4,4224]{2,1,0:T(4,128)(2,1)S(1)}, u32[]{:S(2)}, u32[]{:S(2)}) async-start(bf16[8,4,4224]{2,1,0:T(4,128)(2,1)} %broadcast_in_dim.27), calls=%async_computation.2 | async-start | bytes 540672 | tf_op jit(solution)/shard_map/all_to_all | solution.py:24
  52.6 14.6 %all-to-all-done.2.tokens_ref.note_ref = bf16[8,4,4224]{2,1,0:T(4,128)(2,1)S(1)} async-done(((bf16[8,4,4224]{2,1,0:T(4,128)(2,1)}), bf16[8,4,4224]{2,1,0:T(4,128)(2,1)S(1)}, u32[]{:S(2)}, u32[]{:S(2)}) %all-to-all-start.2) | async-done | bytes 270368 | tf_op jit(solution)/shard_map/all_to_all | solution.py:24
  67.9 3.9 %pick.1 = bf16[2,4,128,1024]{3,2,1,0:T(8,128)(2,1)} custom-call(bf16[8,4,4224]{2,1,0:T(4,128)(2,1)} %copy-done, bf16[8,4,4224]{2,1,0:T(4,128)(2,1)} %copy-done), custom_call_target="tpu_custom_call" | custom-call | tf_op jit(solution)/shard_map/pick/pallas_call | solution.py:104
  71.9 15.3 %all-to-all-start.3 = ((bf16[64,16,1024]{2,1,0:T(8,128)(2,1)}), bf16[64,16,1024]{2,1,0:T(8,128)(2,1)}, u32[]{:S(2)}, u32[]{:S(2)}) async-start(bf16[64,16,1024]{2,1,0:T(8,128)(2,1)} %bitcast.52), calls=%async_computation.3 | async-start | bytes 4194304 | tf_op jit(solution)/shard_map/all_to_all | solution.py:24
  87.3 1.2 constant_dynamic-slice_fusion.1
  88.5 2.1 copy.33
  90.6 3.1 %collective-permute-start = (bf16[2,1024,128]{1,2,0:T(8,128)(2,1)}, bf16[2,1024,128]{1,2,0:T(8,128)(2,1)}, u32[]{:S(2)}, u32[]{:S(2)}) collective-permute-start(bf16[2,1024,128]{1,2,0:T(8,128)(2,1)} %bitcast.14), channel_id=1, source_target_pairs={{0,2},{2,4},{4,6},{6,0},{1,3},{3,5},{5,7},{7,1},{8,10},{10,12},{12... | collective-permute-start | bytes 1572872 | tf_op jit(solution)/shard_map/ppermute | solution.py:192
  93.7 2.0 copy.34
  95.7 2.6 collective-permute-start.1
  99.4 3.9 %collective-permute-start.2 = (bf16[2,1024,128]{1,2,0:T(8,128)(2,1)}, bf16[2,1024,128]{1,2,0:T(8,128)(2,1)}, u32[]{:S(2)}, u32[]{:S(2)}) collective-permute-start(bf16[2,1024,128]{1,2,0:T(8,128)(2,1)} %bitcast.18), channel_id=1, source_target_pairs={{0,6},{2,0},{4,2},{6,4},{1,7},{3,1},{5,3},{7,5},{8,14},{10,8},{12,... | collective-permute-start | bytes 1572872 | tf_op jit(solution)/shard_map/ppermute | solution.py:192
  103.9 17.9 %collective-permute-done = bf16[2,1024,128]{1,2,0:T(8,128)(2,1)} collective-permute-done((bf16[2,1024,128]{1,2,0:T(8,128)(2,1)}, bf16[2,1024,128]{1,2,0:T(8,128)(2,1)}, u32[]{:S(2)}, u32[]{:S(2)}) %collective-permute-start) | collective-permute-done | bytes 524320 | tf_op jit(solution)/shard_map/ppermute | solution.py:192
  121.8 1.1 bitcast_dynamic-update-slice_fusion.2
  123.3 1.1 bitcast_dynamic-update-slice_fusion.1
  124.4 9.4 %collective-permute-done.2 = bf16[2,1024,128]{1,2,0:T(8,128)(2,1)} collective-permute-done((bf16[2,1024,128]{1,2,0:T(8,128)(2,1)}, bf16[2,1024,128]{1,2,0:T(8,128)(2,1)}, u32[]{:S(2)}, u32[]{:S(2)}) %collective-permute-start.2) | collective-permute-done | bytes 524320 | tf_op jit(solution)/shard_map/ppermute | solution.py:192
  133.8 1.1 bitcast_dynamic-update-slice_fusion
  134.9 5.3 %convolution_convert_fusion.1 = bf16[1024,1024]{1,0:T(8,128)(2,1)} fusion(bf16[1024,1024]{1,0:T(8,128)(2,1)} %bitcast.11, bf16[1024,1024]{0,1:T(8,128)(2,1)S(1)} %bitcast.54), kind=kOutput, calls=%fused_computation.2 | convolution fusion | flops 2148532224 | bytes 6291456 | tf_op jit(solution)/shard_map/dot_general | solution.py:214
  140.2 6.4 %all-to-all-start.4 = ((bf16[4,256,1024]{2,1,0:T(8,128)(2,1)}), bf16[4,256,1024]{2,1,0:T(8,128)(2,1)S(1)}, u32[]{:S(2)}, u32[]{:S(2)}) async-start(bf16[4,256,1024]{2,1,0:T(8,128)(2,1)} %bitcast.55), calls=%async_computation.4 | async-start | bytes 4194304 | tf_op jit(solution)/shard_map/all_to_all | solution.py:24
  146.6 3.6 %collective-permute-start.3 = (bf16[4,128,512]{2,1,0:T(8,128)(2,1)}, bf16[4,128,512]{2,1,0:T(8,128)(2,1)S(1)}, u32[]{:S(2)}, u32[]{:S(2)}) collective-permute-start(bf16[4,128,512]{2,1,0:T(8,128)(2,1)} %get-tuple-element.8), channel_id=1, source_target_pairs={{0,1},{1,0},{2,3},{3,2},{4,5},{5,4},{6,7},{7,6},{8,9},{9,8},{10,11... | collective-permute-start | bytes 1572872 | tf_op jit(solution)/shard_map/ppermute | solution.py:211
  150.2 20.7 %all-to-all-done.4 = bf16[4,256,1024]{2,1,0:T(8,128)(2,1)S(1)} async-done(((bf16[4,256,1024]{2,1,0:T(8,128)(2,1)}), bf16[4,256,1024]{2,1,0:T(8,128)(2,1)S(1)}, u32[]{:S(2)}, u32[]{:S(2)}) %all-to-all-start.4) | async-done | bytes 2097184 | tf_op jit(solution)/shard_map/all_to_all | solution.py:24
  171.4 1.1 broadcast_in_dim.33
  172.5 4.7 %all-to-all-start.5 = ((bf16[4,256,512]{2,1,0:T(8,128)(2,1)}), bf16[4,256,512]{2,1,0:T(8,128)(2,1)S(1)}, u32[]{:S(2)}, u32[]{:S(2)}) async-start(bf16[4,256,512]{2,1,0:T(8,128)(2,1)} %broadcast_in_dim.33), calls=%async_computation.5 | async-start | bytes 2097152 | tf_op jit(solution)/shard_map/all_to_all | solution.py:24
  177.1 26.1 %collective-permute-done.3 = bf16[4,128,512]{2,1,0:T(8,128)(2,1)S(1)} collective-permute-done((bf16[4,128,512]{2,1,0:T(8,128)(2,1)}, bf16[4,128,512]{2,1,0:T(8,128)(2,1)S(1)}, u32[]{:S(2)}, u32[]{:S(2)}) %collective-permute-start.3) | collective-permute-done | bytes 524320 | tf_op jit(solution)/shard_map/ppermute | solution.py:211
  203.3 1.2 convolution_convert_fusion
  204.6 38.1 %all_to_all.40 = bf16[64,16,1024]{2,1,0:T(8,128)(2,1)} all-to-all(bf16[64,16,1024]{2,1,0:T(8,128)(2,1)S(1)} %bitcast.56), channel_id=1, replica_groups=mesh['ab'=2,'am'=2,'al'=2,'y'=4,'core'=2,'hidden'=4,'pair'=2] {'al','hid..., dimensions={0} | all-to-all | bytes 4194304 | tf_op jit(solution)/shard_map/all_to_all | solution.py:24
  242.7 4.1 %combine.1 = bf16[8,4,4096]{2,1,0:T(4,128)(2,1)} custom-call(bf16[8,4,4224]{2,1,0:T(4,128)(2,1)} %copy-done, bf16[2,4,128,1024]{3,2,1,0:T(8,128)(2,1)} %bitcast.53), custom_call_target="tpu_custom_call" | custom-call | tf_op jit(solution)/shard_map/combine/pallas_call | solution.py:138
  246.8 25.0 %all_to_all.41 = bf16[8,4,4096]{2,1,0:T(4,128)(2,1)S(1)} all-to-all(bf16[8,4,4096]{2,1,0:T(4,128)(2,1)} %combine.1), channel_id=1, replica_groups=mesh['ab'=2,'am'=2,'al'=2,'y'=4,'core'=2,'hidden'=4,'pair'=2] {'pair','a..., dimensions={0} | all-to-all | bytes 524288 | tf_op jit(solution)/shard_map/all_to_all | solution.py:24
  (49 shorter events, 7.1 us)
Async XLA Ops:
  0.0 8.9 %copy-start.6 = (s32[1,4,2]{1,2,0:T(2,128)S(1)}, s32[1,4,2]{1,2,0:T(2,128)}, u32[]{:S(2)}) copy-start(s32[1,4,2]{1,2,0:T(2,128)} %param.18) | copy-start | bytes 100
  0.0 9.5 %copy-start.7 = (f32[1,4,2]{1,2,0:T(2,128)S(1)}, f32[1,4,2]{1,2,0:T(2,128)}, u32[]{:S(2)}) copy-start(f32[1,4,2]{1,2,0:T(2,128)} %param.17) | copy-start | bytes 100
  3.1 40.1 %copy-start.4 = (bf16[1,4,4096]{2,1,0:T(4,128)(2,1)S(1)}, bf16[1,4,4096]{2,1,0:T(4,128)(2,1)}, u32[]{:S(2)}) copy-start(bf16[1,4,4096]{2,1,0:T(4,128)(2,1)} %param.15) | copy-start | bytes 98308
  3.1 40.3 %copy-start.5 = (f32[4096]{0:T(1024)S(1)}, f32[4096]{0:T(1024)}, u32[]{:S(2)}) copy-start(f32[4096]{0:T(1024)} %param.16) | copy-start | bytes 49156
  3.1 48.5 %copy-start.3 = (bf16[1,1024,512]{2,1,0:T(8,128)(2,1)S(1)}, bf16[1,1024,512]{2,1,0:T(8,128)(2,1)}, u32[]{:S(2)}) copy-start(bf16[1,1024,512]{2,1,0:T(8,128)(2,1)} %param.21) | copy-start | bytes 3145732
  3.2 16.5 %all-to-all-start = ((bf16[8,4,4,4096]{3,2,1,0:T(4,128)(2,1)}), bf16[8,4,4,4096]{3,2,1,0:T(4,128)(2,1)S(1)}, u32[]{:S(2)}, u32[]{:S(2)}) async-start(bf16[8,4,4,4096]{3,2,1,0:T(4,128)(2,1)} %attention.1), calls=%async_computation | async-start | bytes 2097152 | tf_op jit(solution)/shard_map/all_to_all | solution.py:24
  20.9 22.3 %all-to-all-start.1 = ((bf16[4,4,4096]{2,1,0:T(4,128)(2,1)}), bf16[4,4,4096]{2,1,0:T(4,128)(2,1)S(1)}, u32[]{:S(2)}, u32[]{:S(2)}) async-start(bf16[4,4,4096]{2,1,0:T(4,128)(2,1)} %reduce_sum.63), calls=%async_computation.1 | async-start | bytes 262144 | tf_op jit(solution)/shard_map/all_to_all | solution.py:24
  44.3 22.9 %all-to-all-start.2 = ((bf16[8,4,4224]{2,1,0:T(4,128)(2,1)}), bf16[8,4,4224]{2,1,0:T(4,128)(2,1)S(1)}, u32[]{:S(2)}, u32[]{:S(2)}) async-start(bf16[8,4,4224]{2,1,0:T(4,128)(2,1)} %broadcast_in_dim.27), calls=%async_computation.2 | async-start | bytes 540672 | tf_op jit(solution)/shard_map/all_to_all | solution.py:24
  67.2 0.7 copy-start
  71.9 15.4 %copy-start.1 = (bf16[1,2,4096,128]{3,2,1,0:T(8,128)(2,1)S(1)}, bf16[1,2,4096,128]{3,2,1,0:T(8,128)(2,1)}, u32[]{:S(2)}) copy-start(bf16[1,2,4096,128]{3,2,1,0:T(8,128)(2,1)} %param.20) | copy-start | bytes 6291460
  71.9 63.0 %all-to-all-start.3 = ((bf16[64,16,1024]{2,1,0:T(8,128)(2,1)}), bf16[64,16,1024]{2,1,0:T(8,128)(2,1)}, u32[]{:S(2)}, u32[]{:S(2)}) async-start(bf16[64,16,1024]{2,1,0:T(8,128)(2,1)} %bitcast.52), calls=%async_computation.3 | async-start | bytes 4194304 | tf_op jit(solution)/shard_map/all_to_all | solution.py:24
  88.5 14.8 %copy-start.2 = (bf16[2,1,1024,128]{3,2,1,0:T(8,128)(2,1)S(1)}, bf16[2,1,1024,128]{3,2,1,0:T(8,128)(2,1)}, u32[]{:S(2)}) copy-start(bf16[2,1,1024,128]{3,2,1,0:T(8,128)(2,1)} %get-tuple-element.14) | copy-start | bytes 1572868
  90.6 31.2 %collective-permute-start = (bf16[2,1024,128]{1,2,0:T(8,128)(2,1)}, bf16[2,1024,128]{1,2,0:T(8,128)(2,1)}, u32[]{:S(2)}, u32[]{:S(2)}) collective-permute-start(bf16[2,1024,128]{1,2,0:T(8,128)(2,1)} %bitcast.14), channel_id=1, source_target_pairs={{0,2},{2,4},{4,6},{6,0},{1,3},{3,5},{5,7},{7,1},{8,10},{10,12},{12... | collective-permute-start | bytes 1572872 | tf_op jit(solution)/shard_map/ppermute | solution.py:192
  95.7 27.6 %collective-permute-start.1 = (bf16[2,1024,128]{1,2,0:T(8,128)(2,1)}, bf16[2,1024,128]{1,2,0:T(8,128)(2,1)}, u32[]{:S(2)}, u32[]{:S(2)}) collective-permute-start(bf16[2,1024,128]{1,2,0:T(8,128)(2,1)} %bitcast.16), channel_id=1, source_target_pairs={{0,4},{2,6},{4,0},{6,2},{1,5},{3,7},{5,1},{7,3},{8,12},{10,14},{12... | collective-permute-start | bytes 1572872 | tf_op jit(solution)/shard_map/ppermute | solution.py:192
  99.4 34.5 %collective-permute-start.2 = (bf16[2,1024,128]{1,2,0:T(8,128)(2,1)}, bf16[2,1024,128]{1,2,0:T(8,128)(2,1)}, u32[]{:S(2)}, u32[]{:S(2)}) collective-permute-start(bf16[2,1024,128]{1,2,0:T(8,128)(2,1)} %bitcast.18), channel_id=1, source_target_pairs={{0,6},{2,0},{4,2},{6,4},{1,7},{3,1},{5,3},{7,5},{8,14},{10,8},{12,... | collective-permute-start | bytes 1572872 | tf_op jit(solution)/shard_map/ppermute | solution.py:192
  140.2 30.7 %all-to-all-start.4 = ((bf16[4,256,1024]{2,1,0:T(8,128)(2,1)}), bf16[4,256,1024]{2,1,0:T(8,128)(2,1)S(1)}, u32[]{:S(2)}, u32[]{:S(2)}) async-start(bf16[4,256,1024]{2,1,0:T(8,128)(2,1)} %bitcast.55), calls=%async_computation.4 | async-start | bytes 4194304 | tf_op jit(solution)/shard_map/all_to_all | solution.py:24
  146.6 56.6 %collective-permute-start.3 = (bf16[4,128,512]{2,1,0:T(8,128)(2,1)}, bf16[4,128,512]{2,1,0:T(8,128)(2,1)S(1)}, u32[]{:S(2)}, u32[]{:S(2)}) collective-permute-start(bf16[4,128,512]{2,1,0:T(8,128)(2,1)} %get-tuple-element.8), channel_id=1, source_target_pairs={{0,1},{1,0},{2,3},{3,2},{4,5},{5,4},{6,7},{7,6},{8,9},{9,8},{10,11... | collective-permute-start | bytes 1572872 | tf_op jit(solution)/shard_map/ppermute | solution.py:211
  172.5 30.9 %all-to-all-start.5 = ((bf16[4,256,512]{2,1,0:T(8,128)(2,1)}), bf16[4,256,512]{2,1,0:T(8,128)(2,1)S(1)}, u32[]{:S(2)}, u32[]{:S(2)}) async-start(bf16[4,256,512]{2,1,0:T(8,128)(2,1)} %broadcast_in_dim.33), calls=%async_computation.5 | async-start | bytes 2097152 | tf_op jit(solution)/shard_map/all_to_all | solution.py:24
